TPU v7x, 256 devices: a whole 4x4x8 slice. The times are simulated.
256 devices in a mesh: band: 16 (over y, x), lev: 16 (over z, core).
Axes of the slice: x: 4, y: 4, z: 8, core: 2. Of those that a mesh axis runs over, the one named last changes fastest.
Arguments:
- adj_spec: bfloat16 [64, 1280, 2, 1280], P('lev', 'band'), may hold values from -6 to 6
- wave_of_slot: int32 [1280], replicated, may hold values from 0 to 1279, each once
- legendre: bfloat16 [1280, 32, 1280], P('band'), may hold values from -0.15625 to 0.15625
- lat_weight: float32 [32], replicated, may hold values from 0.5 to 1.5
- traj: bfloat16 [64, 64, 5136], P('lev', 'band'), may hold values from -3 to 3
- traj_exp: int32 [64, 64, 4], P('lev', 'band'), may hold values from -2 to 2
- traj_order: int32 [16, 4], P('lev'), may hold values from 0 to 3, each once within a row
- lev_coef: float32 [64], P('lev'), may hold values from 0.02 to 0.2
Outputs:
- adj_out: bfloat16 [64, 1280, 2, 1280], P('lev', 'band')
Inputs may be any that keep to these rules, and one draw needn't show every extreme that they name: `wave_of_slot`: every wavenumber 0 to 1279 is held by exactly one slot. `traj_order`: each row is a permutation of 0 to 3.
All inputs are finite; a program needn't handle non-finite values.
Results may differ from a plain program's by a relative error of at most 0.0085.
Values may be sent and summed in bfloat16 or wider, within the bound.
No kernel may reach another device: no remote copies, remote signals or barrier semaphores. Data moves between devices by JAX's collectives and lax.ppermute only.
A program may use at most 128 MiB of HBM per device.

v0:
```python
import math

import jax
import jax.numpy as jnp
from jax import lax
from jax.sharding import Mesh
from jax.sharding import PartitionSpec as P

NBLK = 4
BAND = ("band_0", "band_1")


def prefix(value, axis, combine, identity):
    size, index = (lax.axis_size(axis), lax.axis_index(axis))
    everything = lax.all_gather(value.astype(jnp.bfloat16), axis)
    start = jnp.broadcast_to(jnp.asarray(identity, value.dtype), value.shape)

    def turn(k, before):
        reached = k < index
        new = combine(before, everything[k].astype(value.dtype))
        return jnp.where(reached, new, before)

    return lax.fori_loop(0, size, turn, start)


def cut_along(value, dim, size):
    lengths = value.shape
    tiles = value.reshape(*lengths[:dim], size, lengths[dim] // size, *lengths[dim + 1 :])
    return jnp.moveaxis(tiles, dim, 0)


def laid_out(tiles, dim):
    tiles = jnp.moveaxis(tiles, 0, dim)
    lengths = tiles.shape
    return tiles.reshape(*lengths[:dim], lengths[dim] * lengths[dim + 1], *lengths[dim + 2 :])


def turned_blocks(tiles, axes, turns):
    inside = tiles.shape[1:]
    whole = tiles.reshape(*(lax.axis_size(a) for a in axes), *inside)
    for k in turns:
        whole = lax.all_to_all(whole, axes[k], k, k, tiled=True)
    return whole.reshape(-1, *inside)


def one_axis_at_a_time(value, axes, turns, split_dim, concat_dim):
    tiles = cut_along(value, split_dim, lax.axis_size(axes))
    return laid_out(turned_blocks(tiles, axes, turns), concat_dim)


def trig_whole(wave_ids, lon_count):
    lon_ids = jnp.arange(lon_count, dtype=jnp.int32)
    phase_int = wave_ids[:, None] * lon_ids[None, :] % lon_count
    angle_rad = phase_int.astype(jnp.float32) * (2.0 * math.pi / lon_count)
    return jnp.stack([jnp.cos(angle_rad), -jnp.sin(angle_rad)], axis=1).astype(jnp.bfloat16)


def add_carry(earlier, later):
    return earlier + later


def body(adj_spec, wave_of_slot, legendre, lat_weight, traj, traj_exp, traj_order, lev_coef):
    highest = lax.Precision.HIGHEST
    levels = adj_spec.shape[0]
    slots = adj_spec.shape[1]
    degrees = adj_spec.shape[3]
    lat_rows = traj.shape[1]
    lon_count = traj.shape[2]
    block_width = lon_count // NBLK
    norm_scale = 1.0 / math.sqrt(degrees)
    first_slot = lax.axis_index(BAND) * slots
    waves_here = lax.dynamic_slice_in_dim(wave_of_slot, first_slot, slots)
    degree_ids = jnp.arange(degrees, dtype=jnp.int32)
    valid_mask = degree_ids[None, :] < (degrees - waves_here)[:, None]
    masked = jnp.where(valid_mask[None, :, None, :], adj_spec, jnp.zeros_like(adj_spec))
    weight_q = jnp.repeat(lat_weight, 2)
    parity_sign = jnp.where(degree_ids % 2 == 0, 1.0, -1.0).astype(jnp.bfloat16)
    stacked = jnp.stack([masked, masked * parity_sign], axis=3)
    side_values = jnp.einsum(
        "lscej,shj->lsche", stacked, legendre, preferred_element_type=jnp.float32
    )
    fourier = (side_values.reshape(levels, slots, 2, -1) * weight_q).astype(jnp.bfloat16)
    fourier_here = lax.all_to_all(fourier, BAND, split_axis=3, concat_axis=1, tiled=True)
    trig_all = trig_whole(wave_of_slot, lon_count)
    order_ids = jnp.arange(levels, dtype=jnp.int32)
    select = (traj_order[0][None, :] == order_ids[:, None]).astype(jnp.float32)
    level_coef = lev_coef[:, None, None]
    grid_list = []
    for block_id in range(NBLK):
        trig_table = trig_all[:, :, block_id * block_width : (block_id + 1) * block_width]
        grid_list.append(
            jnp.einsum(
                "lsca,scw->law", fourier_here, trig_table, preferred_element_type=jnp.float32
            )
            * norm_scale
        )
    grid_all = jnp.stack(grid_list, axis=1)
    running = jnp.cumsum(grid_all, axis=0)
    prior_sum = jnp.concatenate([jnp.zeros_like(grid_all[:1]), running[:-1]], axis=0)
    block_total = running[-1]
    group_carry = prefix(block_total, "lev", add_carry, jnp.zeros_like(block_total))
    above_all = prior_sum + group_carry[None]
    analysis = jnp.zeros((levels, degrees, 2, lat_rows), jnp.float32)
    for block_id in range(NBLK):
        lon_start = block_id * block_width
        trig_table = trig_all[:, :, lon_start : lon_start + block_width]
        exponent = jnp.exp2(traj_exp[:, :, block_id].astype(jnp.float32))
        traj_piece = (
            traj[:, :, lon_start : lon_start + block_width].astype(jnp.float32)
            * exponent[:, :, None]
        )
        traj_value = jnp.einsum("ir,raw->iaw", select, traj_piece, precision=highest)
        forcing = (
            (1.0 + jnp.tanh(traj_value))
            * (grid_all[:, block_id] + level_coef * above_all[:, block_id])
        ).astype(jnp.bfloat16)
        analysis = (
            analysis
            + jnp.einsum("law,scw->lsca", forcing, trig_table, preferred_element_type=jnp.float32)
            * norm_scale
        )
    returned = one_axis_at_a_time(analysis, BAND, (0, 1), 1, 3)
    halves = returned.reshape(levels, slots, 2, -1, 2)
    sym_part = (halves[..., 0] + halves[..., 1]).astype(jnp.bfloat16)
    anti_part = (halves[..., 0] - halves[..., 1]).astype(jnp.bfloat16)
    from_sym = jnp.einsum("lsch,shj->lscj", sym_part, legendre, preferred_element_type=jnp.float32)
    from_anti = jnp.einsum(
        "lsch,shj->lscj", anti_part, legendre, preferred_element_type=jnp.float32
    )
    result = jnp.where(degree_ids % 2 == 0, from_sym, from_anti)
    return jnp.where(valid_mask[None, :, None, :], result, 0.0).astype(jnp.bfloat16)


def solution(mesh):
    torus = Mesh(mesh.devices.reshape(4, 4, mesh.shape["lev"]), ("band_0", "band_1", "lev"))
    return jax.shard_map(
        body,
        mesh=torus,
        in_specs=(
            P("lev", BAND, None, None),
            P(),
            P(BAND, None, None),
            P(),
            P("lev", BAND, None),
            P("lev", BAND, None),
            P("lev", None),
            P("lev"),
        ),
        out_specs=P("lev", BAND, None, None),
        check_vma=False,
    )
```

profile of v0, /device:TPU:1, one launch (start us, length us, event | category | flops | bytes accessed | tf_op | source)
XLA Modules:
  0.0 222.4 jit_solution(7207689764464458243)
XLA Ops:
  0.0 0.8 dynamic-slice_subtract_fusion
  0.8 0.1 iota_compare_fusion
  0.9 3.5 %fusion.94 = (bf16[4,80,2,1,1280]{4,0,3,2,1:T(4,128)(2,1)S(1)}, bf16[4,80,2,1,1280]{4,0,3,2,1:T(4,128)(2,1)S(1)}) fusion(bf16[4,80,2,1280]{3,2,1,0:T(2,128)(2,1)} %param.10, pred[80,1280]{1,0:T(8,128)(4,1)S(1)} %iota_compare_fusion, bf16[1280]{0:T(1024)(128)(2,1)S(1)} %select_convert_fusion.1), kind=kLoop, calls=%fused_computation.79 | loop fusion | flops 1638400 | bytes 5020160 | tf_op jit(solution)/shard_map/stack | solution.py:78
  4.5 6.2 %fusion.89 = f32[4,80,2,32,2]{3,0,4,2,1:T(4,128)S(1)} fusion(bf16[80,32,1280]{2,1,0:T(8,128)(2,1)} %param.12, bf16[4,80,2,1,1280]{4,0,3,2,1:T(4,128)(2,1)S(1)} %get-tuple-element.129, bf16[4,80,2,1,1280]{4,0,3,2,1:T(4,128)(2,1)S(1)} %get-tuple-element.128), kind=kOutput, calls=%fused_computation.78 | convolution fusion | flops 111411200 | bytes 9994240 | tf_op jit(solution)/shard_map/lscej,shj->lsche/dot_general | solution.py:79
  10.6 0.3 copy.69
  11.0 0.1 mul.183
  11.1 0.1 multiply_convert_fusion
  11.2 0.8 copy.70
  12.0 7.6 %all-to-all-start = ((bf16[4,80,2,64]{1,2,0,3:T(2,128)(2,1)}), bf16[4,80,2,64]{1,2,0,3:T(2,128)(2,1)S(1)}, u32[]{:S(2)}, u32[]{:S(2)}) async-start(bf16[4,80,2,64]{1,2,0,3:T(2,128)(2,1)} %copy.70), calls=%async_computation | async-start | bytes 262144 | tf_op jit(solution)/shard_map/all_to_all | solution.py:83
  19.6 109.3 %cosine_convert_fusion = (bf16[1280,1,5136]{0,2,1:T(8,128)(2,1)S(1)}, bf16[1280,1,5136]{0,2,1:T(8,128)(2,1)S(1)}) fusion(s32[1280]{0:T(1024)S(1)} %copy-done.3), kind=kLoop, calls=%fused_computation.11 | loop fusion | flops 78888960 | bytes 26301440 | tf_op jit(solution)/shard_map/convert.2
  128.9 0.2 exponential_reduce_fusion.3
  129.1 10.5 %fusion.6 = (bf16[1280,2,1284]{0,2,1:T(8,128)(2,1)}, bf16[1280,2,1284]{0,2,1:T(8,128)(2,1)}, bf16[1280,2,1284]{0,2,1:T(8,128)(2,1)}, bf16[1280,2,1284]{0,2,1:T(8,128)(2,1)}) fusion(bf16[1280,1,5136]{0,2,1:T(8,128)(2,1)S(1)} %get-tuple-element.136, bf16[1280,1,5136]{0,2,1:T(8,128)(2,1)S(1)} %get-tuple-element.137), kind=kLoop, calls=%fused_computation.17 | loop fusion | flops 52592640 | bytes 52592640 | tf_op jit(solution)/shard_map/stack | solution.py:55
  139.7 0.2 convert_multiply_fusion.3
  139.9 0.2 reshape.151
  140.1 5.0 %fusion.74 = f32[4,4,1284]{2,0,1:T(4,128)S(1)} fusion(bf16[4,1280,2,4]{1,0,2,3:T(4,128)(2,1)S(1)} %reshape.151, bf16[1280,2,1284]{0,2,1:T(8,128)(2,1)} %get-tuple-element.126), kind=kOutput, calls=%fused_computation.59 | convolution fusion | flops 105205824 | bytes 6738176 | tf_op jit(solution)/shard_map/lsca,scw->law/dot_general | solution.py:92
  145.1 5.0 %fusion.68 = f32[4,4,1284]{2,0,1:T(4,128)S(1)} fusion(bf16[4,1280,2,4]{1,0,2,3:T(4,128)(2,1)S(1)} %reshape.151, bf16[1280,2,1284]{0,2,1:T(8,128)(2,1)} %get-tuple-element.127), kind=kOutput, calls=%fused_computation.57 | convolution fusion | flops 105205824 | bytes 6738176 | tf_op jit(solution)/shard_map/lsca,scw->law/dot_general | solution.py:92
  150.1 2.0 fusion.62
  152.1 2.0 fusion.56
  154.2 0.5 reduce_window_sum.11
  154.7 0.1 slice.160
  154.8 23.0 %all_gather.4 = bf16[16,4,4,1284]{3,2,1,0:T(4,128)(2,1)S(1)} all-gather(bf16[1,4,4,1284]{3,2,1,0:T(4,128)(2,1)S(1)} %copy.77), channel_id=1, replica_groups=mesh['band_0'=4,'band_1'=4,'lev'=16] {'lev'}, dimensions={0}, use_global_device_ids=true | all-gather | bytes 698496 | tf_op jit(solution)/shard_map/all_gather | solution.py:15
  177.8 1.7 while.14
  177.9 0.1 add_select_fusion.4
  179.5 0.2 pad_add_fusion
  179.7 0.2 fusion.88
  179.9 4.3 %fusion.8 = f32[1280,2,4,4]{0,3,2,1:T(4,128)S(1)} fusion(bf16[1280,2,1284]{0,2,1:T(8,128)(2,1)} %get-tuple-element.126, bf16[4,4,1284]{2,0,1:T(4,128)(2,1)S(1)} %fusion.88), kind=kOutput, calls=%fused_computation.20 | convolution fusion | flops 105185280 | bytes 6779008 | tf_op jit(solution)/shard_map/law,scw->lsca/dot_general | solution.py:119
  184.3 0.2 fusion.87
  184.5 1.2 fusion.10
  185.8 0.2 fusion.86
  186.0 0.4 slice-done.5
  186.5 1.2 fusion.12
  187.7 0.2 fusion.85
  187.9 0.4 slice-done.3
  188.4 1.2 fusion.50
  189.6 0.2 reshape.131
  189.9 0.1 copy.86
  190.0 10.5 %all_to_all.28 = f32[4,4,4,80,2,4]{3,5,1,4,2,0:T(4,128)S(1)} all-to-all(f32[4,4,4,80,2,4]{3,5,1,4,2,0:T(4,128)S(1)} %copy.86), channel_id=1, replica_groups=mesh['band_0'=4,'band_1'=4,'lev'=16] {'band_0'}, dimensions={0} | all-to-all | bytes 327680 | tf_op jit(solution)/shard_map/all_to_all | solution.py:42
  200.5 0.8 copy.87
  201.3 4.0 %all-to-all-start.2 = ((f32[4,4,4,80,2,4]{3,5,0,4,2,1:T(4,128)}), f32[4,4,4,80,2,4]{3,5,0,4,2,1:T(4,128)S(1)}, u32[]{:S(2)}, u32[]{:S(2)}) async-start(f32[4,4,4,80,2,4]{3,5,0,4,2,1:T(4,128)} %copy.87), calls=%async_computation.2 | async-start | bytes 524288 | tf_op jit(solution)/shard_map/all_to_all | solution.py:42
  205.2 5.5 %all-to-all-done.2 = f32[4,4,4,80,2,4]{3,5,0,4,2,1:T(4,128)S(1)} async-done(((f32[4,4,4,80,2,4]{3,5,0,4,2,1:T(4,128)}), f32[4,4,4,80,2,4]{3,5,0,4,2,1:T(4,128)S(1)}, u32[]{:S(2)}, u32[]{:S(2)}) %all-to-all-start.2) | async-done | bytes 163872 | tf_op jit(solution)/shard_map/all_to_all | solution.py:42
  210.8 0.2 copy.88
  210.9 0.1 copy.89
  211.1 0.3 add_convert_fusion
  211.3 0.2 copy.111
  211.5 3.8 %fusion.26 = bf16[80,4,2,1280]{3,1,2,0:T(4,128)(2,1)S(1)} fusion(bf16[80,32,1280]{2,1,0:T(8,128)(2,1)} %param.12, bf16[4,80,2,32,1]{3,0,2,1,4:T(4,128)(2,1)S(1)} %copy.111), kind=kOutput, calls=%fused_computation.38 | convolution fusion | flops 52428800 | bytes 8232960 | tf_op jit(solution)/shard_map/lsch,shj->lscj/dot_general | solution.py:127
  215.3 0.2 copy.110
  215.5 4.4 %fusion.35 = bf16[4,80,2,1280]{3,0,2,1:T(4,128)(2,1)S(1)} fusion(bf16[80,4,2,1280]{3,1,2,0:T(4,128)(2,1)S(1)} %fusion.26, bf16[80,32,1280]{2,1,0:T(8,128)(2,1)} %param.12, pred[1280]{0:T(1024)(128)(4,1)S(1)} %fusion.117, pred[80,1280]{1,0:T(8,128)(4,1)S(1)} %iota_compare_fusion, bf16[4,80,2,32,1]{3,0,2,1,4:T(4,128)(2,1)S(1)} %copy.110), kind=kOutput, calls=%fused_computation.46 | convolution fusion | flops 54067200 | bytes 9975040 | tf_op jit(solution)/shard_map/lsch,shj->lscj/dot_general | solution.py:126
  219.9 2.4 %copy.92 = bf16[4,80,2,1280]{3,2,1,0:T(2,128)(2,1)} copy(bf16[4,80,2,1280]{3,0,2,1:T(4,128)(2,1)S(1)} %fusion.35) | data formatting | bytes 3276800 | tf_op jit(solution)/shard_map/convert_element_type | solution.py:131
  (57 shorter events, 1.7 us)
Async XLA Ops:
  4.5 6.5 %copy-start.4 = (f32[32]{0:T(128)S(1)}, f32[32]{0:T(128)}, u32[]{:S(2)}) copy-start(f32[32]{0:T(128)} %param.13) | copy-start | bytes 388
  4.5 15.2 %copy-start.3 = (s32[1280]{0:T(1024)S(1)}, s32[1280]{0:T(1024)}, u32[]{:S(2)}) copy-start(s32[1280]{0:T(1024)} %param.11) | copy-start | bytes 15364
  12.0 127.8 %all-to-all-start = ((bf16[4,80,2,64]{1,2,0,3:T(2,128)(2,1)}), bf16[4,80,2,64]{1,2,0,3:T(2,128)(2,1)S(1)}, u32[]{:S(2)}, u32[]{:S(2)}) async-start(bf16[4,80,2,64]{1,2,0,3:T(2,128)(2,1)} %copy.70), calls=%async_computation | async-start | bytes 262144 | tf_op jit(solution)/shard_map/all_to_all | solution.py:83
  19.6 109.3 %copy-start.2 = (s32[4,4,4]{2,1,0:T(4,128)S(1)}, s32[4,4,4]{2,1,0:T(4,128)}, u32[]{:S(2)}) copy-start(s32[4,4,4]{2,1,0:T(4,128)} %param.15) | copy-start | bytes 772
  129.1 10.5 %copy-start.1 = (bf16[4,4,5136]{2,1,0:T(4,128)(2,1)S(1)}, bf16[4,4,5136]{2,1,0:T(4,128)(2,1)}, u32[]{:S(2)}) copy-start(bf16[4,4,5136]{2,1,0:T(4,128)(2,1)} %param.14) | copy-start | bytes 493060
  140.1 10.0 %copy-start = (bf16[1280,2,1284]{0,2,1:T(8,128)(2,1)S(1)}, bf16[1280,2,1284]{0,2,1:T(8,128)(2,1)}, u32[]{:S(2)}) copy-start(bf16[1280,2,1284]{0,2,1:T(8,128)(2,1)} %get-tuple-element.125) | copy-start | bytes 19722244
  140.1 12.0 %slice-start = ((s8[6594560]{0:T(1024)(128)(4,1)}), s8[4194304]{0:T(1024)(128)(4,1)S(1)}, s32[]{:S(2)}) async-start(s8[6594560]{0:T(1024)(128)(4,1)} %bitcast.188), calls=%async_computation.3 | async-start | bytes 8388608
  145.1 7.0 %slice-start.1 = ((s8[6594560]{0:T(1024)(128)(4,1)}), s8[2400256]{0:T(1024)(128)(4,1)S(1)}, s32[]{:S(2)}) async-start(s8[6594560]{0:T(1024)(128)(4,1)} %bitcast.188), calls=%async_computation.4 | async-start | bytes 4800512
  152.1 27.6 %copy-start.5 = (f32[4]{0:T(128)S(1)}, f32[4]{0:T(128)}, u32[]{:S(2)}) copy-start(f32[4]{0:T(128)} %param.17) | copy-start | bytes 52
  152.1 27.6 %copy-start.6 = (s32[1,4]{1,0:T(1,128)S(1)}, s32[1,4]{1,0:T(1,128)}, u32[]{:S(2)}) copy-start(s32[1,4]{1,0:T(1,128)} %param.16) | copy-start | bytes 52
  179.5 5.0 %slice-start.6 = ((s8[6594560]{0:T(1024)(128)(4,1)}), s8[4194304]{0:T(1024)(128)(4,1)S(1)}, s32[]{:S(2)}) async-start(s8[6594560]{0:T(1024)(128)(4,1)} %bitcast.194), calls=%async_computation.9 | async-start | bytes 8388608
  179.9 4.6 %slice-start.7 = ((s8[6594560]{0:T(1024)(128)(4,1)}), s8[2400256]{0:T(1024)(128)(4,1)S(1)}, s32[]{:S(2)}) async-start(s8[6594560]{0:T(1024)(128)(4,1)} %bitcast.194), calls=%async_computation.10 | async-start | bytes 4800512
  179.9 6.1 %slice-start.4 = ((s8[6594560]{0:T(1024)(128)(4,1)}), s8[4194304]{0:T(1024)(128)(4,1)S(1)}, s32[]{:S(2)}) async-start(s8[6594560]{0:T(1024)(128)(4,1)} %bitcast.192), calls=%async_computation.7 | async-start | bytes 8388608
  184.5 1.9 slice-start.5
  184.5 3.4 %slice-start.2 = ((s8[6594560]{0:T(1024)(128)(4,1)}), s8[4194304]{0:T(1024)(128)(4,1)S(1)}, s32[]{:S(2)}) async-start(s8[6594560]{0:T(1024)(128)(4,1)} %bitcast.190), calls=%async_computation.5 | async-start | bytes 8388608
  186.4 1.9 slice-start.3
  201.3 9.5 %all-to-all-start.2 = ((f32[4,4,4,80,2,4]{3,5,0,4,2,1:T(4,128)}), f32[4,4,4,80,2,4]{3,5,0,4,2,1:T(4,128)S(1)}, u32[]{:S(2)}, u32[]{:S(2)}) async-start(f32[4,4,4,80,2,4]{3,5,0,4,2,1:T(4,128)} %copy.87), calls=%async_computation.2 | async-start | bytes 524288 | tf_op jit(solution)/shard_map/all_to_all | solution.py:42
where the time goes:
time: 223 us; the launch traced here: 222 us
  other arithmetic  127 us (57%)
  matrix products  37.2 us (17%)
  blocking collectives  33.5 us (15%)
  starting transfers between devices  11.6 us (5%)
  local copies, waits for them, and re-layouts  6.71 us (3%)
  waiting for transfers between devices  5.52 us (2%)
    another operation x1, other arithmetic  109 us
    all_gather x1, blocking collectives, prefix(): everything = lax.all_gather(value.astype(jnp.bfloat16), axis)  23 us
    dot_general x4, matrix products, body(): jnp.einsum('lsca,scw->law', fourier_here, trig_table, preferred_element_t...  13.9 us
    all_to_all x1, blocking collectives, turned_blocks(): whole = lax.all_to_all(whole, axes[k], k, k, tiled=True)  10.5 us
    another operation x1, other arithmetic, trig_whole(): jnp.stack([jnp.cos(angle_rad), -jnp.sin(angle_rad)], axis=1)  10.5 us
    dot_general x4, matrix products, body(): jnp.einsum('law,scw->lsca', forcing, trig_table, preferred_element_type=j...  8 us
    all_to_all x1, starting transfers between devices, body(): lax.all_to_all(fourier, BAND, split_axis=3, concat_axis=1, tiled=True)  7.59 us
    dot_general x1, matrix products, body(): jnp.einsum('lscej,shj->lsche', stacked, legendre, preferred_element_type=...  6.16 us
  transfers between devices with their start and end apart: 2, of which 1 were waited for; matrix products, arithmetic and copies ran while one was open for 54% of the time, Pallas kernels for 0%

commit v1 on v0

v1 whole, which is shorter than its diff:
```python
import math

import jax
import jax.numpy as jnp
from jax import lax
from jax.sharding import PartitionSpec as P

NBLK = 4
LO = 32


def angles(wave_ids, lon_ids, lon_count):
    phase = lon_ids[:, None] * wave_ids[None, :] % lon_count
    angle = phase.astype(jnp.float32) * (2.0 * math.pi / lon_count)
    return jnp.cos(angle), jnp.sin(angle)


def quarter_table(wave_ids, width, lon_count):
    steps = -(-width // LO)
    low = angles(wave_ids, jnp.arange(LO, dtype=jnp.int32), lon_count)
    high = angles(wave_ids, jnp.arange(steps, dtype=jnp.int32) * LO, lon_count)
    cos_low, sin_low, cos_high, sin_high = lax.optimization_barrier((*low, *high))
    cos_high, sin_high = cos_high[:, None], sin_high[:, None]
    cos_all = cos_high * cos_low - sin_high * sin_low
    sin_all = sin_high * cos_low + cos_high * sin_low
    flat = (steps * LO, wave_ids.shape[0])
    cos_all = cos_all.astype(jnp.bfloat16).reshape(flat)
    sin_all = (-sin_all).astype(jnp.bfloat16).reshape(flat)
    return lax.optimization_barrier((cos_all[:width], sin_all[:width]))


def scan_levels(total):
    size, axis = 16, "lev"
    running = total
    step = 1
    while step < size:
        moved = lax.ppermute(
            running.astype(jnp.bfloat16), axis, [(i, i + step) for i in range(size - step)]
        )
        running = running + moved.astype(jnp.float32)
        step *= 2
    return lax.ppermute(
        running.astype(jnp.bfloat16), axis, [(i, i + 1) for i in range(size - 1)]
    ).astype(jnp.float32)


def body(adj_spec, wave_of_slot, legendre, lat_weight, traj, traj_exp, traj_order, lev_coef):
    bf16, f32 = jnp.bfloat16, jnp.float32
    highest = lax.Precision.HIGHEST
    levels, slots, _, degrees = adj_spec.shape
    lat_rows, lon_count = traj.shape[1:]
    width = lon_count // NBLK
    norm_scale = 1.0 / math.sqrt(degrees)
    waves_here = lax.dynamic_slice_in_dim(wave_of_slot, lax.axis_index("band") * slots, slots)
    degree_ids = jnp.arange(degrees, dtype=jnp.int32)
    valid = degree_ids[None, :] < (degrees - waves_here)[:, None]
    masked = jnp.where(valid[None, :, None, :], adj_spec, jnp.zeros_like(adj_spec))
    sign = jnp.where(degree_ids % 2 == 0, 1.0, -1.0).astype(bf16)
    stacked = jnp.stack([masked, masked * sign], axis=3)
    side = jnp.einsum("lscej,shj->lsche", stacked, legendre, preferred_element_type=f32)
    weight_q = jnp.repeat(lat_weight, 2)
    fourier = (side.reshape(levels, slots, 2, -1) * weight_q).astype(bf16)
    fourier = lax.all_to_all(fourier, "band", split_axis=3, concat_axis=1, tiled=True)
    total = jnp.sum(fourier.astype(f32), axis=0)
    carry = scan_levels(total)

    cos_t, sin_t = quarter_table(wave_of_slot, width, lon_count)
    turn = jnp.arange(NBLK, dtype=jnp.int32)[:, None] * wave_of_slot[None, :] % 4
    cos_b = jnp.where(turn == 0, 1.0, jnp.where(turn == 2, -1.0, 0.0))
    sin_b = jnp.where(turn == 1, 1.0, jnp.where(turn == 3, -1.0, 0.0))

    def to_grid(rows):
        first, second = rows[:, None, :, 0], rows[:, None, :, 1]
        first, second = jnp.moveaxis(first, 2, 3), jnp.moveaxis(second, 2, 3)
        cb, sb = cos_b[None, :, None, :], sin_b[None, :, None, :]
        with_cos = (first * cb - second * sb).astype(bf16)
        with_sin = (first * sb + second * cb).astype(bf16)
        out = jnp.einsum("lbqs,ks->lbqk", with_cos, cos_t, preferred_element_type=f32)
        out = out + jnp.einsum("lbqs,ks->lbqk", with_sin, sin_t, preferred_element_type=f32)
        return out * norm_scale

    grid = to_grid(fourier.astype(f32))
    group = to_grid(carry[None])
    running = jnp.cumsum(grid, axis=0)
    above = jnp.concatenate([jnp.zeros_like(grid[:1]), running[:-1]], axis=0) + group

    order = jnp.arange(levels, dtype=jnp.int32)
    select = (traj_order[0][None, :] == order[:, None]).astype(f32)
    scaled = traj.astype(f32).reshape(levels, lat_rows, NBLK, width)
    scaled = scaled * jnp.exp2(traj_exp.astype(f32))[..., None]
    ordered = jnp.einsum("ir,rqbk->ibqk", select, scaled, precision=highest)
    forcing = (1.0 + jnp.tanh(ordered)) * (grid + lev_coef[:, None, None, None] * above)
    forcing = forcing.astype(bf16)

    by_cos = jnp.einsum("lbqk,ks->lbqs", forcing, cos_t, preferred_element_type=f32)
    by_sin = jnp.einsum("lbqk,ks->lbqs", forcing, sin_t, preferred_element_type=f32)
    cb, sb = cos_b[None, :, None, :], sin_b[None, :, None, :]
    first = jnp.sum(by_cos * cb + by_sin * sb, axis=1) * norm_scale
    second = jnp.sum(by_sin * cb - by_cos * sb, axis=1) * norm_scale
    analysis = jnp.stack([first, second], axis=1)
    halves = analysis.reshape(levels, 2, lat_rows // 2, 2, -1)
    sym = halves[:, :, :, 0] + halves[:, :, :, 1]
    anti = halves[:, :, :, 0] - halves[:, :, :, 1]
    sides = jnp.stack([sym, anti], axis=2).astype(bf16)
    sides = lax.all_to_all(sides, "band", split_axis=4, concat_axis=3, tiled=True)
    both = jnp.einsum("lcehs,shj->lsecj", sides, legendre, preferred_element_type=f32)
    result = jnp.where(degree_ids % 2 == 0, both[:, :, 0], both[:, :, 1])
    return jnp.where(valid[None, :, None, :], result, 0.0).astype(bf16)


def solution(mesh):
    return jax.shard_map(
        body,
        mesh=mesh,
        in_specs=(
            P("lev", "band", None, None),
            P(),
            P("band", None, None),
            P(),
            P("lev", "band", None),
            P("lev", "band", None),
            P("lev", None),
            P("lev"),
        ),
        out_specs=P("lev", "band", None, None),
        check_vma=False,
    )
```

time: 223 us -> 118 us (0.53)
  the two profiles are of different devices: /device:TPU:1 before, /device:TPU:97 now
where the time goes in v1:
time: 118 us; the launch traced here: 117 us
  starting transfers between devices  42 us (36%)
  local copies, waits for them, and re-layouts  33.8 us (29%)
  matrix products  18.2 us (15%)
  other arithmetic  13.1 us (11%)
  waiting for transfers between devices  9.62 us (8%)
    ppermute x4, starting transfers between devices, scan_levels(): lax.ppermute(running.astype(jnp.bfloat16), axis, [(i, i + step) for i in...  14.6 us
    ppermute x1, starting transfers between devices, scan_levels(): lax.ppermute(running.astype(jnp.bfloat16), axis, [(i, i + 1) for i in ran...  13.7 us
    unnamed x28, local copies, waits for them, and re-layouts  12.8 us
    all_to_all x1, starting transfers between devices, body(): lax.all_to_all(sides, 'band', split_axis=4, concat_axis=3, tiled=True)  6.95 us
    all_to_all x1, starting transfers between devices, body(): lax.all_to_all(fourier, 'band', split_axis=3, concat_axis=1, tiled=True)  6.75 us
    all_to_all x1, waiting for transfers between devices, body(): lax.all_to_all(sides, 'band', split_axis=4, concat_axis=3, tiled=True)  6.56 us
    dot_general x1, matrix products, body(): jnp.einsum('lscej,shj->lsche', stacked, legendre, preferred_element_type=...  6.16 us
    dot_general x1, matrix products, body(): jnp.einsum('lcehs,shj->lsecj', sides, legendre, preferred_element_type=f32)  4.15 us
  transfers between devices with their start and end apart: 7, of which 3 were waited for; matrix products, arithmetic and copies ran while one was open for 15% of the time, Pallas kernels for 0%

profile of v1, /device:TPU:97, one launch (start us, length us, event | category | flops | bytes accessed | tf_op | source)
XLA Modules:
  0.0 117.2 jit_solution(4242895154096673147)
XLA Ops:
  0.0 0.8 dynamic-slice_subtract_fusion
  0.8 0.1 iota_compare_fusion
  0.9 0.6 copy-done.2
  1.5 3.5 %fusion.46 = (bf16[4,80,2,1,1280]{4,0,3,2,1:T(4,128)(2,1)S(1)}, bf16[4,80,2,1,1280]{4,0,3,2,1:T(4,128)(2,1)S(1)}) fusion(bf16[4,80,2,1280]{3,2,1,0:T(2,128)(2,1)} %param.8, pred[80,1280]{1,0:T(8,128)(4,1)S(1)} %iota_compare_fusion, bf16[1280]{0:T(1024)(128)(2,1)S(1)} %select_convert_fusion), kind=kLoop, calls=%fused_computation.39 | loop fusion | flops 1638400 | bytes 5020160 | tf_op jit(solution)/shard_map/stack | solution.py:59
  5.1 6.2 %fusion.41 = f32[4,80,2,32,2]{3,0,4,2,1:T(4,128)S(1)} fusion(bf16[80,32,1280]{2,1,0:T(8,128)(2,1)} %param.10, bf16[4,80,2,1,1280]{4,0,3,2,1:T(4,128)(2,1)S(1)} %get-tuple-element.20, bf16[4,80,2,1,1280]{4,0,3,2,1:T(4,128)(2,1)S(1)} %get-tuple-element.19), kind=kOutput, calls=%fused_computation.38 | convolution fusion | flops 111411200 | bytes 9994240 | tf_op jit(solution)/shard_map/lscej,shj->lsche/dot_general | solution.py:60
  11.3 0.3 copy.61
  11.9 0.8 copy.62
  12.6 6.8 %all-to-all-start = ((bf16[4,80,2,64]{1,2,0,3:T(2,128)(2,1)}), bf16[4,80,2,64]{1,2,0,3:T(2,128)(2,1)S(1)}, u32[]{:S(2)}, u32[]{:S(2)}) async-start(bf16[4,80,2,64]{1,2,0,3:T(2,128)(2,1)} %copy.62), calls=%async_computation | async-start | bytes 262144 | tf_op jit(solution)/shard_map/all_to_all | solution.py:63
  19.4 0.7 fusion.61
  20.1 1.1 fusion.51
  21.2 2.5 %negate_convert_fusion = (bf16[41,32,1280]{2,1,0:T(8,128)(2,1)S(1)}, bf16[41,32,1280]{2,1,0:T(8,128)(2,1)S(1)}) fusion(f32[32,1280]{1,0:T(8,128)S(1)} %get-tuple-element.14, f32[41,1280]{1,0:T(8,128)S(1)} %get-tuple-element.13, f32[32,1280]{1,0:T(8,128)S(1)} %get-tuple-element.12, f32[41,1280]{1,0:T(8,128)S(1)} %get-tuple-element.11), kind=kLoop, calls=%fused_computation | loop fusion | flops 15114240 | bytes 7464960 | tf_op jit(solution)/shard_map/convert_element_type | solution.py:28
  23.8 1.9 %slice.48 = bf16[1284,1280]{1,0:T(8,128)(2,1)} slice(bf16[1312,1280]{1,0:T(8,128)(2,1)S(1)} %bitcast.135), slice={[0:1284], [0:1280]} | slice | bytes 6574080 | tf_op jit(solution)/shard_map/slice | solution.py:29
  25.7 0.2 slice.49
  25.9 1.9 %reshape.192 = f32[4,4,4,1284]{3,2,1,0:T(4,128)} reshape(bf16[4,4,5136]{2,1,0:T(4,128)(2,1)} %param.12) | data formatting | bytes 493056 | tf_op jit(solution)/shard_map/reshape | solution.py:89
  27.8 0.7 copy.57
  28.6 0.6 copy.67
  29.2 0.9 reduce_sum.36
  30.1 5.6 %collective-permute-start = (bf16[1280,2,4]{0,2,1:T(4,128)(2,1)S(1)}, bf16[1280,2,4]{0,2,1:T(4,128)(2,1)S(1)}, u32[]{:S(2)}, u32[]{:S(2)}) collective-permute-start(bf16[1280,2,4]{0,2,1:T(4,128)(2,1)S(1)} %convert_element_type.122), channel_id=1, source_target_pairs={{0,1},{1,2},{2,3},{3,4},{4,5},{5,6},{6,7},{7,8},{8,9},{9,10},{10,1... | collective-permute-start | bytes 61448 | tf_op jit(solution)/shard_map/ppermute | solution.py:37
  35.8 0.7 copy.64
  36.5 1.8 %reshape.193 = f32[4,1280,2,4]{1,3,2,0:T(4,128)} reshape(f32[4,16,80,2,4]{2,1,4,3,0:T(8,128)} %copy.64) | data formatting | bytes 327680 | tf_op jit(solution)/shard_map/convert_element_type | solution.py:82
  38.3 2.6 %collective-permute-start.1 = (bf16[1280,2,4]{0,2,1:T(4,128)(2,1)S(1)}, bf16[1280,2,4]{0,2,1:T(4,128)(2,1)S(1)}, u32[]{:S(2)}, u32[]{:S(2)}) collective-permute-start(bf16[1280,2,4]{0,2,1:T(4,128)(2,1)S(1)} %fusion.78), channel_id=1, source_target_pairs={{0,2},{1,3},{2,4},{3,5},{4,6},{5,7},{6,8},{7,9},{8,10},{9,11},{10,... | collective-permute-start | bytes 61448 | tf_op jit(solution)/shard_map/ppermute | solution.py:37
  41.0 0.9 slice_bitcast_fusion.3
  41.9 0.9 collective-permute-done.1
  42.9 3.1 %collective-permute-start.2 = (bf16[1280,2,4]{0,2,1:T(4,128)(2,1)S(1)}, bf16[1280,2,4]{0,2,1:T(4,128)(2,1)S(1)}, u32[]{:S(2)}, u32[]{:S(2)}) collective-permute-start(bf16[1280,2,4]{0,2,1:T(4,128)(2,1)S(1)} %fusion.89), channel_id=1, source_target_pairs={{0,4},{1,5},{2,6},{3,7},{4,8},{5,9},{6,10},{7,11},{8,12},{9,13},{1... | collective-permute-start | bytes 61448 | tf_op jit(solution)/shard_map/ppermute | solution.py:37
  46.0 0.2 subtract_convert_fusion.1
  46.2 2.1 %collective-permute-done.2 = bf16[1280,2,4]{0,2,1:T(4,128)(2,1)S(1)} collective-permute-done((bf16[1280,2,4]{0,2,1:T(4,128)(2,1)S(1)}, bf16[1280,2,4]{0,2,1:T(4,128)(2,1)S(1)}, u32[]{:S(2)}, u32[]{:S(2)}) %collective-permute-start.2) | collective-permute-done | bytes 20512 | tf_op jit(solution)/shard_map/ppermute | solution.py:37
  48.3 3.3 %collective-permute-start.3 = (bf16[1280,2,4]{0,2,1:T(4,128)(2,1)S(1)}, bf16[1280,2,4]{0,2,1:T(4,128)(2,1)S(1)}, u32[]{:S(2)}, u32[]{:S(2)}) collective-permute-start(bf16[1280,2,4]{0,2,1:T(4,128)(2,1)S(1)} %fusion.79), channel_id=1, source_target_pairs={{0,8},{1,9},{2,10},{3,11},{4,12},{5,13},{6,14},{7,15},{16,24},{17,... | collective-permute-start | bytes 61448 | tf_op jit(solution)/shard_map/ppermute | solution.py:37
  51.6 1.2 %fusion.15 = f32[4,4,4,1284]{3,0,1,2:T(4,128)S(1)} fusion(bf16[1284,1280]{1,0:T(8,128)(2,1)S(1)} %slice.49, bf16[4,4,4,1280]{3,2,1,0:T(4,128)(2,1)S(1)} %get-tuple-element.24), kind=kOutput, calls=%fused_computation.15 | convolution fusion | flops 210370560 | bytes 3779584 | tf_op jit(solution)/shard_map/lbqs,ks->lbqk/dot_general | solution.py:79
  52.9 13.7 %collective-permute-start.4 = (bf16[1280,2,4]{0,2,1:T(4,128)(2,1)S(1)}, bf16[1280,2,4]{0,2,1:T(4,128)(2,1)S(1)}, u32[]{:S(2)}, u32[]{:S(2)}) collective-permute-start(bf16[1280,2,4]{0,2,1:T(4,128)(2,1)S(1)} %add_convert_fusion.4), channel_id=1, source_target_pairs={{0,1},{1,2},{2,3},{3,4},{4,5},{5,6},{6,7},{7,8},{8,9},{9,10},{10,1... | collective-permute-start | bytes 61448 | tf_op jit(solution)/shard_map/ppermute | solution.py:42
  66.6 2.0 %fusion.28 = f32[4,4,4,1284]{3,0,1,2:T(4,128)} fusion(f32[4,4,4,1284]{3,0,1,2:T(4,128)S(1)} %fusion.15, bf16[1284,1280]{1,0:T(8,128)(2,1)S(1)} %copy-done, bf16[4,4,4,1280]{3,2,1,0:T(4,128)(2,1)S(1)} %get-tuple-element.23), kind=kOutput, calls=%fused_computation.28 | convolution fusion | flops 210534912 | bytes 4108288 | tf_op jit(solution)/shard_map/lbqs,ks->lbqk/dot_general | solution.py:78
  68.6 2.2 %reduce_window_sum.11 = f32[4,4,4,1284]{3,0,1,2:T(4,128)} reduce-window(f32[4,4,4,1284]{3,0,1,2:T(4,128)} %fusion.28, f32[]{:T(128)} %constant.88.clone.1), window={size=4x1x1x1 pad=3_0x0_0x0_0x0_0}, to_apply=%region_0.1 | reduce-window | flops 246528 | bytes 657412 | tf_op jit(solution)/shard_map/jit(cumsum)/reduce_window_sum | solution.py:84
  70.9 1.0 fusion.11
  71.9 0.8 copy-done.1
  72.7 1.0 fusion.38
  73.9 0.8 fusion.34
  74.7 0.8 fusion.9
  75.5 0.9 add_reduce_fusion
  76.6 3.5 %copy.75 = bf16[4,2,2,2,1280]{0,3,1,2,4:T(2,128)(2,1)S(1)} copy(bf16[4,2,2,2,1280]{4,0,3,1,2:T(4,128)(2,1)S(1)} %pad_maximum_fusion.1) | data formatting | bytes 163840 | tf_op jit(solution)/shard_map/stack | solution.py:104
  80.2 5.7 %reshape.202 = bf16[16,2,1280]{2,1,0:T(2,128)(2,1)} reshape(bf16[1280,2,2,2,4]{4,3,2,1,0:T(2,128)(2,1)S(1)} %bitcast.136) | data formatting | bytes 163840
  85.9 6.9 %all-to-all-start.1 = ((bf16[16,2,1280]{2,1,0:T(2,128)(2,1)}), bf16[16,2,1280]{2,1,0:T(2,128)(2,1)S(1)}, u32[]{:S(2)}, u32[]{:S(2)}) async-start(bf16[16,2,1280]{2,1,0:T(2,128)(2,1)} %reshape.202), calls=%async_computation.1 | async-start | bytes 163840 | tf_op jit(solution)/shard_map/all_to_all | solution.py:105
  92.8 6.6 %all-to-all-done.1 = bf16[16,2,1280]{2,1,0:T(2,128)(2,1)S(1)} async-done(((bf16[16,2,1280]{2,1,0:T(2,128)(2,1)}), bf16[16,2,1280]{2,1,0:T(2,128)(2,1)S(1)}, u32[]{:S(2)}, u32[]{:S(2)}) %all-to-all-start.1) | async-done | bytes 81952 | tf_op jit(solution)/shard_map/all_to_all | solution.py:105
  99.4 5.6 %reshape.203 = bf16[1280,2,2,2,4]{4,3,2,1,0:T(2,128)(2,1)S(1)} reshape(bf16[16,2,1280]{2,1,0:T(2,128)(2,1)S(1)} %all-to-all-done.1) | data formatting | bytes 163840
  105.0 3.6 %copy.93 = bf16[4,2,2,2,16,80]{5,4,3,2,1,0:T(8,128)(2,1)S(1)} copy(bf16[4,2,2,2,16,80]{0,3,1,2,5,4:T(2,128)(2,1)S(1)} %bitcast.137) | data formatting | bytes 163840 | tf_op jit(solution)/shard_map/all_to_all | solution.py:105
  108.6 0.1 copy.77
  108.7 0.2 copy.89
  109.0 4.2 %fusion.4 = bf16[4,80,2,2,1280]{4,0,3,1,2:T(4,128)(2,1)S(1)} fusion(bf16[4,2,2,32,80]{3,0,1,4,2:T(4,128)(2,1)S(1)} %copy.89, bf16[80,32,1280]{2,1,0:T(8,128)(2,1)} %param.10), kind=kOutput, calls=%fused_computation.6 | convolution fusion | flops 104857600 | bytes 9912320 | tf_op jit(solution)/shard_map/lcehs,shj->lsecj/dot_general | solution.py:106
  113.2 1.6 %fusion.21 = bf16[4,80,2,1280]{3,0,2,1:T(4,128)(2,1)S(1)} fusion(bf16[4,80,2,2,1280]{4,0,3,1,2:T(4,128)(2,1)S(1)} %fusion.4, pred[1280]{0:T(1024)(128)(4,1)S(1)} %fusion.81, pred[80,1280]{1,0:T(8,128)(4,1)S(1)} %copy-done.3), kind=kLoop, calls=%fused_computation.22 | loop fusion | flops 1638400 | bytes 5018880 | tf_op jit(solution)/shard_map/convert_element_type | solution.py:108
  114.8 2.4 %copy.80 = bf16[4,80,2,1280]{3,2,1,0:T(2,128)(2,1)} copy(bf16[4,80,2,1280]{3,0,2,1:T(4,128)(2,1)S(1)} %fusion.21) | data formatting | bytes 3276800 | tf_op jit(solution)/shard_map/convert_element_type | solution.py:108
  (51 shorter events, 0.8 us)
Async XLA Ops:
  0.9 0.6 copy-start.2
  5.1 6.5 %copy-start.10 = (f32[32]{0:T(128)S(1)}, f32[32]{0:T(128)}, u32[]{:S(2)}) copy-start(f32[32]{0:T(128)} %param.11) | copy-start | bytes 388
  5.1 14.3 %copy-start.7 = (s32[1280]{0:T(1024)S(1)}, s32[1280]{0:T(1024)}, u32[]{:S(2)}) copy-start(s32[1280]{0:T(1024)} %param.9) | copy-start | bytes 15364
  12.6 15.9 %all-to-all-start = ((bf16[4,80,2,64]{1,2,0,3:T(2,128)(2,1)}), bf16[4,80,2,64]{1,2,0,3:T(2,128)(2,1)S(1)}, u32[]{:S(2)}, u32[]{:S(2)}) async-start(bf16[4,80,2,64]{1,2,0,3:T(2,128)(2,1)} %copy.62), calls=%async_computation | async-start | bytes 262144 | tf_op jit(solution)/shard_map/all_to_all | solution.py:63
  21.2 2.5 %copy-start.8 = (s32[4,4,4]{2,1,0:T(4,128)S(1)}, s32[4,4,4]{2,1,0:T(4,128)}, u32[]{:S(2)}) copy-start(s32[4,4,4]{2,1,0:T(4,128)} %param.13) | copy-start | bytes 772
  30.1 8.2 %collective-permute-start = (bf16[1280,2,4]{0,2,1:T(4,128)(2,1)S(1)}, bf16[1280,2,4]{0,2,1:T(4,128)(2,1)S(1)}, u32[]{:S(2)}, u32[]{:S(2)}) collective-permute-start(bf16[1280,2,4]{0,2,1:T(4,128)(2,1)S(1)} %convert_element_type.122), channel_id=1, source_target_pairs={{0,1},{1,2},{2,3},{3,4},{4,5},{5,6},{6,7},{7,8},{8,9},{9,10},{10,1... | collective-permute-start | bytes 61448 | tf_op jit(solution)/shard_map/ppermute | solution.py:37
  38.3 4.5 %collective-permute-start.1 = (bf16[1280,2,4]{0,2,1:T(4,128)(2,1)S(1)}, bf16[1280,2,4]{0,2,1:T(4,128)(2,1)S(1)}, u32[]{:S(2)}, u32[]{:S(2)}) collective-permute-start(bf16[1280,2,4]{0,2,1:T(4,128)(2,1)S(1)} %fusion.78), channel_id=1, source_target_pairs={{0,2},{1,3},{2,4},{3,5},{4,6},{5,7},{6,8},{7,9},{8,10},{9,11},{10,... | collective-permute-start | bytes 61448 | tf_op jit(solution)/shard_map/ppermute | solution.py:37
  42.9 5.4 %collective-permute-start.2 = (bf16[1280,2,4]{0,2,1:T(4,128)(2,1)S(1)}, bf16[1280,2,4]{0,2,1:T(4,128)(2,1)S(1)}, u32[]{:S(2)}, u32[]{:S(2)}) collective-permute-start(bf16[1280,2,4]{0,2,1:T(4,128)(2,1)S(1)} %fusion.89), channel_id=1, source_target_pairs={{0,4},{1,5},{2,6},{3,7},{4,8},{5,9},{6,10},{7,11},{8,12},{9,13},{1... | collective-permute-start | bytes 61448 | tf_op jit(solution)/shard_map/ppermute | solution.py:37
  46.2 20.4 %copy-start = (bf16[1284,1280]{1,0:T(8,128)(2,1)S(1)}, bf16[1284,1280]{1,0:T(8,128)(2,1)}, u32[]{:S(2)}) copy-start(bf16[1284,1280]{1,0:T(8,128)(2,1)} %slice.48) | copy-start | bytes 9861124
  48.3 4.5 %collective-permute-start.3 = (bf16[1280,2,4]{0,2,1:T(4,128)(2,1)S(1)}, bf16[1280,2,4]{0,2,1:T(4,128)(2,1)S(1)}, u32[]{:S(2)}, u32[]{:S(2)}) collective-permute-start(bf16[1280,2,4]{0,2,1:T(4,128)(2,1)S(1)} %fusion.79), channel_id=1, source_target_pairs={{0,8},{1,9},{2,10},{3,11},{4,12},{5,13},{6,14},{7,15},{16,24},{17,... | collective-permute-start | bytes 61448 | tf_op jit(solution)/shard_map/ppermute | solution.py:37
  52.9 17.9 %collective-permute-start.4 = (bf16[1280,2,4]{0,2,1:T(4,128)(2,1)S(1)}, bf16[1280,2,4]{0,2,1:T(4,128)(2,1)S(1)}, u32[]{:S(2)}, u32[]{:S(2)}) collective-permute-start(bf16[1280,2,4]{0,2,1:T(4,128)(2,1)S(1)} %add_convert_fusion.4), channel_id=1, source_target_pairs={{0,1},{1,2},{2,3},{3,4},{4,5},{5,6},{6,7},{7,8},{8,9},{9,10},{10,1... | collective-permute-start | bytes 61448 | tf_op jit(solution)/shard_map/ppermute | solution.py:42
  70.8 1.9 %copy-start.1 = (bf16[1284,1280]{1,0:T(8,128)(2,1)S(1)}, bf16[1284,1280]{1,0:T(8,128)(2,1)}, u32[]{:S(2)}) copy-start(bf16[1284,1280]{1,0:T(8,128)(2,1)} %slice.48) | copy-start | bytes 9861124
  70.8 3.0 %copy-start.4 = (f32[4,4,4,1284]{3,2,1,0:T(4,128)S(1)}, f32[4,4,4,1284]{3,2,1,0:T(4,128)}, u32[]{:S(2)}) copy-start(f32[4,4,4,1284]{3,2,1,0:T(4,128)} %reshape.192) | copy-start | bytes 986116
  70.8 3.0 %copy-start.5 = (f32[4,4,4,1284]{3,0,1,2:T(4,128)S(1)}, f32[4,4,4,1284]{3,0,1,2:T(4,128)}, u32[]{:S(2)}) copy-start(f32[4,4,4,1284]{3,0,1,2:T(4,128)} %fusion.28) | copy-start | bytes 986116
  70.8 3.0 %copy-start.6 = (f32[4,4,4,1284]{3,0,1,2:T(4,128)S(1)}, f32[4,4,4,1284]{3,0,1,2:T(4,128)}, u32[]{:S(2)}) copy-start(f32[4,4,4,1284]{3,0,1,2:T(4,128)} %reduce_window_sum.11) | copy-start | bytes 986116
  70.9 3.0 %copy-start.9 = (f32[4,4,4]{0,2,1:T(4,128)S(1)}, f32[4,4,4]{0,2,1:T(4,128)}, u32[]{:S(2)}) copy-start(f32[4,4,4]{0,2,1:T(4,128)} %copy.57) | copy-start | bytes 772
  70.9 3.0 %copy-start.11 = (f32[4]{0:T(128)S(1)}, f32[4]{0:T(128)}, u32[]{:S(2)}) copy-start(f32[4]{0:T(128)} %param.15) | copy-start | bytes 52
  70.9 3.0 %copy-start.12 = (s32[1,4]{1,0:T(1,128)S(1)}, s32[1,4]{1,0:T(1,128)}, u32[]{:S(2)}) copy-start(s32[1,4]{1,0:T(1,128)} %param.14) | copy-start | bytes 52
  85.9 13.5 %all-to-all-start.1 = ((bf16[16,2,1280]{2,1,0:T(2,128)(2,1)}), bf16[16,2,1280]{2,1,0:T(2,128)(2,1)S(1)}, u32[]{:S(2)}, u32[]{:S(2)}) async-start(bf16[16,2,1280]{2,1,0:T(2,128)(2,1)} %reshape.202), calls=%async_computation.1 | async-start | bytes 163840 | tf_op jit(solution)/shard_map/all_to_all | solution.py:105
  109.0 4.2 %copy-start.3 = (pred[80,1280]{1,0:T(8,128)(4,1)S(1)}, pred[80,1280]{1,0:T(8,128)(4,1)}, u32[]{:S(2)}) copy-start(pred[80,1280]{1,0:T(8,128)(4,1)} %copy-done.2) | copy-start | bytes 307204

commit v2 on v1

v2 whole, which is shorter than its diff:
```python
import functools
import math

import jax
import jax.numpy as jnp
from jax import lax
from jax.experimental import pallas as pl
from jax.experimental.pallas import tpu as pltpu
from jax.sharding import PartitionSpec as P

F32, BF16, I32 = jnp.float32, jnp.bfloat16, jnp.int32
GROUP = 8


def iota(shape, dim):
    return lax.broadcasted_iota(I32, shape, dim)


def matmul(a, b, ca, cb):
    return lax.dot_general(a, b, (((ca,), (cb,)), ((), ())), preferred_element_type=F32)


def one_hot(rows, cols):
    return jnp.where(rows == cols, 1.0, 0.0).astype(BF16)


def synthesis_kernel(limit_ref, weight_ref, adj_ref, leg_ref, out_ref, acc_ref):
    step = pl.program_id(0)
    levels, groups_slots, comps, degrees = adj_ref.shape
    rows = GROUP * comps
    heights = leg_ref.shape[1]
    for part in range(groups_slots // GROUP):
        here = pl.ds(part * GROUP, GROUP)
        limit = limit_ref[pl.ds(part * rows, rows), :]
        degree = iota((rows, degrees), 1)
        inside = degree < limit
        even = jnp.where(inside & (degree % 2 == 0), 1.0, 0.0).astype(BF16)
        odd = jnp.where(inside & (degree % 2 == 1), 1.0, 0.0).astype(BF16)
        values = [adj_ref[l, here].reshape(rows, degrees) for l in range(levels)]
        left = jnp.concatenate([v * even for v in values] + [v * odd for v in values], axis=0)
        table = leg_ref[here].reshape(GROUP * heights, degrees)
        both = matmul(left, table, 1, 1)
        shape = both.shape
        own = (iota(shape, 0) % rows) // comps == iota(shape, 1) // heights
        both = jnp.where(own, both, 0.0)
        both = both[:, :128] + both[:, 128:]
        both = both + pltpu.roll(both, 64, 1)
        both = both + pltpu.roll(both, 32, 1)
        half = levels * rows
        from_even, from_odd = both[:half], both[half:]
        north = (from_even + from_odd) * weight_ref[...]
        south = (from_even - from_odd) * weight_ref[...]
        at = step * (groups_slots // GROUP) + part
        for l in range(levels):
            acc_ref[l, pl.ds(at * rows, rows), :] = north[l * rows : (l + 1) * rows]
            acc_ref[levels + l, pl.ds(at * rows, rows), :] = south[l * rows : (l + 1) * rows]

    @pl.when(step == pl.num_programs(0) - 1)
    def _():
        total = acc_ref.shape[1]
        slots = total // comps
        sides = 2 * levels
        lane = iota((total, 128), 1) // heights
        blocks = []
        for k in range(sides // 4):
            mix = acc_ref[4 * k]
            for r in range(1, 4):
                mix = jnp.where(lane == r, acc_ref[4 * k + r], mix)
            blocks.append(mix.astype(BF16))
        wide = jnp.concatenate(blocks, axis=1)
        col = iota((total, 2 * 128), 1)
        source = iota((total, 2 * 128), 0)
        comp, slot = col // 128, col % 128
        spread = jnp.where((source == slot * comps + comp) & (slot < slots), 1.0, 0.0).astype(BF16)
        turned = matmul(wide, spread, 0, 0).astype(BF16)
        size = sides * heights
        dest = iota((size, size), 0)
        origin = iota((size, size), 1)
        band, e, hh, l = dest // 16, dest // 8 % 2, dest // 4 % 2, dest % 4
        wanted = (e * levels + l) * heights + band * 2 + hh
        moved = matmul(one_hot(wanted, origin), turned, 1, 0).astype(BF16)
        for d in range(size // 16):
            for c in range(comps):
                out_ref[d, c] = moved[16 * d : 16 * d + 16, 128 * c : 128 * c + slots]


def synthesis(adj, leg, limit, weight):
    levels, slots, comps, degrees = adj.shape
    heights = leg.shape[1]
    wide = 16
    steps = slots // wide
    limit = jnp.repeat(limit, comps)[:, None]
    weight = jnp.tile(weight, 128 // heights)[None, :]
    return pl.pallas_call(
        synthesis_kernel,
        grid=(steps,),
        in_specs=[
            pl.BlockSpec((wide * comps, 1), lambda i: (i, 0)),
            pl.BlockSpec((1, 128), lambda i: (0, 0)),
            pl.BlockSpec((levels, wide, comps, degrees), lambda i: (0, i, 0, 0)),
            pl.BlockSpec((wide, heights, degrees), lambda i: (i, 0, 0)),
        ],
        out_specs=pl.BlockSpec((16, comps, 16, slots), lambda i: (0, 0, 0, 0)),
        out_shape=jax.ShapeDtypeStruct((16, comps, 16, slots), BF16),
        scratch_shapes=[pltpu.VMEM((2 * levels, slots * comps, 128), F32)],
        compiler_params=pltpu.CompilerParams(vmem_limit_bytes=40 * 2**20),
        name="synthesis",
    )(limit, weight, adj, leg)


def analysis_kernel(limit_ref, in_ref, leg_ref, out_ref, left_ref):
    step = pl.program_id(0)
    levels, wide, comps, degrees = out_ref.shape
    heights = leg_ref.shape[1]
    sources, _, sub, slots = in_ref.shape
    rows = GROUP * comps
    kinds = 2 * levels

    @pl.when(step == 0)
    def _():
        size = sources * sub
        row = iota((size, kinds * 128), 0)
        col = iota((size, kinds * 128), 1)
        row_key = (row // 8 % 2 * levels + row % 4) * heights + row // 16 * 2 + row // 4 % 2
        pick = one_hot(row_key, col // 128 * heights + col % heights)
        parts = []
        for c in range(comps):
            flat = jnp.concatenate([in_ref[d, c] for d in range(sources)], axis=0)
            parts.append(matmul(flat, pick, 0, 0).astype(BF16))
        apart = jnp.concatenate(parts, axis=0)
        total = slots * comps
        row = iota((total, total), 0)
        col = iota((total, total), 1)
        weave = one_hot(row % comps * slots + row // comps, col)
        left_ref[...] = matmul(weave, apart, 1, 0).astype(BF16)

    for part in range(wide // GROUP):
        at = step * (wide // GROUP) + part
        here = left_ref[pl.ds(pl.multiple_of(at * rows, rows), rows), :]
        stack = jnp.concatenate([here[:, 128 * k : 128 * k + 128] for k in range(kinds)], axis=0)
        left = jnp.concatenate([stack, stack], axis=1)
        shape = left.shape
        own = (iota(shape, 0) % rows) // comps == iota(shape, 1) // heights
        left = left * jnp.where(own, 1.0, 0.0).astype(BF16)
        table = leg_ref[pl.ds(part * GROUP, GROUP)].reshape(GROUP * heights, degrees)
        both = matmul(left, table, 1, 0)
        limit = limit_ref[pl.ds(part * rows, rows), :]
        degree = iota((rows, degrees), 1)
        inside = degree < limit
        even = degree % 2 == 0
        half = levels * rows
        for l in range(levels):
            sym = both[l * rows : (l + 1) * rows]
            anti = both[half + l * rows : half + (l + 1) * rows]
            value = jnp.where(inside, jnp.where(even, sym, anti), 0.0).astype(BF16)
            out_ref[l, pl.ds(part * GROUP, GROUP)] = value.reshape(GROUP, comps, degrees)


def analysis(sides, leg, limit, levels):
    sources, comps, sub, slots = sides.shape
    heights, degrees = leg.shape[1:]
    wide = 16
    limit = jnp.repeat(limit, comps)[:, None]
    return pl.pallas_call(
        analysis_kernel,
        grid=(slots // wide,),
        in_specs=[
            pl.BlockSpec((wide * comps, 1), lambda i: (i, 0)),
            pl.BlockSpec(sides.shape, lambda i: (0, 0, 0, 0)),
            pl.BlockSpec((wide, heights, degrees), lambda i: (i, 0, 0)),
        ],
        out_specs=pl.BlockSpec((levels, wide, comps, degrees), lambda i: (0, i, 0, 0)),
        out_shape=jax.ShapeDtypeStruct((levels, slots, comps, degrees), BF16),
        scratch_shapes=[pltpu.VMEM((slots * comps, 2 * levels * 128), BF16)],
        compiler_params=pltpu.CompilerParams(vmem_limit_bytes=40 * 2**20),
        name="analysis",
    )(limit, sides, leg)

NBLK = 4


def turns(wave, b):
    turn = (wave * b) & 3
    cos_b = jnp.where(turn == 0, 1.0, jnp.where(turn == 2, -1.0, 0.0))
    sin_b = jnp.where(turn == 1, 1.0, jnp.where(turn == 3, -1.0, 0.0))
    return cos_b, sin_b


def table_kernel(cos_low_ref, sin_low_ref, cos_high_ref, sin_high_ref, cos_ref, sin_ref):
    low = cos_low_ref.shape[0]

    @pl.loop(0, cos_high_ref.shape[0])
    def _(i):
        cos_high = cos_high_ref[pl.ds(i, 1), :]
        sin_high = sin_high_ref[pl.ds(i, 1), :]
        cos_low, sin_low = cos_low_ref[...], sin_low_ref[...]
        at = pl.ds(pl.multiple_of(i * low, low), low)
        cos_ref[at, :] = (cos_high * cos_low - sin_high * sin_low).astype(BF16)
        sin_ref[at, :] = (-(sin_high * cos_low + cos_high * sin_low)).astype(BF16)


def angles(wave_ids, lon_ids, lon_count):
    phase = lon_ids[:, None] * wave_ids[None, :] % lon_count
    angle = phase.astype(F32) * (2.0 * math.pi / lon_count)
    return jnp.cos(angle), jnp.sin(angle)


def quarter_table(wave_ids, width, lon_count):
    low_count = 16
    steps = -(-width // low_count)
    low = angles(wave_ids, jnp.arange(low_count, dtype=I32), lon_count)
    high = angles(wave_ids, jnp.arange(steps, dtype=I32) * low_count, lon_count)
    shape = jax.ShapeDtypeStruct((steps * low_count, wave_ids.shape[0]), BF16)
    return pl.pallas_call(
        table_kernel,
        out_shape=(shape, shape),
        compiler_params=pltpu.CompilerParams(vmem_limit_bytes=24 * 2**20),
        cost_estimate=pl.CostEstimate(flops=12_000_000, bytes_accessed=8_000_000, transcendentals=0),
        name="trig_table",
    )(*low, *high)


def gather_kernel(in_ref, out_ref, total_ref):
    sources, comps, sub, slots = in_ref.shape
    rows = iota((8, comps * sub), 0)
    cols = iota((8, comps * sub), 1)
    pick = one_hot(cols // 4, rows)
    flat = []
    for c in range(comps):
        flat.append(jnp.concatenate([in_ref[d, c] for d in range(sources)], axis=1))
        out_ref[c] = flat[-1]
    total_ref[...] = matmul(pick, jnp.concatenate(flat, axis=0), 1, 0).astype(BF16)


def gather_rows(blocks):
    sources, comps, sub, slots = blocks.shape
    return pl.pallas_call(
        gather_kernel,
        out_shape=(
            jax.ShapeDtypeStruct((comps, sub, sources * slots), BF16),
            jax.ShapeDtypeStruct((comps * sub // 4, sources * slots), BF16),
        ),
        name="gather_rows",
    )(blocks)


def to_longitudes(first, second, wave, cos_ref, sin_ref):
    with_cos, with_sin = [], []
    for b in range(NBLK):
        cos_b, sin_b = (v.astype(BF16) for v in turns(wave, b))
        with_cos.append(first * cos_b - second * sin_b)
        with_sin.append(first * sin_b + second * cos_b)
    with_cos = jnp.concatenate(with_cos, axis=0)
    with_sin = jnp.concatenate(with_sin, axis=0)
    return matmul(with_cos, cos_ref[...], 1, 1) + matmul(with_sin, sin_ref[...], 1, 1)


def grid_kernel(four_ref, wave_ref, coef_ref, scale_ref, pick_ref, traj_ref, cos_ref, sin_ref, sum_ref, gain_ref, *, width, norm):
    grid = to_longitudes(four_ref[0], four_ref[1], wave_ref[...], cos_ref, sin_ref)
    level = iota(grid.shape, 0) % 4
    prior = jnp.where(level >= 1, pltpu.roll(grid, 1, 0), 0.0)
    prior = prior + jnp.where(level >= 2, pltpu.roll(grid, 2, 0), 0.0)
    prior = prior + jnp.where(level >= 3, pltpu.roll(grid, 3, 0), 0.0)
    sum_ref[...] = grid + coef_ref[...] * prior
    levels, lats, lons = traj_ref.shape
    stored = jnp.concatenate([traj_ref[r] for r in range(levels)], axis=0)
    ordered = matmul(pick_ref[...], stored, 1, 0)
    sub = levels * lats
    full = cos_ref.shape[0]
    for b in range(NBLK):
        piece = ordered[:, b * width : (b + 1) * width] * scale_ref[b * sub : (b + 1) * sub, :]
        gain = norm * (1.0 + jnp.tanh(piece))
        gain_ref[b * sub : (b + 1) * sub, :] = jnp.concatenate(
            [gain, jnp.zeros((sub, full - width), F32)], axis=1
        )


def grid_part(four, wave, coef, scale, pick, traj, cos_t, sin_t, width, norm):
    shape = jax.ShapeDtypeStruct((NBLK * four.shape[1], cos_t.shape[0]), F32)
    return pl.pallas_call(
        functools.partial(grid_kernel, width=width, norm=norm),
        out_shape=(shape, shape),
        compiler_params=pltpu.CompilerParams(vmem_limit_bytes=40 * 2**20),
        cost_estimate=pl.CostEstimate(flops=450_000_000, bytes_accessed=8_000_000, transcendentals=100_000),
        name="grid_part",
    )(four, wave, coef, scale, pick, traj, cos_t, sin_t)


def forcing_kernel(index_ref, total_ref, wave_ref, coef_ref, sum_ref, gain_ref, cos_ref, sin_ref, out_ref, *, norm):
    me = index_ref[0]
    groups, rows, waves = total_ref.shape
    carry = jnp.zeros((rows, waves), F32)
    for g in range(groups):
        carry = carry + jnp.where(g < me, total_ref[g].astype(F32), 0.0)
    sub = 16
    copies = one_hot(iota((2 * sub, rows), 0) // 4, iota((2 * sub, rows), 1))
    spread = matmul(copies, carry.astype(BF16), 1, 0).astype(BF16)
    wave = wave_ref[...]
    group = to_longitudes(spread[:sub], spread[sub:], wave, cos_ref, sin_ref)
    forcing = (gain_ref[...] * (sum_ref[...] + coef_ref[...] * group)).astype(BF16)
    by_cos = matmul(forcing, cos_ref[...], 1, 0)
    by_sin = matmul(forcing, sin_ref[...], 1, 0)
    first = jnp.zeros((sub, waves), F32)
    second = jnp.zeros((sub, waves), F32)
    for b in range(NBLK):
        cos_b, sin_b = turns(wave, b)
        part_cos, part_sin = by_cos[b * sub : (b + 1) * sub], by_sin[b * sub : (b + 1) * sub]
        first = first + part_cos * cos_b + part_sin * sin_b
        second = second + part_sin * cos_b - part_cos * sin_b
    bands, comps, _, slots = out_ref.shape
    half = sub // 2
    for c, value in enumerate((first, second)):
        value = value * norm
        sym, anti = value[:half] + value[half:], value[:half] - value[half:]
        sides = jnp.concatenate([sym, anti], axis=0).astype(BF16)
        for d in range(bands):
            out_ref[d, c] = sides[:, slots * d : slots * (d + 1)]


def forcing_part(index, totals, wave, coef, sums, gain, cos_t, sin_t, shape, norm):
    vmem = pl.BlockSpec(memory_space=pltpu.VMEM)
    return pl.pallas_call(
        functools.partial(forcing_kernel, norm=norm),
        in_specs=[pl.BlockSpec(memory_space=pltpu.SMEM)] + [vmem] * 7,
        out_specs=vmem,
        out_shape=jax.ShapeDtypeStruct(shape, BF16),
        compiler_params=pltpu.CompilerParams(vmem_limit_bytes=40 * 2**20),
        cost_estimate=pl.CostEstimate(flops=900_000_000, bytes_accessed=8_000_000, transcendentals=0),
        name="forcing_part",
    )(index, totals, wave, coef, sums, gain, cos_t, sin_t)


def body(adj_spec, wave_of_slot, legendre, lat_weight, traj, traj_exp, traj_order, lev_coef):
    levels, slots, _, degrees = adj_spec.shape
    lats, lon_count = traj.shape[1:]
    width = lon_count // NBLK
    norm = 1.0 / math.sqrt(degrees)
    waves_here = lax.dynamic_slice_in_dim(wave_of_slot, lax.axis_index("band") * slots, slots)
    limit = degrees - waves_here
    blocks = synthesis(adj_spec, legendre, limit, lat_weight)
    blocks = lax.all_to_all(blocks, "band", split_axis=0, concat_axis=0, tiled=True)
    cos_t, sin_t = quarter_table(wave_of_slot, width, lon_count)
    four, total = gather_rows(blocks)
    totals = lax.all_gather(total, "lev")

    wave = wave_of_slot[None, :]
    row = jnp.arange(NBLK * lats * levels, dtype=I32)
    blk, side, pair, level = row // 16, row // 8 % 2, row // 4 % 2, row % 4
    stored = jnp.argmax(traj_order[0][None, :] == jnp.arange(levels, dtype=I32)[:, None], axis=1)
    stored_row = stored[level]
    lat = 2 * pair + side
    scale = jnp.exp2(traj_exp[stored_row, lat, blk].astype(F32))[:, None]
    coef = lev_coef[level][:, None]
    source = (stored_row * lats + lat)[:16]
    pick = (source[:, None] == jnp.arange(16, dtype=I32)[None, :]).astype(BF16)
    sums, gain = grid_part(four, wave, coef, scale, pick, traj, cos_t, sin_t, width, norm)
    index = lax.axis_index("lev").astype(I32)[None]
    sides = forcing_part(index, totals, wave, coef, sums, gain, cos_t, sin_t, blocks.shape, norm)
    sides = lax.all_to_all(sides, "band", split_axis=0, concat_axis=0, tiled=True)
    return analysis(sides, legendre, limit, levels)


def solution(mesh):
    return jax.shard_map(
        body,
        mesh=mesh,
        in_specs=(
            P("lev", "band", None, None),
            P(),
            P("band", None, None),
            P(),
            P("lev", "band", None),
            P("lev", "band", None),
            P("lev", None),
            P("lev"),
        ),
        out_specs=P("lev", "band", None, None),
        check_vma=False,
    )
```

time: 118 us -> 89.4 us (0.76)
  the two profiles are of different devices: /device:TPU:97 before, /device:TPU:1 now
where the time goes in v2:
time: 89.4 us; the launch traced here: 88.8 us
  blocking collectives  35.4 us (40%)
  Pallas kernels  19.3 us (22%)
  local copies, waits for them, and re-layouts  16 us (18%)
  other arithmetic  10.4 us (12%)
  starting transfers between devices  7.64 us (9%)
    all_gather x1, blocking collectives, body(): totals = lax.all_gather(total, 'lev')  21.9 us
    all_to_all x1, blocking collectives, body(): lax.all_to_all(sides, 'band', split_axis=0, concat_axis=0, tiled=True)  13.5 us
    unnamed x30, local copies, waits for them, and re-layouts  12.7 us
    all_to_all x1, starting transfers between devices, body(): lax.all_to_all(blocks, 'band', split_axis=0, concat_axis=0, tiled=True)  7.64 us
    pallas_call x1, Pallas kernels, synthesis(): pl.pallas_call(synthesis_kernel, grid=(steps,), in_specs=[pl.BlockSpec((w...  5.25 us
    pallas_call x1, Pallas kernels, analysis(): pl.pallas_call(analysis_kernel, grid=(slots // wide,), in_specs=[pl.Block...  3.84 us
    sin x2, other arithmetic, angles(): return (jnp.cos(angle), jnp.sin(angle))  3.72 us
    pallas_call x1, Pallas kernels, forcing_part(): pl.pallas_call(functools.partial(forcing_kernel, norm=norm), in_specs=[pl...  3.63 us
  transfers between devices with their start and end apart: 1, of which 0 were waited for; matrix products, arithmetic and copies ran while one was open for 14% of the time, Pallas kernels for 3%

profile of v2, /device:TPU:1, one launch (start us, length us, event | category | flops | bytes accessed | tf_op | source)
XLA Modules:
  0.0 88.8 jit_solution(13044731305522890927)
XLA Ops:
  0.0 0.0 copy-start
  0.0 0.8 dynamic-slice_subtract_fusion
  0.8 0.1 broadcast_in_dim.8
  0.9 0.1 broadcast_in_dim_reshape.5.limit_ref
  0.9 0.7 tile.2
  1.6 0.1 broadcast_in_dim_tile.3.weight_ref
  1.7 2.9 %copy-done.1 = bf16[80,32,1280]{2,1,0:T(8,128)(2,1)S(1)} copy-done((bf16[80,32,1280]{2,1,0:T(8,128)(2,1)S(1)}, bf16[80,32,1280]{2,1,0:T(8,128)(2,1)}, u32[]{:S(2)}) %copy-start.1) | copy-done | bytes 6553624
  4.6 0.0 copy-start.6
  4.6 1.4 %copy-done.6 = bf16[4,80,2,1280]{3,2,1,0:T(2,128)(2,1)S(1)} copy-done((bf16[4,80,2,1280]{3,2,1,0:T(2,128)(2,1)S(1)}, bf16[4,80,2,1280]{3,2,1,0:T(2,128)(2,1)}, u32[]{:S(2)}) %copy-start.6) | copy-done | bytes 1638424
  6.0 0.0 copy-start.10
  6.0 0.0 copy-start.12
  6.0 0.0 copy-start.11
  6.0 5.3 %synthesis.1 = bf16[16,2,16,80]{3,2,1,0:T(8,128)(2,1)} custom-call(s32[160,1]{1,0:T(8,128)S(1)} %broadcast_in_dim_reshape.5.limit_ref, f32[1,128]{1,0:T(1,128)S(1)} %broadcast_in_dim_tile.3.weight_ref, bf16[4,80,2,1280]{3,2,1,0:T(2,128)(2,1)S(1)} %copy-done.6, bf16[80,32,1280]{2,1,0:T(8,128)(2,1)S(1)} %copy-done.1), custom_call_target="tpu_custom_call" | custom-call | tf_op jit(solution)/shard_map/synthesis/pallas_call | solution.py:94
  11.2 7.6 %all-to-all-start = ((bf16[16,2,16,80]{3,2,1,0:T(8,128)(2,1)}), bf16[16,2,16,80]{3,2,1,0:T(8,128)(2,1)}, u32[]{:S(2)}, u32[]{:S(2)}) async-start(bf16[16,2,16,80]{3,2,1,0:T(8,128)(2,1)} %synthesis.1), calls=%async_computation | async-start | bytes 262144 | tf_op jit(solution)/shard_map/all_to_all | solution.py:341
  18.9 0.0 copy-done.10
  18.9 1.0 %fusion.11 = (f32[16,1280]{1,0:T(8,128)S(1)}, f32[16,1280]{1,0:T(8,128)}) fusion(s32[1280]{0:T(1024)S(1)} %copy-done.10), kind=kLoop, calls=%fused_computation.20 | loop fusion | flops 184320 | bytes 168960 | tf_op jit(solution)/shard_map/sin | solution.py:205
  19.9 0.0 copy-done.12
  19.9 0.6 iota_reduce_fusion
  20.5 0.7 fusion.45
  21.2 2.7 %fusion.28 = (s32[64]{0:T(128)S(1)}, s32[64]{0:T(128)S(1)}) fusion(s32[]{:T(128)} %bitcast.7, s32[]{:T(128)} %bitcast.8, s32[]{:T(128)} %bitcast.10, s32[]{:T(128)} %bitcast.9), kind=kLoop, calls=%fused_computation.53 | loop fusion | flops 4800 | bytes 528 | tf_op jit(solution)/shard_map/concatenate | solution.py:352
  23.9 0.0 copy-done
  23.9 1.0 %gather_fusion = s32[64]{0:T(128)S(1)} fusion(s32[4,4,4]{2,1,0:T(4,128)S(1)} %copy-done, s32[64]{0:T(128)S(1)} %get-tuple-element.31), kind=kCustom, calls=%fused_computation | custom fusion | bytes 1280 | tf_op jit(solution)/shard_map/gather | solution.py:352
  24.8 0.1 copy.14.scale_ref
  24.9 0.0 copy-done.11
  24.9 0.7 fusion.46
  25.6 0.1 fusion.39.pick_ref
  25.7 2.7 %fusion.4 = (f32[81,1280]{1,0:T(8,128)}, f32[81,1280]{1,0:T(8,128)}) fusion(s32[1280]{0:T(1024)S(1)} %copy-done.10, s32[81]{0:T(128)S(1)} %iota_multiply_fusion), kind=kLoop, calls=%fused_computation.7 | loop fusion | flops 933120 | bytes 834884 | tf_op jit(solution)/shard_map/sin | solution.py:205
  28.4 0.0 copy-start.4
  28.4 1.0 %copy-done.4 = f32[81,1280]{1,0:T(8,128)S(1)} copy-done((f32[81,1280]{1,0:T(8,128)S(1)}, f32[81,1280]{1,0:T(8,128)}, u32[]{:S(2)}) %copy-start.4) | copy-done | bytes 414744
  29.5 1.0 %copy-done.5 = f32[81,1280]{1,0:T(8,128)S(1)} copy-done((f32[81,1280]{1,0:T(8,128)S(1)}, f32[81,1280]{1,0:T(8,128)}, u32[]{:S(2)}) %copy-start.5) | copy-done | bytes 414744
  30.5 0.9 copy-done.7
  31.4 2.6 %trig_table.1 = (bf16[1296,1280]{1,0:T(8,128)(2,1)S(1)}, bf16[1296,1280]{1,0:T(8,128)(2,1)S(1)}) custom-call(f32[16,1280]{1,0:T(8,128)S(1)} %copy-done.7, f32[16,1280]{1,0:T(8,128)S(1)} %get-tuple-element.21.sin_low_ref, f32[81,1280]{1,0:T(8,128)S(1)} %copy-done.5, f32[81,1280]{1,0:T(8,128)S(1)} %copy-done.4), custom_call_target="tpu_custom_call" | custom-call | flops 12000000 | bytes 8000000 | tf_op jit(solution)/shard_map/trig_table/pallas_call | solution.py:214
  34.0 0.0 copy-start.2
  34.0 1.7 %copy-done.2 = bf16[1296,1280]{1,0:T(8,128)(2,1)} copy-done((bf16[1296,1280]{1,0:T(8,128)(2,1)}, bf16[1296,1280]{1,0:T(8,128)(2,1)S(1)}, u32[]{:S(2)}) %copy-start.2) | copy-done | bytes 3317784
  35.7 2.5 %select_select_fusion.1.coef_ref = f32[64,1]{1,0:T(8,128)S(1)} fusion(f32[]{:T(128)} %bitcast.2, f32[]{:T(128)} %bitcast.3, f32[]{:T(128)} %bitcast.5, f32[]{:T(128)} %bitcast.4), kind=kLoop, calls=%fused_computation.60 | loop fusion | flops 960 | bytes 272 | tf_op jit(solution)/shard_map/gather | solution.py:353
  38.2 0.0 all-to-all-done.in_ref
  38.2 1.7 %gather_rows.1 = (bf16[2,16,1280]{2,1,0:T(8,128)(2,1)}, bf16[8,1280]{1,0:T(8,128)(2,1)}) custom-call(bf16[16,2,16,80]{3,2,1,0:T(8,128)(2,1)} %all-to-all-done.in_ref), custom_call_target="tpu_custom_call" | custom-call | tf_op jit(solution)/shard_map/gather_rows/pallas_call | solution.py:237
  40.0 21.9 %all-gather = bf16[128,1280]{1,0:T(8,128)(2,1)S(1)} all-gather(bf16[8,1280]{1,0:T(8,128)(2,1)} %get-tuple-element.12), channel_id=2, replica_groups=mesh['band'=16,'lev'=16] {'lev'}, dimensions={0}, use_global_device_ids=true | all-gather | bytes 348160 | tf_op jit(solution)/shard_map/all_gather | solution.py:344
  61.8 1.9 %copy-done.3 = bf16[1296,1280]{1,0:T(8,128)(2,1)S(1)} copy-done((bf16[1296,1280]{1,0:T(8,128)(2,1)S(1)}, bf16[1296,1280]{1,0:T(8,128)(2,1)}, u32[]{:S(2)}) %copy-start.3) | copy-done | bytes 3317784
  63.8 0.9 %copy-done.8 = bf16[4,4,5136]{2,1,0:T(4,128)(2,1)S(1)} copy-done((bf16[4,4,5136]{2,1,0:T(4,128)(2,1)S(1)}, bf16[4,4,5136]{2,1,0:T(4,128)(2,1)}, u32[]{:S(2)}) %copy-start.8) | copy-done | bytes 164376
  64.7 0.9 copy-done.9
  65.6 2.2 %grid_part.1 = (f32[64,1296]{1,0:T(8,128)S(1)}, f32[64,1296]{1,0:T(8,128)S(1)}) custom-call(bf16[2,16,1280]{2,1,0:T(8,128)(2,1)S(1)} %copy-done.9, s32[1,1280]{1,0:T(1,128)S(1)} %broadcast_in_dim.10.wave_ref, f32[64,1]{1,0:T(8,128)S(1)} %select_select_fusion.1.coef_ref, f32[64,1]{1,0:T(8,128)S(1)} %copy.14.scale_ref, bf16[16,16]{1,0:T(8,128)(2,1)S(1)} %fusion.39.pick_ref, ...), custom_call_target="tpu_custom_call" | custom-call | flops 450000000 | bytes 8000000 | tf_op jit(solution)/shard_map/grid_part/pallas_call | solution.py:280
  67.8 0.0 slice-start.1
  67.8 3.6 %forcing_part.1 = bf16[16,2,16,80]{3,2,1,0:T(8,128)(2,1)S(1)} custom-call(s32[1]{0:T(128)} %bitcast.index_ref, bf16[16,8,1280]{2,1,0:T(8,128)(2,1)S(1)} %bitcast.16, s32[1,1280]{1,0:T(1,128)S(1)} %broadcast_in_dim.10.wave_ref, f32[64,1]{1,0:T(8,128)S(1)} %select_select_fusion.1.coef_ref, f32[64,1296]{1,0:T(8,128)S(1)} %get-tuple-element.17.sum_ref, ...), custom_call_target="tpu_custom_call" | custom-call | flops 900000000 | bytes 8000000 | tf_op jit(solution)/shard_map/forcing_part/pallas_call | solution.py:322
  71.4 13.5 %all_to_all.10.in_ref = bf16[16,2,16,80]{3,2,1,0:T(8,128)(2,1)S(1)} all-to-all(bf16[16,2,16,80]{3,2,1,0:T(8,128)(2,1)S(1)} %forcing_part.1), channel_id=1, replica_groups=mesh['band'=16,'lev'=16] {'band'}, dimensions={0} | all-to-all | bytes 163840 | tf_op jit(solution)/shard_map/all_to_all | solution.py:359
  85.0 0.0 slice-done
  85.0 0.0 slice-done.1
  85.0 3.8 %analysis.1 = bf16[4,80,2,1280]{3,2,1,0:T(2,128)(2,1)} custom-call(s32[160,1]{1,0:T(8,128)S(1)} %broadcast_in_dim_reshape.5.limit_ref, bf16[16,2,16,80]{3,2,1,0:T(8,128)(2,1)S(1)} %all_to_all.10.in_ref, bf16[80,32,1280]{2,1,0:T(8,128)(2,1)S(1)} %bitcast.15), custom_call_target="tpu_custom_call" | custom-call | tf_op jit(solution)/shard_map/analysis/pallas_call | solution.py:164
  (12 shorter events, 0.0 us)
Async XLA Ops:
  0.0 23.9 %copy-start = (s32[4,4,4]{2,1,0:T(4,128)S(1)}, s32[4,4,4]{2,1,0:T(4,128)}, u32[]{:S(2)}) copy-start(s32[4,4,4]{2,1,0:T(4,128)} %param.13) | copy-start | bytes 772
  1.7 2.9 %copy-start.1 = (bf16[80,32,1280]{2,1,0:T(8,128)(2,1)S(1)}, bf16[80,32,1280]{2,1,0:T(8,128)(2,1)}, u32[]{:S(2)}) copy-start(bf16[80,32,1280]{2,1,0:T(8,128)(2,1)} %leg_ref.3) | copy-start | bytes 19660804
  4.6 1.4 %copy-start.6 = (bf16[4,80,2,1280]{3,2,1,0:T(2,128)(2,1)S(1)}, bf16[4,80,2,1280]{3,2,1,0:T(2,128)(2,1)}, u32[]{:S(2)}) copy-start(bf16[4,80,2,1280]{3,2,1,0:T(2,128)(2,1)} %adj_ref.1) | copy-start | bytes 4915204
  6.0 12.9 %copy-start.10 = (s32[1280]{0:T(1024)S(1)}, s32[1280]{0:T(1024)}, u32[]{:S(2)}) copy-start(s32[1280]{0:T(1024)} %param.9) | copy-start | bytes 15364
  6.0 13.9 %copy-start.12 = (s32[1,4]{1,0:T(1,128)S(1)}, s32[1,4]{1,0:T(1,128)}, u32[]{:S(2)}) copy-start(s32[1,4]{1,0:T(1,128)} %param.14) | copy-start | bytes 52
  6.0 18.9 %copy-start.11 = (f32[4]{0:T(128)S(1)}, f32[4]{0:T(128)}, u32[]{:S(2)}) copy-start(f32[4]{0:T(128)} %param.15) | copy-start | bytes 52
  11.2 27.0 %all-to-all-start = ((bf16[16,2,16,80]{3,2,1,0:T(8,128)(2,1)}), bf16[16,2,16,80]{3,2,1,0:T(8,128)(2,1)}, u32[]{:S(2)}, u32[]{:S(2)}) async-start(bf16[16,2,16,80]{3,2,1,0:T(8,128)(2,1)} %synthesis.1), calls=%async_computation | async-start | bytes 262144 | tf_op jit(solution)/shard_map/all_to_all | solution.py:341
  28.4 1.0 %copy-start.4 = (f32[81,1280]{1,0:T(8,128)S(1)}, f32[81,1280]{1,0:T(8,128)}, u32[]{:S(2)}) copy-start(f32[81,1280]{1,0:T(8,128)} %get-tuple-element.19.sin_high_ref) | copy-start | bytes 1244164
  29.5 1.0 %copy-start.5 = (f32[81,1280]{1,0:T(8,128)S(1)}, f32[81,1280]{1,0:T(8,128)}, u32[]{:S(2)}) copy-start(f32[81,1280]{1,0:T(8,128)} %get-tuple-element.20.cos_high_ref) | copy-start | bytes 1244164
  30.5 0.9 copy-start.7
  34.0 1.7 %copy-start.2 = (bf16[1296,1280]{1,0:T(8,128)(2,1)}, bf16[1296,1280]{1,0:T(8,128)(2,1)S(1)}, u32[]{:S(2)}) copy-start(bf16[1296,1280]{1,0:T(8,128)(2,1)S(1)} %get-tuple-element.16.sin_ref) | copy-start | bytes 9953284
  61.8 1.9 %copy-start.3 = (bf16[1296,1280]{1,0:T(8,128)(2,1)S(1)}, bf16[1296,1280]{1,0:T(8,128)(2,1)}, u32[]{:S(2)}) copy-start(bf16[1296,1280]{1,0:T(8,128)(2,1)} %copy-done.2) | copy-start | bytes 9953284
  63.8 0.9 %copy-start.8 = (bf16[4,4,5136]{2,1,0:T(4,128)(2,1)S(1)}, bf16[4,4,5136]{2,1,0:T(4,128)(2,1)}, u32[]{:S(2)}) copy-start(bf16[4,4,5136]{2,1,0:T(4,128)(2,1)} %traj_ref.1) | copy-start | bytes 493060
  64.7 0.9 copy-start.9
  65.6 19.4 %slice-start = ((s8[6553600]{0:T(1024)(128)(4,1)}), s8[4194304]{0:T(1024)(128)(4,1)S(1)}, s32[]{:S(2)}) async-start(s8[6553600]{0:T(1024)(128)(4,1)} %bitcast.14), calls=%async_computation.2 | async-start | bytes 8388608
  67.8 17.2 %slice-start.1 = ((s8[6553600]{0:T(1024)(128)(4,1)}), s8[2359296]{0:T(1024)(128)(4,1)S(1)}, s32[]{:S(2)}) async-start(s8[6553600]{0:T(1024)(128)(4,1)} %bitcast.14), calls=%async_computation.3 | async-start | bytes 4718592

commit v3 on v2

v3 whole, which is shorter than its diff:
```python
import functools
import math

import jax
import jax.numpy as jnp
from jax import lax
from jax.experimental import pallas as pl
from jax.experimental.pallas import tpu as pltpu
from jax.sharding import PartitionSpec as P

F32, BF16, I32 = jnp.float32, jnp.bfloat16, jnp.int32
GROUP = 8


def iota(shape, dim):
    return lax.broadcasted_iota(I32, shape, dim)


def matmul(a, b, ca, cb):
    return lax.dot_general(a, b, (((ca,), (cb,)), ((), ())), preferred_element_type=F32)


def one_hot(rows, cols):
    return jnp.where(rows == cols, 1.0, 0.0).astype(BF16)


def limits(band_ref, wave_ref, at, slots, comps, degrees):
    rows = GROUP * comps
    slot = iota((rows, 1), 0) // comps
    first = band_ref[0] * slots + at * GROUP
    limit = jnp.zeros((rows, 1), I32)
    for s in range(GROUP):
        limit = jnp.where(slot == s, degrees - wave_ref[first + s], limit)
    return limit


def synthesis_kernel(band_ref, wave_ref, weight_ref, adj_ref, leg_ref, out_ref, acc_ref):
    step = pl.program_id(0)
    levels, groups_slots, comps, degrees = adj_ref.shape
    rows = GROUP * comps
    heights = leg_ref.shape[1]
    weight = jnp.concatenate([weight_ref[...]] * (128 // heights), axis=1)
    for part in range(groups_slots // GROUP):
        here = pl.ds(part * GROUP, GROUP)
        at = step * (groups_slots // GROUP) + part
        limit = limits(band_ref, wave_ref, at, acc_ref.shape[1] // comps, comps, degrees)
        degree = iota((rows, degrees), 1)
        inside = degree < limit
        even = jnp.where(inside & (degree % 2 == 0), 1.0, 0.0).astype(BF16)
        odd = jnp.where(inside & (degree % 2 == 1), 1.0, 0.0).astype(BF16)
        values = [adj_ref[l, here].reshape(rows, degrees) for l in range(levels)]
        left = jnp.concatenate([v * even for v in values] + [v * odd for v in values], axis=0)
        table = leg_ref[here].reshape(GROUP * heights, degrees)
        both = matmul(left, table, 1, 1)
        shape = both.shape
        own = (iota(shape, 0) % rows) // comps == iota(shape, 1) // heights
        both = jnp.where(own, both, 0.0)
        both = both[:, :128] + both[:, 128:]
        both = both + pltpu.roll(both, 64, 1)
        both = both + pltpu.roll(both, 32, 1)
        half = levels * rows
        from_even, from_odd = both[:half], both[half:]
        north = (from_even + from_odd) * weight
        south = (from_even - from_odd) * weight
        for l in range(levels):
            acc_ref[l, pl.ds(at * rows, rows), :] = north[l * rows : (l + 1) * rows]
            acc_ref[levels + l, pl.ds(at * rows, rows), :] = south[l * rows : (l + 1) * rows]

    @pl.when(step == pl.num_programs(0) - 1)
    def _():
        total = acc_ref.shape[1]
        slots = total // comps
        sides = 2 * levels
        lane = iota((total, 128), 1) // heights
        blocks = []
        for k in range(sides // 4):
            mix = acc_ref[4 * k]
            for r in range(1, 4):
                mix = jnp.where(lane == r, acc_ref[4 * k + r], mix)
            blocks.append(mix.astype(BF16))
        wide = jnp.concatenate(blocks, axis=1)
        col = iota((total, 2 * 128), 1)
        source = iota((total, 2 * 128), 0)
        comp, slot = col // 128, col % 128
        spread = jnp.where((source == slot * comps + comp) & (slot < slots), 1.0, 0.0).astype(BF16)
        turned = matmul(wide, spread, 0, 0).astype(BF16)
        size = sides * heights
        dest = iota((size, size), 0)
        origin = iota((size, size), 1)
        band, e, hh, l = dest // 16, dest // 8 % 2, dest // 4 % 2, dest % 4
        wanted = (e * levels + l) * heights + band * 2 + hh
        moved = matmul(one_hot(wanted, origin), turned, 1, 0).astype(BF16)
        for d in range(size // 16):
            for c in range(comps):
                out_ref[d, c] = moved[16 * d : 16 * d + 16, 128 * c : 128 * c + slots]


def synthesis(adj, leg, band, waves, weight):
    levels, slots, comps, degrees = adj.shape
    heights = leg.shape[1]
    wide = 16
    steps = slots // wide
    return pl.pallas_call(
        synthesis_kernel,
        grid=(steps,),
        in_specs=[
            pl.BlockSpec(memory_space=pltpu.SMEM),
            pl.BlockSpec(memory_space=pltpu.SMEM),
            pl.BlockSpec((1, heights), lambda i: (0, 0)),
            pl.BlockSpec((levels, wide, comps, degrees), lambda i: (0, i, 0, 0)),
            pl.BlockSpec((wide, heights, degrees), lambda i: (i, 0, 0)),
        ],
        out_specs=pl.BlockSpec((16, comps, 16, slots), lambda i: (0, 0, 0, 0)),
        out_shape=jax.ShapeDtypeStruct((16, comps, 16, slots), BF16),
        scratch_shapes=[pltpu.VMEM((2 * levels, slots * comps, 128), F32)],
        compiler_params=pltpu.CompilerParams(vmem_limit_bytes=60 * 2**20),
        name="synthesis",
    )(band, waves, weight[None, :], adj, leg)


def analysis_kernel(band_ref, wave_ref, in_ref, leg_ref, out_ref, left_ref):
    step = pl.program_id(0)
    levels, wide, comps, degrees = out_ref.shape
    heights = leg_ref.shape[1]
    sources, _, sub, slots = in_ref.shape
    rows = GROUP * comps
    kinds = 2 * levels

    @pl.when(step == 0)
    def _():
        size = sources * sub
        row = iota((size, kinds * 128), 0)
        col = iota((size, kinds * 128), 1)
        row_key = (row // 8 % 2 * levels + row % 4) * heights + row // 16 * 2 + row // 4 % 2
        pick = one_hot(row_key, col // 128 * heights + col % heights)
        parts = []
        for c in range(comps):
            flat = jnp.concatenate([in_ref[d, c] for d in range(sources)], axis=0)
            parts.append(matmul(flat, pick, 0, 0).astype(BF16))
        apart = jnp.concatenate(parts, axis=0)
        total = slots * comps
        row = iota((total, total), 0)
        col = iota((total, total), 1)
        weave = one_hot(row % comps * slots + row // comps, col)
        left_ref[...] = matmul(weave, apart, 1, 0).astype(BF16)

    for part in range(wide // GROUP):
        at = step * (wide // GROUP) + part
        here = left_ref[pl.ds(pl.multiple_of(at * rows, rows), rows), :]
        stack = jnp.concatenate([here[:, 128 * k : 128 * k + 128] for k in range(kinds)], axis=0)
        left = jnp.concatenate([stack, stack], axis=1)
        shape = left.shape
        own = (iota(shape, 0) % rows) // comps == iota(shape, 1) // heights
        left = left * jnp.where(own, 1.0, 0.0).astype(BF16)
        table = leg_ref[pl.ds(part * GROUP, GROUP)].reshape(GROUP * heights, degrees)
        both = matmul(left, table, 1, 0)
        limit = limits(band_ref, wave_ref, at, slots, comps, degrees)
        degree = iota((rows, degrees), 1)
        inside = degree < limit
        even = degree % 2 == 0
        half = levels * rows
        for l in range(levels):
            sym = both[l * rows : (l + 1) * rows]
            anti = both[half + l * rows : half + (l + 1) * rows]
            value = jnp.where(inside, jnp.where(even, sym, anti), 0.0).astype(BF16)
            out_ref[l, pl.ds(part * GROUP, GROUP)] = value.reshape(GROUP, comps, degrees)


def analysis(sides, leg, band, waves, levels):
    sources, comps, sub, slots = sides.shape
    heights, degrees = leg.shape[1:]
    wide = 16
    return pl.pallas_call(
        analysis_kernel,
        grid=(slots // wide,),
        in_specs=[
            pl.BlockSpec(memory_space=pltpu.SMEM),
            pl.BlockSpec(memory_space=pltpu.SMEM),
            pl.BlockSpec(sides.shape, lambda i: (0, 0, 0, 0)),
            pl.BlockSpec((wide, heights, degrees), lambda i: (i, 0, 0)),
        ],
        out_specs=pl.BlockSpec((levels, wide, comps, degrees), lambda i: (0, i, 0, 0)),
        out_shape=jax.ShapeDtypeStruct((levels, slots, comps, degrees), BF16),
        scratch_shapes=[pltpu.VMEM((slots * comps, 2 * levels * 128), BF16)],
        compiler_params=pltpu.CompilerParams(vmem_limit_bytes=60 * 2**20),
        name="analysis",
    )(band, waves, sides, leg)

NBLK = 4
LOW = 16


def turns(wave, b):
    turn = (wave * b) & 3
    cos_b = jnp.where(turn == 0, 1.0, jnp.where(turn == 2, -1.0, 0.0))
    sin_b = jnp.where(turn == 1, 1.0, jnp.where(turn == 3, -1.0, 0.0))
    return cos_b, sin_b


def circle(product, lon_count):
    quarter = lon_count // 4
    count = jnp.floor(product * (1.0 / quarter) + 0.5)
    angle = (product - count * quarter) * (2.0 * math.pi / lon_count)
    turn = count.astype(I32) & 3
    square = angle * angle
    cos = 1.0 + square * (-1 / 2 + square * (1 / 24 + square * (-1 / 720 + square * (1 / 40320))))
    sin = angle * (
        1.0 + square * (-1 / 6 + square * (1 / 120 + square * (-1 / 5040 + square * (1 / 362880))))
    )
    swap = (turn & 1) == 1
    near, far = jnp.where(swap, sin, cos), jnp.where(swap, cos, sin)
    near = jnp.where((turn == 1) | (turn == 2), -near, near)
    far = jnp.where(turn >= 2, -far, far)
    return near, far


def prepare_kernel(
    order_ref, wave_ref, exp_ref, traj_ref, cos_ref, sin_ref, gain_ref, cos_high_ref, sin_high_ref, *, norm
):
    levels, lats, lons = traj_ref.shape
    width = lons // NBLK
    wave = wave_ref[...].astype(F32)
    shape = (LOW, wave.shape[1])
    cos_low, sin_low = circle(iota(shape, 0).astype(F32) * wave, lons)
    shape = cos_high_ref.shape
    cos_high_ref[...], sin_high_ref[...] = circle((iota(shape, 0) * LOW).astype(F32) * wave, lons)

    @pl.loop(0, cos_ref.shape[0] // LOW)
    def _(i):
        cos_high = cos_high_ref[pl.ds(i, 1), :]
        sin_high = sin_high_ref[pl.ds(i, 1), :]
        at = pl.ds(pl.multiple_of(i * LOW, LOW), LOW)
        cos_ref[at, :] = (cos_high * cos_low - sin_high * sin_low).astype(BF16)
        sin_ref[at, :] = (-(sin_high * cos_low + cos_high * sin_low)).astype(BF16)

    sub = levels * lats
    row, col = iota((sub, sub), 0), iota((sub, sub), 1)
    held = jnp.zeros((sub, sub), I32)
    for r in range(levels):
        held = jnp.where(col // lats == r, order_ref[0, r], held)
    lat = row // 4 % 2 * 2 + row // 8
    pick = jnp.where((held == row % 4) & (col % lats == lat), 1.0, 0.0).astype(BF16)
    power = jnp.concatenate([exp_ref[r] for r in range(levels)], axis=0).astype(F32)
    scale = matmul(pick, jnp.exp2(power).astype(BF16), 1, 0)
    stored = jnp.concatenate([traj_ref[r] for r in range(levels)], axis=0)
    ordered = matmul(pick, stored, 1, 0)
    full = cos_ref.shape[0]
    ahead = iota((sub, full), 1)
    reverse = jnp.where(iota((full, full), 0) + iota((full, full), 1) == full, 1.0, 0.0).astype(BF16)
    for b in range(NBLK):
        start = b * width
        piece = ordered[:, start : start + full] * scale[:, b : b + 1]
        gain = jnp.where(ahead <= width // 2, norm * (1.0 + jnp.tanh(piece)), 0.0)
        gain_ref[b * sub : (b + 1) * sub, :] = gain
        back = ordered[:, start + width - full : start + width].astype(BF16)
        piece = matmul(back, reverse, 1, 0) * scale[:, b : b + 1]
        gain = norm * (1.0 + jnp.tanh(piece))
        gain = jnp.where((ahead >= 1) & (2 * ahead < width), gain, 0.0)
        at = (NBLK + (b + 1) % NBLK) * sub
        gain_ref[at : at + sub, :] = gain


def prepare(order, wave, exps, traj, norm):
    levels, lats, lons = traj.shape
    waves = wave.shape[1]
    high = -(-(lons // NBLK // 2 + 1) // LOW)
    table = jax.ShapeDtypeStruct((high * LOW, waves), BF16)
    vmem = pl.BlockSpec(memory_space=pltpu.VMEM)
    return pl.pallas_call(
        functools.partial(prepare_kernel, norm=norm),
        in_specs=[pl.BlockSpec(memory_space=pltpu.SMEM)] + [vmem] * 3,
        out_specs=[vmem] * 3,
        out_shape=(table, table, jax.ShapeDtypeStruct((2 * NBLK * levels * lats, high * LOW), F32)),
        scratch_shapes=[pltpu.VMEM((-(-high // 8) * 8, waves), F32)] * 2,
        compiler_params=pltpu.CompilerParams(vmem_limit_bytes=16 * 2**20),
        cost_estimate=pl.CostEstimate(flops=12_000_000, bytes_accessed=20_000_000, transcendentals=0),
        name="prepare",
    )(order, wave, exps, traj)


def gather_kernel(in_ref, out_ref, total_ref):
    sources, comps, sub, slots = in_ref.shape
    pick = one_hot(iota((8, comps * sub), 1) // 4, iota((8, comps * sub), 0))
    flat = [jnp.concatenate([in_ref[d, c] for d in range(sources)], axis=1) for c in range(comps)]
    flat = jnp.concatenate(flat, axis=0)
    out_ref[...] = flat
    total_ref[...] = matmul(pick, flat, 1, 0).astype(BF16)


def gather_rows(blocks):
    sources, comps, sub, slots = blocks.shape
    return pl.pallas_call(
        gather_kernel,
        out_shape=(
            jax.ShapeDtypeStruct((comps * sub, sources * slots), BF16),
            jax.ShapeDtypeStruct((comps * sub // 4, sources * slots), BF16),
        ),
        compiler_params=pltpu.CompilerParams(vmem_limit_bytes=8 * 2**20),
        name="gather_rows",
    )(blocks)


def forcing_kernel(index_ref, coef_ref, total_ref, four_ref, wave_ref, gain_ref, cos_ref, sin_ref, out_ref, held_ref, held_sem, *, norm):
    fetch = pltpu.make_async_copy(gain_ref, held_ref, held_sem)
    fetch.start()
    me = index_ref[0]
    groups, rows, waves = total_ref.shape
    both = four_ref.shape[0]
    sub = both // 2
    wave = wave_ref[...]
    carry = jnp.zeros((rows, waves), F32)
    for g in range(groups):
        carry = carry + jnp.where(g < me, total_ref[g].astype(F32), 0.0)
    four = four_ref[...]
    row, col = iota((both, both), 0), iota((both, both), 1)
    earlier = jnp.where((row // 4 == col // 4) & (col < row), 1.0, 0.0).astype(BF16)
    copies = one_hot(iota((both, rows), 0) // 4, iota((both, rows), 1))
    above = matmul(earlier, four, 1, 0) + matmul(copies, carry.astype(BF16), 1, 0)
    level = iota((both, 1), 0) % 4
    coef = jnp.zeros((both, 1), F32)
    for l in range(4):
        coef = jnp.where(level == l, coef_ref[l], coef)
    mixed = (four.astype(F32) + coef * above).astype(BF16)
    first, second = mixed[:sub], mixed[sub:]
    with_cos, with_sin = [], []
    for b in range(NBLK):
        cos_b, sin_b = (v.astype(BF16) for v in turns(wave, b))
        with_cos.append(first * cos_b - second * sin_b)
        with_sin.append(first * sin_b + second * cos_b)
    with_cos = jnp.concatenate(with_cos, axis=0)
    with_sin = jnp.concatenate(with_sin, axis=0)
    even = matmul(with_cos, cos_ref[...], 1, 1)
    odd = matmul(with_sin, sin_ref[...], 1, 1)
    half = NBLK * sub
    fetch.wait()
    ahead = held_ref[:half, :] * (even + odd)
    behind = held_ref[half:, :] * (even - odd)
    forcing = jnp.concatenate([ahead, behind], axis=0).astype(BF16)
    by_cos = matmul(forcing, cos_ref[...], 1, 0)
    by_sin = matmul(forcing, sin_ref[...], 1, 0)
    by_cos = by_cos[:half] + by_cos[half:]
    by_sin = by_sin[:half] - by_sin[half:]
    first = jnp.zeros((sub, waves), F32)
    second = jnp.zeros((sub, waves), F32)
    for b in range(NBLK):
        cos_b, sin_b = turns(wave, b)
        part_cos, part_sin = by_cos[b * sub : (b + 1) * sub], by_sin[b * sub : (b + 1) * sub]
        first = first + part_cos * cos_b + part_sin * sin_b
        second = second + part_sin * cos_b - part_cos * sin_b
    bands, comps, _, slots = out_ref.shape
    half = sub // 2
    for c, value in enumerate((first, second)):
        value = value * norm
        sym, anti = value[:half] + value[half:], value[:half] - value[half:]
        sides = jnp.concatenate([sym, anti], axis=0).astype(BF16)
        for d in range(bands):
            out_ref[d, c] = sides[:, slots * d : slots * (d + 1)]


def forcing_part(index, coef, totals, four, wave, gain, cos_t, sin_t, shape, norm):
    vmem = pl.BlockSpec(memory_space=pltpu.VMEM)
    smem = pl.BlockSpec(memory_space=pltpu.SMEM)
    return pl.pallas_call(
        functools.partial(forcing_kernel, norm=norm),
        in_specs=[smem] * 2 + [vmem] * 3 + [pl.BlockSpec(memory_space=pltpu.HBM)] + [vmem] * 2,
        out_specs=vmem,
        scratch_shapes=[pltpu.VMEM(gain.shape, F32), pltpu.SemaphoreType.DMA],
        out_shape=jax.ShapeDtypeStruct(shape, BF16),
        compiler_params=pltpu.CompilerParams(vmem_limit_bytes=16 * 2**20),
        cost_estimate=pl.CostEstimate(flops=900_000_000, bytes_accessed=8_000_000, transcendentals=0),
        name="forcing_part",
    )(index, coef, totals, four, wave, gain, cos_t, sin_t)


def body(adj_spec, wave_of_slot, legendre, lat_weight, traj, traj_exp, traj_order, lev_coef):
    levels, degrees = adj_spec.shape[0], adj_spec.shape[3]
    norm = 1.0 / math.sqrt(degrees)
    band = lax.axis_index("band").astype(I32)[None]
    index = lax.axis_index("lev").astype(I32)[None]
    wave = wave_of_slot[None, :]
    blocks = synthesis(adj_spec, legendre, band, wave_of_slot, lat_weight)
    blocks = lax.all_to_all(blocks, "band", split_axis=0, concat_axis=0, tiled=True)
    cos_t, sin_t, gain = prepare(traj_order, wave, traj_exp, traj, norm)
    four, total = gather_rows(blocks)
    totals = lax.all_gather(total, "lev")
    sides = forcing_part(
        index, lev_coef, totals, four, wave, gain, cos_t, sin_t, blocks.shape, norm
    )
    sides = lax.all_to_all(sides, "band", split_axis=0, concat_axis=0, tiled=True)
    return analysis(sides, legendre, band, wave_of_slot, levels)


def solution(mesh):
    return jax.shard_map(
        body,
        mesh=mesh,
        in_specs=(
            P("lev", "band", None, None),
            P(),
            P("band", None, None),
            P(),
            P("lev", "band", None),
            P("lev", "band", None),
            P("lev", None),
            P("lev"),
        ),
        out_specs=P("lev", "band", None, None),
        check_vma=False,
    )
```

time: 89.4 us -> 66.5 us (0.74)
  local copies, waits for them, and re-layouts: 16 us -> 2.68 us
  other arithmetic: 10.4 us -> 0 us
  blocking collectives: 35.4 us -> 33.2 us
  waiting for transfers between devices: 0.01 us -> 2.17 us
  Pallas kernels: 19.3 us -> 20.4 us
    unnamed x30 -> x14, local copies, waits for them, and re-layouts: 12.7 us -> 2.67 us
    sin x2 -> x0, other arithmetic: 3.72 us -> none  [angles(): return (jnp.cos(angle), jnp.sin(angle))]
    all_to_all x1, blocking collectives: 13.5 us -> 10.4 us  [body(): lax.all_to_all(sides, 'band', split_axis=0, concat_axis=0, tiled=True)]
    pallas_call x1, Pallas kernels: 3.84 us -> 6.79 us  [analysis(): pl.pallas_call(analysis_kernel, grid=(slots // wide,), in_specs=[pl.Block...]
    concatenate x1 -> x0, other arithmetic: 2.68 us -> none  [body(): scale = jnp.exp2(traj_exp[stored_row, lat, blk].astype(F32))[:, None]]
    gather x1 -> x0, other arithmetic: 2.5 us -> none  [body(): coef = lev_coef[level][:, None]]
    gather x3 -> x0, local copies, waits for them, and re-layouts: 2.29 us -> none  [the longest x1 0.96 us: body(): scale = jnp.exp2(traj_exp[stored_row, lat, blk].astype(F32))[:, None]]
    all_to_all x1, waiting for transfers between devices: 0.01 us -> 2.17 us  [body(): lax.all_to_all(blocks, 'band', split_axis=0, concat_axis=0, tiled=True)]
  transfers between devices with their start and end apart: 1 -> 1, of which waited for: 0 -> 1; matrix products, arithmetic and copies ran while one was open for 14% -> 0% of each run, Pallas kernels for 3% -> 4%
where the time goes in v3:
time: 66.5 us; the launch traced here: 66.1 us
  blocking collectives  33.2 us (50%)
  Pallas kernels  20.4 us (31%)
  starting transfers between devices  7.58 us (11%)
  local copies, waits for them, and re-layouts  2.68 us (4%)
  waiting for transfers between devices  2.17 us (3%)
    all_gather x1, blocking collectives, body(): totals = lax.all_gather(total, 'lev')  22.8 us
    all_to_all x1, blocking collectives, body(): lax.all_to_all(sides, 'band', split_axis=0, concat_axis=0, tiled=True)  10.4 us
    pallas_call x1, Pallas kernels, synthesis(): pl.pallas_call(synthesis_kernel, grid=(steps,), in_specs=[pl.BlockSpec(me...  7.63 us
    all_to_all x1, starting transfers between devices, body(): lax.all_to_all(blocks, 'band', split_axis=0, concat_axis=0, tiled=True)  7.58 us
    pallas_call x1, Pallas kernels, analysis(): pl.pallas_call(analysis_kernel, grid=(slots // wide,), in_specs=[pl.Block...  6.79 us
    pallas_call x1, Pallas kernels, prepare(): pl.pallas_call(functools.partial(prepare_kernel, norm=norm), in_specs=[pl...  2.97 us
    pallas_call x1, Pallas kernels, forcing_part(): pl.pallas_call(functools.partial(forcing_kernel, norm=norm), in_specs=[sm...  2.81 us
    unnamed x14, local copies, waits for them, and re-layouts  2.67 us
  transfers between devices with their start and end apart: 1, of which 1 were waited for; matrix products, arithmetic and copies ran while one was open for 0% of the time, Pallas kernels for 4%

profile of v3, /device:TPU:1, one launch (start us, length us, event | category | flops | bytes accessed | tf_op | source)
XLA Modules:
  0.0 66.1 jit_solution(3042549508888897563)
XLA Ops:
  0.0 0.0 copy-start.6
  0.0 0.0 copy-start.3
  0.0 0.0 copy-start.4
  0.0 0.0 copy-start.5
  0.0 7.6 %synthesis.1 = bf16[16,2,16,80]{3,2,1,0:T(8,128)(2,1)} custom-call(s32[1]{0:T(128)} %bitcast.band_ref, s32[1280]{0:T(1024)} %wave_ref.3, f32[1,32]{1,0:T(1,128)} %bitcast.5, bf16[4,80,2,1280]{3,2,1,0:T(2,128)(2,1)} %adj_ref.1, bf16[80,32,1280]{2,1,0:T(8,128)(2,1)} %leg_ref.3), custom_call_target="tpu_custom_call" | custom-call | tf_op jit(solution)/shard_map/synthesis/pallas_call | solution.py:103
  7.6 7.6 %all-to-all-start = ((bf16[16,2,16,80]{3,2,1,0:T(8,128)(2,1)}), bf16[16,2,16,80]{3,2,1,0:T(8,128)(2,1)S(1)}, u32[]{:S(2)}, u32[]{:S(2)}) async-start(bf16[16,2,16,80]{3,2,1,0:T(8,128)(2,1)} %synthesis.1), calls=%async_computation | async-start | bytes 262144 | tf_op jit(solution)/shard_map/all_to_all | solution.py:382
  15.2 0.0 copy-done.6
  15.3 0.0 copy-done.3
  15.3 0.0 copy-done.4
  15.3 0.0 copy-start.2
  15.3 0.9 %copy-done.2 = bf16[4,4,5136]{2,1,0:T(4,128)(2,1)S(1)} copy-done((bf16[4,4,5136]{2,1,0:T(4,128)(2,1)S(1)}, bf16[4,4,5136]{2,1,0:T(4,128)(2,1)}, u32[]{:S(2)}) %copy-start.2) | copy-done | bytes 164376
  16.2 3.0 %prepare.1 = (bf16[656,1280]{1,0:T(8,128)(2,1)S(1)}, bf16[656,1280]{1,0:T(8,128)(2,1)S(1)}, f32[128,656]{1,0:T(8,128)S(1)}) custom-call(s32[1,4]{1,0:T(1,128)S(1)} %copy-done.4, s32[1,1280]{1,0:T(1,128)S(1)} %broadcast_in_dim.15.wave_ref, s32[4,4,4]{2,1,0:T(4,128)S(1)} %copy-done.3, bf16[4,4,5136]{2,1,0:T(4,128)(2,1)S(1)} %copy-done.2), custom_call_target="tpu_custom_call" | custom-call | flops 12000000 | bytes 20000000 | tf_op jit(solution)/shard_map/prepare/pallas_call | solution.py:269
  19.2 0.0 copy-start
  19.2 0.7 %copy-done = f32[128,656]{1,0:T(8,128)} copy-done((f32[128,656]{1,0:T(8,128)}, f32[128,656]{1,0:T(8,128)S(1)}, u32[]{:S(2)}) %copy-start) | copy-done | bytes 335896
  19.9 2.2 %all-to-all-done.in_ref = bf16[16,2,16,80]{3,2,1,0:T(8,128)(2,1)S(1)} async-done(((bf16[16,2,16,80]{3,2,1,0:T(8,128)(2,1)}), bf16[16,2,16,80]{3,2,1,0:T(8,128)(2,1)S(1)}, u32[]{:S(2)}, u32[]{:S(2)}) %all-to-all-start) | async-done | bytes 81952 | tf_op jit(solution)/shard_map/all_to_all | solution.py:382
  22.1 0.2 gather_rows.1
  22.3 22.8 %all-gather = bf16[128,1280]{1,0:T(8,128)(2,1)S(1)} all-gather(bf16[8,1280]{1,0:T(8,128)(2,1)S(1)} %get-tuple-element.10), channel_id=2, replica_groups=mesh['band'=16,'lev'=16] {'lev'}, dimensions={0}, use_global_device_ids=true | all-gather | bytes 348160 | tf_op jit(solution)/shard_map/all_gather | solution.py:385
  45.1 0.0 copy-done.5
  45.1 0.0 copy-start.1
  45.1 1.0 %copy-done.1 = f32[128,656]{1,0:T(8,128)S(1)} copy-done((f32[128,656]{1,0:T(8,128)S(1)}, f32[128,656]{1,0:T(8,128)}, u32[]{:S(2)}) %copy-start.1) | copy-done | bytes 335896
  46.1 2.8 %forcing_part.1 = bf16[16,2,16,80]{3,2,1,0:T(8,128)(2,1)S(1)} custom-call(s32[1]{0:T(128)} %bitcast.1.index_ref, f32[4]{0:T(128)S(1)} %copy-done.5, bf16[16,8,1280]{2,1,0:T(8,128)(2,1)S(1)} %bitcast.4, bf16[32,1280]{1,0:T(8,128)(2,1)S(1)} %get-tuple-element.11.four_ref, s32[1,1280]{1,0:T(1,128)S(1)} %broadcast_in_dim.15.wave_ref, f32[128,656]{1,0:T(8,128)S(1)} %copy-done.1, ...), custom_call_target="tpu_custom_call" | custom-call | flops 900000000 | bytes 8000000 | tf_op jit(solution)/shard_map/forcing_part/pallas_call | solution.py:363
  48.9 10.4 %all_to_all.10.in_ref = bf16[16,2,16,80]{3,2,1,0:T(8,128)(2,1)} all-to-all(bf16[16,2,16,80]{3,2,1,0:T(8,128)(2,1)S(1)} %forcing_part.1), channel_id=1, replica_groups=mesh['band'=16,'lev'=16] {'band'}, dimensions={0} | all-to-all | bytes 163840 | tf_op jit(solution)/shard_map/all_to_all | solution.py:389
  59.3 6.8 %analysis.1 = bf16[4,80,2,1280]{3,2,1,0:T(2,128)(2,1)} custom-call(s32[1]{0:T(128)} %bitcast.band_ref, s32[1280]{0:T(1024)} %wave_ref.3, bf16[16,2,16,80]{3,2,1,0:T(8,128)(2,1)} %all_to_all.10.in_ref, bf16[80,32,1280]{2,1,0:T(8,128)(2,1)} %leg_ref.3), custom_call_target="tpu_custom_call" | custom-call | tf_op jit(solution)/shard_map/analysis/pallas_call | solution.py:173
  (1 shorter events, 0.0 us)
Async XLA Ops:
  0.0 15.2 %copy-start.6 = (s32[1280]{0:T(1024)S(1)}, s32[1280]{0:T(1024)}, u32[]{:S(2)}) copy-start(s32[1280]{0:T(1024)} %wave_ref.3) | copy-start | bytes 15364
  0.0 15.3 %copy-start.3 = (s32[4,4,4]{2,1,0:T(4,128)S(1)}, s32[4,4,4]{2,1,0:T(4,128)}, u32[]{:S(2)}) copy-start(s32[4,4,4]{2,1,0:T(4,128)} %exp_ref.1) | copy-start | bytes 772
  0.0 15.3 %copy-start.4 = (s32[1,4]{1,0:T(1,128)S(1)}, s32[1,4]{1,0:T(1,128)}, u32[]{:S(2)}) copy-start(s32[1,4]{1,0:T(1,128)} %order_ref.1) | copy-start | bytes 52
  0.0 45.1 %copy-start.5 = (f32[4]{0:T(128)S(1)}, f32[4]{0:T(128)}, u32[]{:S(2)}) copy-start(f32[4]{0:T(128)} %coef_ref.1) | copy-start | bytes 52
  7.6 14.5 %all-to-all-start = ((bf16[16,2,16,80]{3,2,1,0:T(8,128)(2,1)}), bf16[16,2,16,80]{3,2,1,0:T(8,128)(2,1)S(1)}, u32[]{:S(2)}, u32[]{:S(2)}) async-start(bf16[16,2,16,80]{3,2,1,0:T(8,128)(2,1)} %synthesis.1), calls=%async_computation | async-start | bytes 262144 | tf_op jit(solution)/shard_map/all_to_all | solution.py:382
  15.3 0.9 %copy-start.2 = (bf16[4,4,5136]{2,1,0:T(4,128)(2,1)S(1)}, bf16[4,4,5136]{2,1,0:T(4,128)(2,1)}, u32[]{:S(2)}) copy-start(bf16[4,4,5136]{2,1,0:T(4,128)(2,1)} %traj_ref.1) | copy-start | bytes 493060
  19.2 0.8 %copy-start = (f32[128,656]{1,0:T(8,128)}, f32[128,656]{1,0:T(8,128)S(1)}, u32[]{:S(2)}) copy-start(f32[128,656]{1,0:T(8,128)S(1)} %get-tuple-element.12.gain_ref) | copy-start | bytes 1007620
  45.1 1.0 %copy-start.1 = (f32[128,656]{1,0:T(8,128)S(1)}, f32[128,656]{1,0:T(8,128)}, u32[]{:S(2)}) copy-start(f32[128,656]{1,0:T(8,128)} %copy-done) | copy-start | bytes 1007620

commit v4 on v3

v4 whole, which is shorter than its diff:
```python
import functools
import math

import jax
import jax.numpy as jnp
from jax import lax
from jax.experimental import pallas as pl
from jax.experimental.pallas import tpu as pltpu
from jax.sharding import Mesh
from jax.sharding import PartitionSpec as P

F32, BF16, I32 = jnp.float32, jnp.bfloat16, jnp.int32
GROUP = 8


def iota(shape, dim):
    return lax.broadcasted_iota(I32, shape, dim)


def matmul(a, b, ca, cb):
    return lax.dot_general(a, b, (((ca,), (cb,)), ((), ())), preferred_element_type=F32)


def one_hot(rows, cols):
    return jnp.where(rows == cols, 1.0, 0.0).astype(BF16)


def limits(band_ref, wave_ref, at, slots, comps, degrees):
    rows = GROUP * comps
    slot = iota((rows, 1), 0) // comps
    first = band_ref[0] * slots + at * GROUP
    limit = jnp.zeros((rows, 1), I32)
    for s in range(GROUP):
        limit = jnp.where(slot == s, degrees - wave_ref[first + s], limit)
    return limit


def synthesis_kernel(
    band_ref, wave_ref, weight_ref, adj_hbm, leg_hbm, out_ref, adj_ref, leg_ref, acc_ref, adj_sem, leg_sem
):
    levels, slots, comps, degrees = adj_ref.shape
    rows = GROUP * comps
    heights = leg_ref.shape[1]
    steps = slots // GROUP
    fetches = []
    for g in range(steps):
        here = pl.ds(g * GROUP, GROUP)
        fetches.append((
            pltpu.make_async_copy(adj_hbm.at[:, here], adj_ref.at[:, here], adj_sem.at[g]),
            pltpu.make_async_copy(leg_hbm.at[here], leg_ref.at[here], leg_sem.at[g]),
        ))
        for fetch in fetches[-1]:
            fetch.start()
    weight = jnp.concatenate([weight_ref[...]] * (128 // heights), axis=1)
    half = levels * rows
    for g in range(steps):
        for fetch in fetches[g]:
            fetch.wait()
        here = pl.ds(g * GROUP, GROUP)
        limit = limits(band_ref, wave_ref, g, slots, comps, degrees)
        degree = iota((rows, degrees), 1)
        inside = degree < limit
        even = jnp.where(inside & (degree % 2 == 0), 1.0, 0.0).astype(BF16)
        odd = jnp.where(inside & (degree % 2 == 1), 1.0, 0.0).astype(BF16)
        values = [adj_ref[l, here].reshape(rows, degrees) for l in range(levels)]
        left = jnp.concatenate([v * even for v in values] + [v * odd for v in values], axis=0)
        table = leg_ref[here].reshape(GROUP * heights, degrees)
        both = matmul(left, table, 1, 1)
        shape = both.shape
        own = (iota(shape, 0) % rows) // comps == iota(shape, 1) // heights
        both = jnp.where(own, both, 0.0)
        both = both[:, :128] + both[:, 128:]
        both = both + pltpu.roll(both, 64, 1)
        both = both + pltpu.roll(both, 32, 1)
        from_even, from_odd = both[:half], both[half:]
        north = (from_even + from_odd) * weight
        south = (from_even - from_odd) * weight
        for l in range(levels):
            acc_ref[l, g * rows : (g + 1) * rows, :] = north[l * rows : (l + 1) * rows]
            acc_ref[levels + l, g * rows : (g + 1) * rows, :] = south[l * rows : (l + 1) * rows]
    total = acc_ref.shape[1]
    sides = 2 * levels
    lane = iota((total, 128), 1) // heights
    blocks = []
    for k in range(sides // 4):
        mix = acc_ref[4 * k]
        for r in range(1, 4):
            mix = jnp.where(lane == r, acc_ref[4 * k + r], mix)
        blocks.append(mix.astype(BF16))
    wide = jnp.concatenate(blocks, axis=1)
    col = iota((total, 2 * 128), 1)
    source = iota((total, 2 * 128), 0)
    comp, slot = col // 128, col % 128
    spread = jnp.where((source == slot * comps + comp) & (slot < slots), 1.0, 0.0).astype(BF16)
    turned = matmul(wide, spread, 0, 0).astype(BF16)
    size = sides * heights
    dest = iota((size, size), 0)
    origin = iota((size, size), 1)
    band, e, hh, l = dest // 16, dest // 8 % 2, dest // 4 % 2, dest % 4
    wanted = (e * levels + l) * heights + band * 2 + hh
    moved = matmul(one_hot(wanted, origin), turned, 1, 0).astype(BF16)
    for d in range(size // 16):
        for c in range(comps):
            tile = moved[16 * d : 16 * d + 16, 128 * c : 128 * c + slots]
            for core in range(2):
                out_ref[2 * d + core, c] = tile


def synthesis(adj, leg, band, waves, weight):
    levels, slots, comps, degrees = adj.shape
    heights = leg.shape[1]
    smem = pl.BlockSpec(memory_space=pltpu.SMEM)
    vmem = pl.BlockSpec(memory_space=pltpu.VMEM)
    hbm = pl.BlockSpec(memory_space=pltpu.HBM)
    return pl.pallas_call(
        synthesis_kernel,
        in_specs=[smem, smem, vmem, hbm, hbm],
        out_specs=vmem,
        out_shape=jax.ShapeDtypeStruct((32, comps, 16, slots), BF16),
        scratch_shapes=[
            pltpu.VMEM(adj.shape, BF16),
            pltpu.VMEM(leg.shape, BF16),
            pltpu.VMEM((2 * levels, slots * comps, 128), F32),
            pltpu.SemaphoreType.DMA((slots // GROUP,)),
            pltpu.SemaphoreType.DMA((slots // GROUP,)),
        ],
        compiler_params=pltpu.CompilerParams(vmem_limit_bytes=60 * 2**20),
        name="synthesis",
    )(band, waves, weight[None, :], adj, leg)


def analysis_kernel(band_ref, wave_ref, in_ref, leg_hbm, out_hbm, leg_ref, left_ref, out_ref, leg_sem, out_sem):
    slots, heights, degrees = leg_ref.shape
    levels, _, comps, _ = out_ref.shape
    sources, _, sub, _ = in_ref.shape
    rows = GROUP * comps
    kinds = 2 * levels
    steps = slots // GROUP
    fetches = []
    for g in range(steps):
        here = pl.ds(g * GROUP, GROUP)
        fetches.append(pltpu.make_async_copy(leg_hbm.at[here], leg_ref.at[here], leg_sem.at[g]))
        fetches[-1].start()
    size = sources * sub
    row = iota((size, kinds * 128), 0)
    col = iota((size, kinds * 128), 1)
    row_key = (row // 8 % 2 * levels + row % 4) * heights + row // 16 * 2 + row // 4 % 2
    pick = one_hot(row_key, col // 128 * heights + col % heights)
    parts = []
    for c in range(comps):
        flat = jnp.concatenate([in_ref[d, c] for d in range(sources)], axis=0)
        parts.append(matmul(flat, pick, 0, 0).astype(BF16))
    apart = jnp.concatenate(parts, axis=0)
    total = slots * comps
    weave = one_hot(
        iota((total, total), 0) % comps * slots + iota((total, total), 0) // comps,
        iota((total, total), 1),
    )
    left_ref[...] = matmul(weave, apart, 1, 0).astype(BF16)
    half = levels * rows
    sends = []
    for g in range(steps):
        here = pl.ds(g * GROUP, GROUP)
        own_rows = left_ref[g * rows : (g + 1) * rows, :]
        stack = jnp.concatenate([own_rows[:, 128 * k : 128 * k + 128] for k in range(kinds)], axis=0)
        left = jnp.concatenate([stack, stack], axis=1)
        shape = left.shape
        own = (iota(shape, 0) % rows) // comps == iota(shape, 1) // heights
        left = left * jnp.where(own, 1.0, 0.0).astype(BF16)
        fetches[g].wait()
        both = matmul(left, leg_ref[here].reshape(GROUP * heights, degrees), 1, 0)
        limit = limits(band_ref, wave_ref, g, slots, comps, degrees)
        degree = iota((rows, degrees), 1)
        inside = degree < limit
        even = degree % 2 == 0
        for l in range(levels):
            sym = both[l * rows : (l + 1) * rows]
            anti = both[half + l * rows : half + (l + 1) * rows]
            value = jnp.where(inside, jnp.where(even, sym, anti), 0.0).astype(BF16)
            out_ref[l, here] = value.reshape(GROUP, comps, degrees)
        sends.append(pltpu.make_async_copy(out_ref.at[:, here], out_hbm.at[:, here], out_sem.at[g]))
        sends[-1].start()
    for send in sends:
        send.wait()


def analysis(sides, leg, band, waves, levels):
    sources, comps, sub, slots = sides.shape
    heights, degrees = leg.shape[1:]
    smem = pl.BlockSpec(memory_space=pltpu.SMEM)
    vmem = pl.BlockSpec(memory_space=pltpu.VMEM)
    hbm = pl.BlockSpec(memory_space=pltpu.HBM)
    shape = (levels, slots, comps, degrees)
    return pl.pallas_call(
        analysis_kernel,
        in_specs=[smem, smem, vmem, hbm],
        out_specs=hbm,
        out_shape=jax.ShapeDtypeStruct(shape, BF16),
        scratch_shapes=[
            pltpu.VMEM(leg.shape, BF16),
            pltpu.VMEM((slots * comps, 2 * levels * 128), BF16),
            pltpu.VMEM(shape, BF16),
            pltpu.SemaphoreType.DMA((slots // GROUP,)),
            pltpu.SemaphoreType.DMA((slots // GROUP,)),
        ],
        compiler_params=pltpu.CompilerParams(vmem_limit_bytes=60 * 2**20),
        name="analysis",
    )(band, waves, sides, leg)

NBLK = 4
LOW = 16


def turns(wave, b):
    turn = (wave * b) & 3
    cos_b = jnp.where(turn == 0, 1.0, jnp.where(turn == 2, -1.0, 0.0))
    sin_b = jnp.where(turn == 1, 1.0, jnp.where(turn == 3, -1.0, 0.0))
    return cos_b, sin_b


def circle(product, lon_count):
    quarter = lon_count // 4
    count = jnp.floor(product * (1.0 / quarter) + 0.5)
    angle = (product - count * quarter) * (2.0 * math.pi / lon_count)
    turn = count.astype(I32) & 3
    square = angle * angle
    cos = 1.0 + square * (-1 / 2 + square * (1 / 24 + square * (-1 / 720 + square * (1 / 40320))))
    sin = angle * (
        1.0 + square * (-1 / 6 + square * (1 / 120 + square * (-1 / 5040 + square * (1 / 362880))))
    )
    swap = (turn & 1) == 1
    near, far = jnp.where(swap, sin, cos), jnp.where(swap, cos, sin)
    near = jnp.where((turn == 1) | (turn == 2), -near, near)
    far = jnp.where(turn >= 2, -far, far)
    return near, far


def prepare_kernel(
    order_ref, wave_ref, exp_ref, traj_ref, cos_ref, sin_ref, gain_hbm, token_ref,
    cos_high_ref, sin_high_ref, gain_ref, gain_sem, *, norm
):
    levels, lats, lons = traj_ref.shape
    width = lons // NBLK
    wave = wave_ref[...].astype(F32)
    shape = (LOW, wave.shape[1])
    cos_low, sin_low = circle(iota(shape, 0).astype(F32) * wave, lons)
    shape = cos_high_ref.shape
    cos_high_ref[...], sin_high_ref[...] = circle((iota(shape, 0) * LOW).astype(F32) * wave, lons)

    @pl.loop(0, cos_ref.shape[0] // LOW)
    def _(i):
        cos_high = cos_high_ref[pl.ds(i, 1), :]
        sin_high = sin_high_ref[pl.ds(i, 1), :]
        at = pl.ds(pl.multiple_of(i * LOW, LOW), LOW)
        cos_ref[at, :] = (cos_high * cos_low - sin_high * sin_low).astype(BF16)
        sin_ref[at, :] = (-(sin_high * cos_low + cos_high * sin_low)).astype(BF16)

    sub = levels * lats
    row, col = iota((sub, sub), 0), iota((sub, sub), 1)
    held = jnp.zeros((sub, sub), I32)
    for r in range(levels):
        held = jnp.where(col // lats == r, order_ref[0, r], held)
    lat = row // 4 % 2 * 2 + row // 8
    pick = jnp.where((held == row % 4) & (col % lats == lat), 1.0, 0.0).astype(BF16)
    power = jnp.concatenate([exp_ref[r] for r in range(levels)], axis=0).astype(F32)
    scale = matmul(pick, jnp.exp2(power).astype(BF16), 1, 0)
    stored = jnp.concatenate([traj_ref[r] for r in range(levels)], axis=0)
    ordered = matmul(pick, stored, 1, 0)
    full = cos_ref.shape[0]
    ahead = iota((sub, full), 1)
    reverse = jnp.where(iota((full, full), 0) + iota((full, full), 1) == full, 1.0, 0.0).astype(BF16)
    for b in range(NBLK):
        start = b * width
        piece = ordered[:, start : start + full] * scale[:, b : b + 1]
        gain = jnp.where(ahead <= width // 2, norm * (1.0 + jnp.tanh(piece)), 0.0)
        gain_ref[b * sub : (b + 1) * sub, :] = gain
        back = ordered[:, start + width - full : start + width].astype(BF16)
        piece = matmul(back, reverse, 1, 0) * scale[:, b : b + 1]
        gain = norm * (1.0 + jnp.tanh(piece))
        gain = jnp.where((ahead >= 1) & (2 * ahead < width), gain, 0.0)
        at = (NBLK + (b + 1) % NBLK) * sub
        gain_ref[at : at + sub, :] = gain
    send = pltpu.make_async_copy(gain_ref, gain_hbm, gain_sem)
    send.start()
    token_ref[...] = jnp.zeros(token_ref.shape, F32)
    send.wait()


def prepare(order, wave, exps, traj, norm):
    levels, lats, lons = traj.shape
    waves = wave.shape[1]
    high = -(-(lons // NBLK // 2 + 1) // LOW)
    table = jax.ShapeDtypeStruct((high * LOW, waves), BF16)
    gain = jax.ShapeDtypeStruct((2 * NBLK * levels * lats, high * LOW), F32)
    vmem = pl.BlockSpec(memory_space=pltpu.VMEM)
    return pl.pallas_call(
        functools.partial(prepare_kernel, norm=norm),
        in_specs=[pl.BlockSpec(memory_space=pltpu.SMEM)] + [vmem] * 3,
        out_specs=[vmem, vmem, pl.BlockSpec(memory_space=pltpu.HBM), vmem],
        out_shape=(table, table, gain, jax.ShapeDtypeStruct((8, 128), F32)),
        scratch_shapes=[pltpu.VMEM((-(-high // 8) * 8, waves), F32)] * 2
        + [pltpu.VMEM(gain.shape, F32), pltpu.SemaphoreType.DMA],
        compiler_params=pltpu.CompilerParams(vmem_limit_bytes=16 * 2**20),
        cost_estimate=pl.CostEstimate(flops=12_000_000, bytes_accessed=20_000_000, transcendentals=0),
        name="prepare",
    )(order, wave, exps, traj)


def gather_kernel(index_ref, token_ref, in_ref, out_ref, below_ref, share_ref):
    core = index_ref[0] % 2
    sources, comps, sub, slots = in_ref.shape
    bands = sources // 2
    pick = one_hot(iota((sub // 4, sub), 1) // 4, iota((sub // 4, sub), 0))
    totals = []
    for side in range(2):
        at = core if side == 0 else 1 - core
        flat = [
            jnp.concatenate([in_ref[2 * d + at, c] for d in range(bands)], axis=1)
            for c in range(comps)
        ]
        if side == 0:
            out_ref[...] = jnp.concatenate(flat, axis=0)
        totals.append([matmul(pick, value, 1, 0) for value in flat])
    below_ref[...] = jnp.concatenate(totals[1], axis=0)
    chip = [mine + other for mine, other in zip(*totals)]
    chip = jnp.where(core == 0, chip[0], chip[1])
    half = chip.shape[1] // 2
    share = jnp.concatenate([chip[:, :half], chip[:, half:]], axis=0).astype(BF16)
    for d in range(share_ref.shape[0]):
        share_ref[d] = share


def gather_rows(index, token, blocks, groups):
    sources, comps, sub, slots = blocks.shape
    waves = sources // 2 * slots
    smem = pl.BlockSpec(memory_space=pltpu.SMEM)
    vmem = pl.BlockSpec(memory_space=pltpu.VMEM)
    return pl.pallas_call(
        gather_kernel,
        in_specs=[smem, vmem, vmem],
        out_specs=[vmem] * 3,
        out_shape=(
            jax.ShapeDtypeStruct((comps * sub, waves), BF16),
            jax.ShapeDtypeStruct((comps * sub // 4, waves), F32),
            jax.ShapeDtypeStruct((groups, sub // 2, waves // 2), BF16),
        ),
        compiler_params=pltpu.CompilerParams(vmem_limit_bytes=8 * 2**20),
        name="gather_rows",
    )(index, token, blocks)


def forcing_kernel(
    index_ref, coef_ref, total_ref, below_ref, four_ref, wave_ref, gain_ref, cos_ref, sin_ref,
    out_ref, held_ref, held_sem, *, norm
):
    fetch = pltpu.make_async_copy(gain_ref, held_ref, held_sem)
    fetch.start()
    me = index_ref[0]
    groups = total_ref.shape[0]
    rows, waves = below_ref.shape
    both = four_ref.shape[0]
    sub = both // 2
    wave = wave_ref[...]
    parts = []
    for c in range(2):
        part = jnp.zeros(total_ref.shape[1:], F32)
        for z in range(groups // 2):
            part = part + jnp.where(z < me // 2, total_ref[2 * z + c].astype(F32), 0.0)
        parts.append(jnp.concatenate([part[: rows // 2], part[rows // 2 :]], axis=1))
    carry = jnp.concatenate(parts, axis=0) + jnp.where(me % 2 == 1, below_ref[...], 0.0)
    four = four_ref[...]
    row, col = iota((both, both), 0), iota((both, both), 1)
    earlier = jnp.where((row // 4 == col // 4) & (col < row), 1.0, 0.0).astype(BF16)
    copies = one_hot(iota((both, rows), 0) // 4, iota((both, rows), 1))
    above = matmul(earlier, four, 1, 0) + matmul(copies, carry.astype(BF16), 1, 0)
    level = iota((both, 1), 0) % 4
    coef = jnp.zeros((both, 1), F32)
    for l in range(4):
        coef = jnp.where(level == l, coef_ref[l], coef)
    mixed = (four.astype(F32) + coef * above).astype(BF16)
    first, second = mixed[:sub], mixed[sub:]
    with_cos, with_sin = [], []
    for b in range(NBLK):
        cos_b, sin_b = (v.astype(BF16) for v in turns(wave, b))
        with_cos.append(first * cos_b - second * sin_b)
        with_sin.append(first * sin_b + second * cos_b)
    with_cos = jnp.concatenate(with_cos, axis=0)
    with_sin = jnp.concatenate(with_sin, axis=0)
    even = matmul(with_cos, cos_ref[...], 1, 1)
    odd = matmul(with_sin, sin_ref[...], 1, 1)
    half = NBLK * sub
    fetch.wait()
    ahead = held_ref[:half, :] * (even + odd)
    behind = held_ref[half:, :] * (even - odd)
    forcing = jnp.concatenate([ahead, behind], axis=0).astype(BF16)
    by_cos = matmul(forcing, cos_ref[...], 1, 0)
    by_sin = matmul(forcing, sin_ref[...], 1, 0)
    by_cos = by_cos[:half] + by_cos[half:]
    by_sin = by_sin[:half] - by_sin[half:]
    first = jnp.zeros((sub, waves), F32)
    second = jnp.zeros((sub, waves), F32)
    for b in range(NBLK):
        cos_b, sin_b = turns(wave, b)
        part_cos, part_sin = by_cos[b * sub : (b + 1) * sub], by_sin[b * sub : (b + 1) * sub]
        first = first + part_cos * cos_b + part_sin * sin_b
        second = second + part_sin * cos_b - part_cos * sin_b
    bands, comps, _, slots = out_ref.shape
    half = sub // 2
    for c, value in enumerate((first, second)):
        value = value * norm
        sym, anti = value[:half] + value[half:], value[:half] - value[half:]
        sides = jnp.concatenate([sym, anti], axis=0).astype(BF16)
        for d in range(bands):
            out_ref[d, c] = sides[:, slots * d : slots * (d + 1)]


def forcing_part(index, coef, totals, below, four, wave, gain, cos_t, sin_t, shape, norm):
    vmem = pl.BlockSpec(memory_space=pltpu.VMEM)
    smem = pl.BlockSpec(memory_space=pltpu.SMEM)
    return pl.pallas_call(
        functools.partial(forcing_kernel, norm=norm),
        in_specs=[smem] * 2 + [vmem] * 4 + [pl.BlockSpec(memory_space=pltpu.HBM)] + [vmem] * 2,
        out_specs=vmem,
        scratch_shapes=[pltpu.VMEM(gain.shape, F32), pltpu.SemaphoreType.DMA],
        out_shape=jax.ShapeDtypeStruct(shape, BF16),
        compiler_params=pltpu.CompilerParams(vmem_limit_bytes=40 * 2**20),
        cost_estimate=pl.CostEstimate(flops=900_000_000, bytes_accessed=8_000_000, transcendentals=0),
        name="forcing_part",
    )(index, coef, totals, below, four, wave, gain, cos_t, sin_t)


def body(adj_spec, wave_of_slot, legendre, lat_weight, traj, traj_exp, traj_order, lev_coef):
    levels, degrees = adj_spec.shape[0], adj_spec.shape[3]
    groups = lax.axis_size(("z", "core"))
    norm = 1.0 / math.sqrt(degrees)
    band = lax.axis_index("band").astype(I32)[None]
    index = lax.axis_index(("z", "core")).astype(I32)[None]
    wave = wave_of_slot[None, :]
    blocks = synthesis(adj_spec, legendre, band, wave_of_slot, lat_weight)
    blocks = lax.all_to_all(blocks, ("band", "core"), split_axis=0, concat_axis=0, tiled=True)
    cos_t, sin_t, gain, token = prepare(traj_order, wave, traj_exp, traj, norm)
    four, below, shares = gather_rows(index, token, blocks, groups)
    totals = lax.all_to_all(shares, ("z", "core"), split_axis=0, concat_axis=0, tiled=True)
    shape = (blocks.shape[0] // 2, *blocks.shape[1:])
    sides = forcing_part(
        index, lev_coef, totals, below, four, wave, gain, cos_t, sin_t, shape, norm
    )
    sides = lax.all_to_all(sides, "band", split_axis=0, concat_axis=0, tiled=True)
    return analysis(sides, legendre, band, wave_of_slot, levels)


def solution(mesh):
    chips = Mesh(mesh.devices.reshape(mesh.shape["band"], -1, 2), ("band", "z", "core"))
    lev = ("z", "core")
    return jax.shard_map(
        body,
        mesh=chips,
        in_specs=(
            P(lev, "band", None, None),
            P(),
            P("band", None, None),
            P(),
            P(lev, "band", None),
            P(lev, "band", None),
            P(lev, None),
            P(lev),
        ),
        out_specs=P(lev, "band", None, None),
        check_vma=False,
    )
```

time: 66.5 us -> 67.2 us (1.011)
  blocking collectives: 33.2 us -> 28.8 us
  waiting for transfers between devices: 2.17 us -> 4.95 us
  Pallas kernels: 20.4 us -> 22.6 us
  starting transfers between devices: 7.58 us -> 8.66 us
  local copies, waits for them, and re-layouts: 2.68 us -> 1.76 us
    all_gather x1 -> x0, blocking collectives: 22.8 us -> none  [body(): totals = lax.all_gather(total, 'lev')]
    all_to_all x0 -> x1, blocking collectives: none -> 18.2 us  [body(): lax.all_to_all(shares, ('z', 'core'), split_axis=0, concat_axis=0, tiled=...]
    all_to_all x1, waiting for transfers between devices: 2.17 us -> 4.95 us  [body(): lax.all_to_all(blocks, ('band', 'core'), split_axis=0, concat_axis=0, til...]
    pallas_call x3, Pallas kernels: 14.6 us -> 16.6 us  [the longest x1 9.75 us: synthesis(): pl.pallas_call(synthesis_kernel, in_specs=[smem, smem, vmem, hbm, hbm], o...]
    all_to_all x1, starting transfers between devices: 7.58 us -> 8.66 us  [body(): lax.all_to_all(blocks, ('band', 'core'), split_axis=0, concat_axis=0, til...]
    unnamed x14, local copies, waits for them, and re-layouts: 2.67 us -> 1.76 us
  transfers between devices with their start and end apart: 1 -> 1, of which waited for: 1 -> 1; matrix products, arithmetic and copies ran while one was open for 0% -> 0% of each run, Pallas kernels for 4% -> 5%
where the time goes in v4:
time: 67.2 us; the launch traced here: 66.9 us
  blocking collectives  28.8 us (43%)
  Pallas kernels  22.6 us (34%)
  starting transfers between devices  8.66 us (13%)
  waiting for transfers between devices  4.95 us (7%)
  local copies, waits for them, and re-layouts  1.76 us (3%)
    all_to_all x1, blocking collectives, body(): lax.all_to_all(shares, ('z', 'core'), split_axis=0, concat_axis=0, tiled=...  18.2 us
    all_to_all x1, blocking collectives, body(): lax.all_to_all(sides, 'band', split_axis=0, concat_axis=0, tiled=True)  10.7 us
    pallas_call x1, Pallas kernels, synthesis(): pl.pallas_call(synthesis_kernel, in_specs=[smem, smem, vmem, hbm, hbm], o...  9.75 us
    all_to_all x1, starting transfers between devices, body(): lax.all_to_all(blocks, ('band', 'core'), split_axis=0, concat_axis=0, til...  8.66 us
    pallas_call x1, Pallas kernels, analysis(): pl.pallas_call(analysis_kernel, in_specs=[smem, smem, vmem, hbm], out_spe...  5.64 us
    all_to_all x1, waiting for transfers between devices, body(): lax.all_to_all(blocks, ('band', 'core'), split_axis=0, concat_axis=0, til...  4.95 us
    pallas_call x1, Pallas kernels, prepare(): pl.pallas_call(functools.partial(prepare_kernel, norm=norm), in_specs=[pl...  3.18 us
    pallas_call x1, Pallas kernels, forcing_part(): pl.pallas_call(functools.partial(forcing_kernel, norm=norm), in_specs=[sm...  2.8 us
  transfers between devices with their start and end apart: 1, of which 1 were waited for; matrix products, arithmetic and copies ran while one was open for 0% of the time, Pallas kernels for 5%

profile of v4, /device:TPU:1, one launch (start us, length us, event | category | flops | bytes accessed | tf_op | source)
XLA Modules:
  0.0 66.9 jit_solution(10845752558312474884)
XLA Ops:
  0.0 0.0 copy-start.6
  0.0 0.0 copy-start.2
  0.0 0.0 copy-start.3
  0.0 0.0 copy-start.4
  0.0 0.0 copy-start.5
  0.0 9.8 %synthesis.1 = bf16[32,2,16,80]{3,2,1,0:T(8,128)(2,1)} custom-call(s32[1]{0:T(128)} %bitcast.band_ref, s32[1280]{0:T(1024)} %wave_ref.3, f32[1,32]{1,0:T(1,128)} %bitcast.3, bf16[4,80,2,1280]{3,2,1,0:T(2,128)(2,1)} %adj_hbm.1, bf16[80,32,1280]{2,1,0:T(8,128)(2,1)} %leg_hbm.3), custom_call_target="tpu_custom_call" | custom-call | tf_op jit(solution)/shard_map/synthesis/pallas_call | solution.py:115
  9.8 8.7 %all-to-all-start = ((bf16[32,2,16,80]{3,2,1,0:T(8,128)(2,1)}), bf16[32,2,16,80]{3,2,1,0:T(8,128)(2,1)}, u32[]{:S(2)}, u32[]{:S(2)}) async-start(bf16[32,2,16,80]{3,2,1,0:T(8,128)(2,1)} %synthesis.1), calls=%async_computation | async-start | bytes 524288 | tf_op jit(solution)/shard_map/all_to_all | solution.py:440
  18.5 0.0 copy-done.6
  18.5 0.0 copy-done.2
  18.5 0.0 copy-done.3
  18.5 0.0 copy-done.4
  18.5 3.2 %prepare.1 = (bf16[656,1280]{1,0:T(8,128)(2,1)S(1)}, bf16[656,1280]{1,0:T(8,128)(2,1)S(1)}, f32[128,656]{1,0:T(8,128)S(1)}, f32[8,128]{1,0:T(8,128)S(1)}) custom-call(s32[1,4]{1,0:T(1,128)S(1)} %copy-done.4, s32[1,1280]{1,0:T(1,128)S(1)} %broadcast_in_dim.14.wave_ref, s32[4,4,4]{2,1,0:T(4,128)S(1)} %copy-done.3, bf16[4,4,5136]{2,1,0:T(4,128)(2,1)S(1)} %copy-done.2), custom_call_target="tpu_custom_call" | custom-call | flops 12000000 | bytes 20000000 | tf_op jit(solution)/shard_map/prepare/pallas_call | solution.py:296
  21.7 0.0 copy-start
  21.7 0.7 %copy-done = f32[128,656]{1,0:T(8,128)} copy-done((f32[128,656]{1,0:T(8,128)}, f32[128,656]{1,0:T(8,128)S(1)}, u32[]{:S(2)}) %copy-start) | copy-done | bytes 335896
  22.5 5.0 %all-to-all-done.in_ref = bf16[32,2,16,80]{3,2,1,0:T(8,128)(2,1)} async-done(((bf16[32,2,16,80]{3,2,1,0:T(8,128)(2,1)}), bf16[32,2,16,80]{3,2,1,0:T(8,128)(2,1)}, u32[]{:S(2)}, u32[]{:S(2)}) %all-to-all-start) | async-done | bytes 163872 | tf_op jit(solution)/shard_map/all_to_all | solution.py:440
  27.4 1.2 %gather_rows.1 = (bf16[32,1280]{1,0:T(8,128)(2,1)S(1)}, f32[8,1280]{1,0:T(8,128)S(1)}, bf16[16,8,640]{2,1,0:T(8,128)(2,1)S(1)}) custom-call(s32[1]{0:T(128)} %bitcast.1.index_ref, f32[8,128]{1,0:T(8,128)S(1)} %get-tuple-element.12.token_ref, bf16[32,2,16,80]{3,2,1,0:T(8,128)(2,1)} %all-to-all-done.in_ref), custom_call_target="tpu_custom_call" | custom-call | tf_op jit(solution)/shard_map/gather_rows/pallas_call | solution.py:338
  28.6 18.2 %all_to_all.15.total_ref = bf16[16,8,640]{2,1,0:T(8,128)(2,1)S(1)} all-to-all(bf16[16,8,640]{2,1,0:T(8,128)(2,1)S(1)} %get-tuple-element.13), channel_id=1, replica_groups=mesh['band'=16,'z'=8,'core'=2] {'z','core'}, dimensions={0} | all-to-all | bytes 327680 | tf_op jit(solution)/shard_map/all_to_all | solution.py:443
  46.8 0.0 copy-done.5
  46.8 0.0 copy-start.1
  46.8 1.0 %copy-done.1 = f32[128,656]{1,0:T(8,128)S(1)} copy-done((f32[128,656]{1,0:T(8,128)S(1)}, f32[128,656]{1,0:T(8,128)}, u32[]{:S(2)}) %copy-start.1) | copy-done | bytes 335896
  47.8 2.8 %forcing_part.1 = bf16[16,2,16,80]{3,2,1,0:T(8,128)(2,1)S(1)} custom-call(s32[1]{0:T(128)} %bitcast.1.index_ref, f32[4]{0:T(128)S(1)} %copy-done.5, bf16[16,8,640]{2,1,0:T(8,128)(2,1)S(1)} %all_to_all.15.total_ref, f32[8,1280]{1,0:T(8,128)S(1)} %get-tuple-element.14.below_ref, bf16[32,1280]{1,0:T(8,128)(2,1)S(1)} %get-tuple-element.15.four_ref, ...), custom_call_target="tpu_custom_call" | custom-call | flops 900000000 | bytes 8000000 | tf_op jit(solution)/shard_map/forcing_part/pallas_call | solution.py:420
  50.6 10.7 %all_to_all.16.in_ref = bf16[16,2,16,80]{3,2,1,0:T(8,128)(2,1)} all-to-all(bf16[16,2,16,80]{3,2,1,0:T(8,128)(2,1)S(1)} %forcing_part.1), channel_id=1, replica_groups=mesh['band'=16,'z'=8,'core'=2] {'band'}, dimensions={0} | all-to-all | bytes 163840 | tf_op jit(solution)/shard_map/all_to_all | solution.py:448
  61.3 5.6 %analysis.1 = bf16[4,80,2,1280]{3,2,1,0:T(2,128)(2,1)} custom-call(s32[1]{0:T(128)} %bitcast.band_ref, s32[1280]{0:T(1024)} %wave_ref.3, bf16[16,2,16,80]{3,2,1,0:T(8,128)(2,1)} %all_to_all.16.in_ref, bf16[80,32,1280]{2,1,0:T(8,128)(2,1)} %leg_hbm.3), custom_call_target="tpu_custom_call" | custom-call | tf_op jit(solution)/shard_map/analysis/pallas_call | solution.py:194
  (1 shorter events, 0.0 us)
Async XLA Ops:
  0.0 18.5 %copy-start.6 = (s32[1280]{0:T(1024)S(1)}, s32[1280]{0:T(1024)}, u32[]{:S(2)}) copy-start(s32[1280]{0:T(1024)} %wave_ref.3) | copy-start | bytes 15364
  0.0 18.5 %copy-start.2 = (bf16[4,4,5136]{2,1,0:T(4,128)(2,1)S(1)}, bf16[4,4,5136]{2,1,0:T(4,128)(2,1)}, u32[]{:S(2)}) copy-start(bf16[4,4,5136]{2,1,0:T(4,128)(2,1)} %traj_ref.1) | copy-start | bytes 493060
  0.0 18.5 %copy-start.3 = (s32[4,4,4]{2,1,0:T(4,128)S(1)}, s32[4,4,4]{2,1,0:T(4,128)}, u32[]{:S(2)}) copy-start(s32[4,4,4]{2,1,0:T(4,128)} %exp_ref.1) | copy-start | bytes 772
  0.0 18.5 %copy-start.4 = (s32[1,4]{1,0:T(1,128)S(1)}, s32[1,4]{1,0:T(1,128)}, u32[]{:S(2)}) copy-start(s32[1,4]{1,0:T(1,128)} %order_ref.1) | copy-start | bytes 52
  0.0 46.8 %copy-start.5 = (f32[4]{0:T(128)S(1)}, f32[4]{0:T(128)}, u32[]{:S(2)}) copy-start(f32[4]{0:T(128)} %coef_ref.1) | copy-start | bytes 52
  9.8 17.6 %all-to-all-start = ((bf16[32,2,16,80]{3,2,1,0:T(8,128)(2,1)}), bf16[32,2,16,80]{3,2,1,0:T(8,128)(2,1)}, u32[]{:S(2)}, u32[]{:S(2)}) async-start(bf16[32,2,16,80]{3,2,1,0:T(8,128)(2,1)} %synthesis.1), calls=%async_computation | async-start | bytes 524288 | tf_op jit(solution)/shard_map/all_to_all | solution.py:440
  21.7 0.7 %copy-start = (f32[128,656]{1,0:T(8,128)}, f32[128,656]{1,0:T(8,128)S(1)}, u32[]{:S(2)}) copy-start(f32[128,656]{1,0:T(8,128)S(1)} %get-tuple-element.16.gain_ref) | copy-start | bytes 1007620
  46.8 1.0 %copy-start.1 = (f32[128,656]{1,0:T(8,128)S(1)}, f32[128,656]{1,0:T(8,128)}, u32[]{:S(2)}) copy-start(f32[128,656]{1,0:T(8,128)} %copy-done) | copy-start | bytes 1007620

commit v5 on v4

--- a/solution.py
+++ b/solution.py
@@ -11,6 +11,7 @@
 
 F32, BF16, I32 = jnp.float32, jnp.bfloat16, jnp.int32
 GROUP = 8
+CHUNK = 2
 
 
 def iota(shape, dim):
@@ -36,7 +37,8 @@
 
 
 def synthesis_kernel(
-    band_ref, wave_ref, weight_ref, adj_hbm, leg_hbm, out_ref, adj_ref, leg_ref, acc_ref, adj_sem, leg_sem
+    band_ref, wave_ref, weight_ref, adj_hbm, leg_hbm, out_ref,
+    adj_ref, leg_ref, acc_ref, spread_ref, order_ref, adj_sem, leg_sem
 ):
     levels, slots, comps, degrees = adj_ref.shape
     rows = GROUP * comps
@@ -52,63 +54,60 @@
         for fetch in fetches[-1]:
             fetch.start()
     weight = jnp.concatenate([weight_ref[...]] * (128 // heights), axis=1)
-    half = levels * rows
-    for g in range(steps):
-        for fetch in fetches[g]:
-            fetch.wait()
-        here = pl.ds(g * GROUP, GROUP)
-        limit = limits(band_ref, wave_ref, g, slots, comps, degrees)
-        degree = iota((rows, degrees), 1)
-        inside = degree < limit
-        even = jnp.where(inside & (degree % 2 == 0), 1.0, 0.0).astype(BF16)
-        odd = jnp.where(inside & (degree % 2 == 1), 1.0, 0.0).astype(BF16)
-        values = [adj_ref[l, here].reshape(rows, degrees) for l in range(levels)]
-        left = jnp.concatenate([v * even for v in values] + [v * odd for v in values], axis=0)
-        table = leg_ref[here].reshape(GROUP * heights, degrees)
-        both = matmul(left, table, 1, 1)
-        shape = both.shape
-        own = (iota(shape, 0) % rows) // comps == iota(shape, 1) // heights
-        both = jnp.where(own, both, 0.0)
-        both = both[:, :128] + both[:, 128:]
-        both = both + pltpu.roll(both, 64, 1)
-        both = both + pltpu.roll(both, 32, 1)
-        from_even, from_odd = both[:half], both[half:]
-        north = (from_even + from_odd) * weight
-        south = (from_even - from_odd) * weight
-        for l in range(levels):
-            acc_ref[l, g * rows : (g + 1) * rows, :] = north[l * rows : (l + 1) * rows]
-            acc_ref[levels + l, g * rows : (g + 1) * rows, :] = south[l * rows : (l + 1) * rows]
-    total = acc_ref.shape[1]
-    sides = 2 * levels
-    lane = iota((total, 128), 1) // heights
-    blocks = []
-    for k in range(sides // 4):
-        mix = acc_ref[4 * k]
-        for r in range(1, 4):
-            mix = jnp.where(lane == r, acc_ref[4 * k + r], mix)
-        blocks.append(mix.astype(BF16))
-    wide = jnp.concatenate(blocks, axis=1)
-    col = iota((total, 2 * 128), 1)
-    source = iota((total, 2 * 128), 0)
-    comp, slot = col // 128, col % 128
-    spread = jnp.where((source == slot * comps + comp) & (slot < slots), 1.0, 0.0).astype(BF16)
-    turned = matmul(wide, spread, 0, 0).astype(BF16)
-    size = sides * heights
-    dest = iota((size, size), 0)
-    origin = iota((size, size), 1)
+    total = slots * comps
+    col, source = iota((total, comps * 128), 1), iota((total, comps * 128), 0)
+    slot = col % 128
+    own = (source == slot * comps + col // 128) & (slot < slots)
+    spread_ref[...] = jnp.where(own, 1.0, 0.0).astype(BF16)
+    size = 2 * levels * heights
+    dest, origin = iota((size, size), 1), iota((size, size), 0)
     band, e, hh, l = dest // 16, dest // 8 % 2, dest // 4 % 2, dest % 4
-    wanted = (e * levels + l) * heights + band * 2 + hh
-    moved = matmul(one_hot(wanted, origin), turned, 1, 0).astype(BF16)
+    order_ref[...] = one_hot((e * levels + l) * heights + band * 2 + hh, origin)
+    shape = (2 * levels * rows, GROUP * heights)
+    own = (iota(shape, 0) % rows) // comps == iota(shape, 1) // heights
+    degree = iota((rows, degrees), 1)
+    sign = jnp.where(degree % 2 == 0, 1.0, -1.0).astype(BF16)
+    lane = iota((rows, 128), 1) // heights
+    for first in range(0, steps, CHUNK):
+        group = range(first, first + CHUNK)
+        for g in group:
+            for fetch in fetches[g]:
+                fetch.wait()
+        wide = []
+        for g in group:
+            here = pl.ds(g * GROUP, GROUP)
+            limit = limits(band_ref, wave_ref, g, slots, comps, degrees)
+            inside = jnp.where(degree < limit, 1.0, 0.0).astype(BF16)
+            flipped = inside * sign
+            values = [adj_ref[l, here].reshape(rows, degrees) for l in range(levels)]
+            left = jnp.concatenate(
+                [v * inside for v in values] + [v * flipped for v in values], axis=0
+            )
+            both = matmul(left, leg_ref[here].reshape(GROUP * heights, degrees), 1, 1)
+            both = jnp.where(own, both, 0.0)
+            both = both[:, :128] + both[:, 128:]
+            both = both + pltpu.roll(both, 64, 1)
+            both = (both + pltpu.roll(both, 32, 1)) * weight
+            blocks = []
+            for k in range(2 * levels // 4):
+                mix = both[4 * k * rows : (4 * k + 1) * rows]
+                for r in range(1, 4):
+                    part = both[(4 * k + r) * rows : (4 * k + r + 1) * rows]
+                    mix = jnp.where(lane == r, part, mix)
+                blocks.append(mix.astype(BF16))
+            wide.append(jnp.concatenate(blocks, axis=1))
+        acc_ref[first * rows : (first + CHUNK) * rows, :] = jnp.concatenate(wide, axis=0)
+    wide = matmul(acc_ref[...], order_ref[...], 1, 0).astype(BF16)
+    moved = matmul(wide, spread_ref[...], 0, 0).astype(BF16)
     for d in range(size // 16):
         for c in range(comps):
-            tile = moved[16 * d : 16 * d + 16, 128 * c : 128 * c + slots]
-            for core in range(2):
-                out_ref[2 * d + core, c] = tile
+            out_ref[d, c] = moved[16 * d : 16 * d + 16, 128 * c : 128 * c + slots]
 
 
 def synthesis(adj, leg, band, waves, weight):
     levels, slots, comps, degrees = adj.shape
     heights = leg.shape[1]
+    size = 2 * levels * heights
     smem = pl.BlockSpec(memory_space=pltpu.SMEM)
     vmem = pl.BlockSpec(memory_space=pltpu.VMEM)
     hbm = pl.BlockSpec(memory_space=pltpu.HBM)
@@ -116,11 +115,13 @@
         synthesis_kernel,
         in_specs=[smem, smem, vmem, hbm, hbm],
         out_specs=vmem,
-        out_shape=jax.ShapeDtypeStruct((32, comps, 16, slots), BF16),
+        out_shape=jax.ShapeDtypeStruct((16, comps, 16, slots), BF16),
         scratch_shapes=[
             pltpu.VMEM(adj.shape, BF16),
             pltpu.VMEM(leg.shape, BF16),
-            pltpu.VMEM((2 * levels, slots * comps, 128), F32),
+            pltpu.VMEM((slots * comps, size), BF16),
+            pltpu.VMEM((slots * comps, comps * 128), BF16),
+            pltpu.VMEM((size, size), BF16),
             pltpu.SemaphoreType.DMA((slots // GROUP,)),
             pltpu.SemaphoreType.DMA((slots // GROUP,)),
         ],
@@ -306,47 +307,57 @@
     )(order, wave, exps, traj)
 
 
-def gather_kernel(index_ref, token_ref, in_ref, out_ref, below_ref, share_ref):
+def gather_kernel(token_ref, in_ref, out_ref, total_ref):
+    sources, comps, sub, slots = in_ref.shape
+    pick = one_hot(iota((8, comps * sub), 1) // 4, iota((8, comps * sub), 0))
+    flat = [jnp.concatenate([in_ref[d, c] for d in range(sources)], axis=1) for c in range(comps)]
+    flat = jnp.concatenate(flat, axis=0)
+    out_ref[...] = flat
+    total_ref[...] = matmul(pick, flat, 1, 0)
+
+
+def gather_rows(token, blocks):
+    sources, comps, sub, slots = blocks.shape
+    vmem = pl.BlockSpec(memory_space=pltpu.VMEM)
+    return pl.pallas_call(
+        gather_kernel,
+        in_specs=[vmem] * 2,
+        out_specs=[vmem] * 2,
+        out_shape=(
+            jax.ShapeDtypeStruct((comps * sub, sources * slots), BF16),
+            jax.ShapeDtypeStruct((comps * sub // 4, sources * slots), F32),
+        ),
+        compiler_params=pltpu.CompilerParams(vmem_limit_bytes=8 * 2**20),
+        name="gather_rows",
+    )(token, blocks)
+
+
+def share_kernel(index_ref, pair_ref, share_ref, below_ref):
     core = index_ref[0] % 2
-    sources, comps, sub, slots = in_ref.shape
-    bands = sources // 2
-    pick = one_hot(iota((sub // 4, sub), 1) // 4, iota((sub // 4, sub), 0))
-    totals = []
-    for side in range(2):
-        at = core if side == 0 else 1 - core
-        flat = [
-            jnp.concatenate([in_ref[2 * d + at, c] for d in range(bands)], axis=1)
-            for c in range(comps)
-        ]
-        if side == 0:
-            out_ref[...] = jnp.concatenate(flat, axis=0)
-        totals.append([matmul(pick, value, 1, 0) for value in flat])
-    below_ref[...] = jnp.concatenate(totals[1], axis=0)
-    chip = [mine + other for mine, other in zip(*totals)]
-    chip = jnp.where(core == 0, chip[0], chip[1])
-    half = chip.shape[1] // 2
+    chip = pair_ref[0] + pair_ref[1]
+    below_ref[...] = pair_ref[1 - core]
+    rows, waves = chip.shape
+    half = waves // 2
+    chip = jnp.where(core == 0, chip[: rows // 2], chip[rows // 2 :])
     share = jnp.concatenate([chip[:, :half], chip[:, half:]], axis=0).astype(BF16)
     for d in range(share_ref.shape[0]):
         share_ref[d] = share
 
 
-def gather_rows(index, token, blocks, groups):
-    sources, comps, sub, slots = blocks.shape
-    waves = sources // 2 * slots
-    smem = pl.BlockSpec(memory_space=pltpu.SMEM)
-    vmem = pl.BlockSpec(memory_space=pltpu.VMEM)
-    return pl.pallas_call(
-        gather_kernel,
-        in_specs=[smem, vmem, vmem],
-        out_specs=[vmem] * 3,
+def share_rows(index, pair, groups):
+    _, rows, waves = pair.shape
+    vmem = pl.BlockSpec(memory_space=pltpu.VMEM)
+    return pl.pallas_call(
+        share_kernel,
+        in_specs=[pl.BlockSpec(memory_space=pltpu.SMEM), vmem],
+        out_specs=[vmem] * 2,
         out_shape=(
-            jax.ShapeDtypeStruct((comps * sub, waves), BF16),
-            jax.ShapeDtypeStruct((comps * sub // 4, waves), F32),
-            jax.ShapeDtypeStruct((groups, sub // 2, waves // 2), BF16),
+            jax.ShapeDtypeStruct((groups, rows, waves // 2), BF16),
+            jax.ShapeDtypeStruct((rows, waves), F32),
         ),
         compiler_params=pltpu.CompilerParams(vmem_limit_bytes=8 * 2**20),
-        name="gather_rows",
-    )(index, token, blocks)
+        name="share_rows",
+    )(index, pair)
 
 
 def forcing_kernel(
@@ -423,7 +434,7 @@
         out_specs=vmem,
         scratch_shapes=[pltpu.VMEM(gain.shape, F32), pltpu.SemaphoreType.DMA],
         out_shape=jax.ShapeDtypeStruct(shape, BF16),
-        compiler_params=pltpu.CompilerParams(vmem_limit_bytes=40 * 2**20),
+        compiler_params=pltpu.CompilerParams(vmem_limit_bytes=41_943_040),
         cost_estimate=pl.CostEstimate(flops=900_000_000, bytes_accessed=8_000_000, transcendentals=0),
         name="forcing_part",
     )(index, coef, totals, below, four, wave, gain, cos_t, sin_t)
@@ -437,13 +448,14 @@
     index = lax.axis_index(("z", "core")).astype(I32)[None]
     wave = wave_of_slot[None, :]
     blocks = synthesis(adj_spec, legendre, band, wave_of_slot, lat_weight)
-    blocks = lax.all_to_all(blocks, ("band", "core"), split_axis=0, concat_axis=0, tiled=True)
+    blocks = lax.all_to_all(blocks, "band", split_axis=0, concat_axis=0, tiled=True)
     cos_t, sin_t, gain, token = prepare(traj_order, wave, traj_exp, traj, norm)
-    four, below, shares = gather_rows(index, token, blocks, groups)
+    four, total = gather_rows(token, blocks)
+    pair = lax.all_gather(total, "core")
+    shares, below = share_rows(index, pair, groups)
     totals = lax.all_to_all(shares, ("z", "core"), split_axis=0, concat_axis=0, tiled=True)
-    shape = (blocks.shape[0] // 2, *blocks.shape[1:])
     sides = forcing_part(
-        index, lev_coef, totals, below, four, wave, gain, cos_t, sin_t, shape, norm
+        index, lev_coef, totals, below, four, wave, gain, cos_t, sin_t, blocks.shape, norm
     )
     sides = lax.all_to_all(sides, "band", split_axis=0, concat_axis=0, tiled=True)
     return analysis(sides, legendre, band, wave_of_slot, levels)

time: 67.2 us -> 64.6 us (0.961)
  blocking collectives: 28.8 us -> 33 us
  Pallas kernels: 22.6 us -> 18.9 us
  waiting for transfers between devices: 4.95 us -> 1.96 us
  starting transfers between devices: 8.66 us -> 7.59 us
  local copies, waits for them, and re-layouts: 1.76 us -> 2.67 us
    all_gather x0 -> x1, blocking collectives: none -> 3.59 us  [body(): pair = lax.all_gather(total, 'core')]
    all_to_all x1, waiting for transfers between devices: 4.95 us -> 1.96 us  [body(): lax.all_to_all(blocks, 'band', split_axis=0, concat_axis=0, tiled=True)]
    pallas_call x1, Pallas kernels: 9.75 us -> 7.09 us  [synthesis(): pl.pallas_call(synthesis_kernel, in_specs=[smem, smem, vmem, hbm, hbm], o...]
    all_to_all x1, starting transfers between devices: 8.66 us -> 7.59 us  [body(): lax.all_to_all(blocks, 'band', split_axis=0, concat_axis=0, tiled=True)]
    pallas_call x1 -> x2, Pallas kernels: 1.22 us -> 0.23 us  [the longest x1 0.21 us: gather_rows(): pl.pallas_call(gather_kernel, in_specs=[vmem] * 2, out_specs=[vmem] * 2,...]
    unnamed x14, local copies, waits for them, and re-layouts: 1.76 us -> 2.66 us
where the time goes in v5:
time: 64.6 us; the launch traced here: 64.2 us
  blocking collectives  33 us (51%)
  Pallas kernels  18.9 us (29%)
  starting transfers between devices  7.59 us (12%)
  local copies, waits for them, and re-layouts  2.67 us (4%)
  waiting for transfers between devices  1.96 us (3%)
    all_to_all x1, blocking collectives, body(): lax.all_to_all(shares, ('z', 'core'), split_axis=0, concat_axis=0, tiled=...  18.3 us
    all_to_all x1, blocking collectives, body(): lax.all_to_all(sides, 'band', split_axis=0, concat_axis=0, tiled=True)  11.1 us
    all_to_all x1, starting transfers between devices, body(): lax.all_to_all(blocks, 'band', split_axis=0, concat_axis=0, tiled=True)  7.59 us
    pallas_call x1, Pallas kernels, synthesis(): pl.pallas_call(synthesis_kernel, in_specs=[smem, smem, vmem, hbm, hbm], o...  7.09 us
    pallas_call x1, Pallas kernels, analysis(): pl.pallas_call(analysis_kernel, in_specs=[smem, smem, vmem, hbm], out_spe...  5.64 us
    all_gather x1, blocking collectives, body(): pair = lax.all_gather(total, 'core')  3.59 us
    pallas_call x1, Pallas kernels, prepare(): pl.pallas_call(functools.partial(prepare_kernel, norm=norm), in_specs=[pl...  3.18 us
    pallas_call x1, Pallas kernels, forcing_part(): pl.pallas_call(functools.partial(forcing_kernel, norm=norm), in_specs=[sm...  2.81 us
  transfers between devices with their start and end apart: 1, of which 1 were waited for; matrix products, arithmetic and copies ran while one was open for 0% of the time, Pallas kernels for 5%

profile of v5, /device:TPU:1, one launch (start us, length us, event | category | flops | bytes accessed | tf_op | source)
XLA Modules:
  0.0 64.2 jit_solution(4902428900410191632)
XLA Ops:
  0.0 0.0 copy-start.6
  0.0 0.0 copy-start.3
  0.0 0.0 copy-start.4
  0.0 0.0 copy-start.5
  0.0 7.1 %synthesis.1 = bf16[16,2,16,80]{3,2,1,0:T(8,128)(2,1)} custom-call(s32[1]{0:T(128)} %bitcast.band_ref, s32[1280]{0:T(1024)} %wave_ref.3, f32[1,32]{1,0:T(1,128)} %bitcast.5, bf16[4,80,2,1280]{3,2,1,0:T(2,128)(2,1)} %adj_hbm.1, bf16[80,32,1280]{2,1,0:T(8,128)(2,1)} %leg_hbm.3), custom_call_target="tpu_custom_call" | custom-call | tf_op jit(solution)/shard_map/synthesis/pallas_call | solution.py:114
  7.1 7.6 %all-to-all-start = ((bf16[16,2,16,80]{3,2,1,0:T(8,128)(2,1)}), bf16[16,2,16,80]{3,2,1,0:T(8,128)(2,1)S(1)}, u32[]{:S(2)}, u32[]{:S(2)}) async-start(bf16[16,2,16,80]{3,2,1,0:T(8,128)(2,1)} %synthesis.1), calls=%async_computation | async-start | bytes 262144 | tf_op jit(solution)/shard_map/all_to_all | solution.py:451
  14.7 0.0 copy-done.6
  14.7 0.0 copy-done.3
  14.8 0.0 copy-done.4
  14.8 0.0 copy-start.2
  14.8 0.9 %copy-done.2 = bf16[4,4,5136]{2,1,0:T(4,128)(2,1)S(1)} copy-done((bf16[4,4,5136]{2,1,0:T(4,128)(2,1)S(1)}, bf16[4,4,5136]{2,1,0:T(4,128)(2,1)}, u32[]{:S(2)}) %copy-start.2) | copy-done | bytes 164376
  15.7 3.2 %prepare.1 = (bf16[656,1280]{1,0:T(8,128)(2,1)S(1)}, bf16[656,1280]{1,0:T(8,128)(2,1)S(1)}, f32[128,656]{1,0:T(8,128)S(1)}, f32[8,128]{1,0:T(8,128)S(1)}) custom-call(s32[1,4]{1,0:T(1,128)S(1)} %copy-done.4, s32[1,1280]{1,0:T(1,128)S(1)} %broadcast_in_dim.14.wave_ref, s32[4,4,4]{2,1,0:T(4,128)S(1)} %copy-done.3, bf16[4,4,5136]{2,1,0:T(4,128)(2,1)S(1)} %copy-done.2), custom_call_target="tpu_custom_call" | custom-call | flops 12000000 | bytes 20000000 | tf_op jit(solution)/shard_map/prepare/pallas_call | solution.py:297
  18.9 0.0 copy-start
  18.9 0.7 %copy-done = f32[128,656]{1,0:T(8,128)} copy-done((f32[128,656]{1,0:T(8,128)}, f32[128,656]{1,0:T(8,128)S(1)}, u32[]{:S(2)}) %copy-start) | copy-done | bytes 335896
  19.6 2.0 %all-to-all-done.in_ref = bf16[16,2,16,80]{3,2,1,0:T(8,128)(2,1)S(1)} async-done(((bf16[16,2,16,80]{3,2,1,0:T(8,128)(2,1)}), bf16[16,2,16,80]{3,2,1,0:T(8,128)(2,1)S(1)}, u32[]{:S(2)}, u32[]{:S(2)}) %all-to-all-start) | async-done | bytes 81952 | tf_op jit(solution)/shard_map/all_to_all | solution.py:451
  21.6 0.2 gather_rows.1
  21.8 3.6 %all-gather = f32[16,1280]{1,0:T(8,128)S(1)} all-gather(f32[8,1280]{1,0:T(8,128)S(1)} %get-tuple-element.14), channel_id=2, replica_groups=mesh['band'=16,'z'=8,'core'=2] {'core'}, dimensions={0}, use_global_device_ids=true | all-gather | bytes 122880 | tf_op jit(solution)/shard_map/all_gather | solution.py:454
  25.4 18.3 %all_to_all.15.total_ref = bf16[16,8,640]{2,1,0:T(8,128)(2,1)S(1)} all-to-all(bf16[16,8,640]{2,1,0:T(8,128)(2,1)S(1)} %get-tuple-element.15), channel_id=1, replica_groups=mesh['band'=16,'z'=8,'core'=2] {'z','core'}, dimensions={0} | all-to-all | bytes 327680 | tf_op jit(solution)/shard_map/all_to_all | solution.py:456
  43.7 0.0 copy-done.5
  43.7 0.0 copy-start.1
  43.7 1.0 %copy-done.1 = f32[128,656]{1,0:T(8,128)S(1)} copy-done((f32[128,656]{1,0:T(8,128)S(1)}, f32[128,656]{1,0:T(8,128)}, u32[]{:S(2)}) %copy-start.1) | copy-done | bytes 335896
  44.7 2.8 %forcing_part.1 = bf16[16,2,16,80]{3,2,1,0:T(8,128)(2,1)S(1)} custom-call(s32[1]{0:T(128)} %bitcast.1.index_ref, f32[4]{0:T(128)S(1)} %copy-done.5, bf16[16,8,640]{2,1,0:T(8,128)(2,1)S(1)} %all_to_all.15.total_ref, f32[8,1280]{1,0:T(8,128)S(1)} %get-tuple-element.16.below_ref, bf16[32,1280]{1,0:T(8,128)(2,1)S(1)} %get-tuple-element.17.four_ref, ...), custom_call_target="tpu_custom_call" | custom-call | flops 900000000 | bytes 8000000 | tf_op jit(solution)/shard_map/forcing_part/pallas_call | solution.py:431
  47.5 11.1 %all_to_all.16.in_ref = bf16[16,2,16,80]{3,2,1,0:T(8,128)(2,1)} all-to-all(bf16[16,2,16,80]{3,2,1,0:T(8,128)(2,1)S(1)} %forcing_part.1), channel_id=1, replica_groups=mesh['band'=16,'z'=8,'core'=2] {'band'}, dimensions={0} | all-to-all | bytes 163840 | tf_op jit(solution)/shard_map/all_to_all | solution.py:460
  58.6 5.6 %analysis.1 = bf16[4,80,2,1280]{3,2,1,0:T(2,128)(2,1)} custom-call(s32[1]{0:T(128)} %bitcast.band_ref, s32[1280]{0:T(1024)} %wave_ref.3, bf16[16,2,16,80]{3,2,1,0:T(8,128)(2,1)} %all_to_all.16.in_ref, bf16[80,32,1280]{2,1,0:T(8,128)(2,1)} %leg_hbm.3), custom_call_target="tpu_custom_call" | custom-call | tf_op jit(solution)/shard_map/analysis/pallas_call | solution.py:195
  (2 shorter events, 0.0 us)
Async XLA Ops:
  0.0 14.7 %copy-start.6 = (s32[1280]{0:T(1024)S(1)}, s32[1280]{0:T(1024)}, u32[]{:S(2)}) copy-start(s32[1280]{0:T(1024)} %wave_ref.3) | copy-start | bytes 15364
  0.0 14.7 %copy-start.3 = (s32[4,4,4]{2,1,0:T(4,128)S(1)}, s32[4,4,4]{2,1,0:T(4,128)}, u32[]{:S(2)}) copy-start(s32[4,4,4]{2,1,0:T(4,128)} %exp_ref.1) | copy-start | bytes 772
  0.0 14.8 %copy-start.4 = (s32[1,4]{1,0:T(1,128)S(1)}, s32[1,4]{1,0:T(1,128)}, u32[]{:S(2)}) copy-start(s32[1,4]{1,0:T(1,128)} %order_ref.1) | copy-start | bytes 52
  0.0 43.7 %copy-start.5 = (f32[4]{0:T(128)S(1)}, f32[4]{0:T(128)}, u32[]{:S(2)}) copy-start(f32[4]{0:T(128)} %coef_ref.1) | copy-start | bytes 52
  7.1 14.5 %all-to-all-start = ((bf16[16,2,16,80]{3,2,1,0:T(8,128)(2,1)}), bf16[16,2,16,80]{3,2,1,0:T(8,128)(2,1)S(1)}, u32[]{:S(2)}, u32[]{:S(2)}) async-start(bf16[16,2,16,80]{3,2,1,0:T(8,128)(2,1)} %synthesis.1), calls=%async_computation | async-start | bytes 262144 | tf_op jit(solution)/shard_map/all_to_all | solution.py:451
  14.8 0.9 %copy-start.2 = (bf16[4,4,5136]{2,1,0:T(4,128)(2,1)S(1)}, bf16[4,4,5136]{2,1,0:T(4,128)(2,1)}, u32[]{:S(2)}) copy-start(bf16[4,4,5136]{2,1,0:T(4,128)(2,1)} %traj_ref.1) | copy-start | bytes 493060
  18.9 0.7 %copy-start = (f32[128,656]{1,0:T(8,128)}, f32[128,656]{1,0:T(8,128)S(1)}, u32[]{:S(2)}) copy-start(f32[128,656]{1,0:T(8,128)S(1)} %get-tuple-element.18.gain_ref) | copy-start | bytes 1007620
  43.7 1.0 %copy-start.1 = (f32[128,656]{1,0:T(8,128)S(1)}, f32[128,656]{1,0:T(8,128)}, u32[]{:S(2)}) copy-start(f32[128,656]{1,0:T(8,128)} %copy-done) | copy-start | bytes 1007620

commit v6 on v5

--- a/solution.py
+++ b/solution.py
@@ -12,6 +12,8 @@
 F32, BF16, I32 = jnp.float32, jnp.bfloat16, jnp.int32
 GROUP = 8
 CHUNK = 2
+NBLK = 4
+LOW = 16
 
 
 def iota(shape, dim):
@@ -36,10 +38,84 @@
     return limit
 
 
+def turns(wave, b):
+    turn = (wave * b) & 3
+    cos_b = jnp.where(turn == 0, 1.0, jnp.where(turn == 2, -1.0, 0.0))
+    sin_b = jnp.where(turn == 1, 1.0, jnp.where(turn == 3, -1.0, 0.0))
+    return cos_b, sin_b
+
+
+def circle(product, lon_count):
+    quarter = lon_count // 4
+    count = jnp.floor(product * (1.0 / quarter) + 0.5)
+    angle = (product - count * quarter) * (2.0 * math.pi / lon_count)
+    turn = count.astype(I32) & 3
+    square = angle * angle
+    cos = 1.0 + square * (-1 / 2 + square * (1 / 24 + square * (-1 / 720 + square * (1 / 40320))))
+    sin = angle * (
+        1.0 + square * (-1 / 6 + square * (1 / 120 + square * (-1 / 5040 + square * (1 / 362880))))
+    )
+    swap = (turn & 1) == 1
+    near, far = jnp.where(swap, sin, cos), jnp.where(swap, cos, sin)
+    near = jnp.where((turn == 1) | (turn == 2), -near, near)
+    far = jnp.where(turn >= 2, -far, far)
+    return near, far
+
+
+def fill_tables(wave_ref, cos_ref, sin_ref, cos_high_ref, sin_high_ref, lons):
+    wave = wave_ref[...].astype(F32)
+    shape = (LOW, wave.shape[1])
+    cos_low, sin_low = circle(iota(shape, 0).astype(F32) * wave, lons)
+    shape = cos_high_ref.shape
+    cos_high_ref[...], sin_high_ref[...] = circle((iota(shape, 0) * LOW).astype(F32) * wave, lons)
+
+    @pl.loop(0, cos_ref.shape[0] // LOW)
+    def _(i):
+        cos_high = cos_high_ref[pl.ds(i, 1), :]
+        sin_high = sin_high_ref[pl.ds(i, 1), :]
+        at = pl.ds(pl.multiple_of(i * LOW, LOW), LOW)
+        cos_ref[at, :] = (cos_high * cos_low - sin_high * sin_low).astype(BF16)
+        sin_ref[at, :] = (-(sin_high * cos_low + cos_high * sin_low)).astype(BF16)
+
+
+def fill_gain(order_ref, exp_ref, traj_ref, gain_ref, norm):
+    levels, lats, lons = traj_ref.shape
+    width = lons // NBLK
+    sub = levels * lats
+    row, col = iota((sub, sub), 0), iota((sub, sub), 1)
+    held = jnp.zeros((sub, sub), I32)
+    for r in range(levels):
+        held = jnp.where(col // lats == r, order_ref[0, r], held)
+    lat = row // 4 % 2 * 2 + row // 8
+    pick = jnp.where((held == row % 4) & (col % lats == lat), 1.0, 0.0).astype(BF16)
+    power = jnp.concatenate([exp_ref[r] for r in range(levels)], axis=0).astype(F32)
+    scale = matmul(pick, jnp.exp2(power).astype(BF16), 1, 0)
+    stored = jnp.concatenate([traj_ref[r] for r in range(levels)], axis=0)
+    ordered = matmul(pick, stored, 1, 0)
+    full = gain_ref.shape[1]
+    ahead = iota((sub, full), 1)
+    reverse = jnp.where(iota((full, full), 0) + iota((full, full), 1) == full, 1.0, 0.0).astype(BF16)
+    for b in range(NBLK):
+        start = b * width
+        piece = ordered[:, start : start + full] * scale[:, b : b + 1]
+        gain = jnp.where(ahead <= width // 2, norm * (1.0 + jnp.tanh(piece)), 0.0)
+        gain_ref[b * sub : (b + 1) * sub, :] = gain
+        back = ordered[:, start + width - full : start + width].astype(BF16)
+        piece = matmul(back, reverse, 1, 0) * scale[:, b : b + 1]
+        gain = norm * (1.0 + jnp.tanh(piece))
+        gain = jnp.where((ahead >= 1) & (2 * ahead < width), gain, 0.0)
+        at = (NBLK + (b + 1) % NBLK) * sub
+        gain_ref[at : at + sub, :] = gain
+
+
 def synthesis_kernel(
-    band_ref, wave_ref, weight_ref, adj_hbm, leg_hbm, out_ref,
-    adj_ref, leg_ref, acc_ref, spread_ref, order_ref, adj_sem, leg_sem
+    band_ref, index_ref, wave_ref, held_ref, weight_ref, row_ref, exp_ref, traj_hbm, adj_hbm, leg_hbm,
+    out_ref, leg_ref, cos_ref, sin_ref, gain_ref,
+    adj_ref, traj_ref, acc_ref, spread_ref, order_ref, cos_high_ref, sin_high_ref,
+    adj_sem, leg_sem, traj_sem, *, norm
 ):
+    traj_fetch = pltpu.make_async_copy(traj_hbm, traj_ref, traj_sem)
+    traj_fetch.start()
     levels, slots, comps, degrees = adj_ref.shape
     rows = GROUP * comps
     heights = leg_ref.shape[1]
@@ -68,6 +144,9 @@
     degree = iota((rows, degrees), 1)
     sign = jnp.where(degree % 2 == 0, 1.0, -1.0).astype(BF16)
     lane = iota((rows, 128), 1) // heights
+    fill_tables(row_ref, cos_ref, sin_ref, cos_high_ref, sin_high_ref, traj_ref.shape[2])
+    traj_fetch.wait()
+    fill_gain(held_ref, exp_ref, traj_ref, gain_ref, norm)
     for first in range(0, steps, CHUNK):
         group = range(first, first + CHUNK)
         for g in group:
@@ -104,44 +183,52 @@
             out_ref[d, c] = moved[16 * d : 16 * d + 16, 128 * c : 128 * c + slots]
 
 
-def synthesis(adj, leg, band, waves, weight):
+def synthesis(adj, leg, band, index, waves, row, weight, order, exps, traj, norm):
     levels, slots, comps, degrees = adj.shape
     heights = leg.shape[1]
+    lats, lons = traj.shape[1:]
     size = 2 * levels * heights
+    count = waves.shape[0]
+    high = -(-(lons // NBLK // 2 + 1) // LOW)
+    table = jax.ShapeDtypeStruct((high * LOW, count), BF16)
     smem = pl.BlockSpec(memory_space=pltpu.SMEM)
     vmem = pl.BlockSpec(memory_space=pltpu.VMEM)
     hbm = pl.BlockSpec(memory_space=pltpu.HBM)
     return pl.pallas_call(
-        synthesis_kernel,
-        in_specs=[smem, smem, vmem, hbm, hbm],
-        out_specs=vmem,
-        out_shape=jax.ShapeDtypeStruct((16, comps, 16, slots), BF16),
+        functools.partial(synthesis_kernel, norm=norm),
+        in_specs=[smem] * 4 + [vmem] * 3 + [hbm] * 3,
+        out_specs=[vmem] * 5,
+        out_shape=(
+            jax.ShapeDtypeStruct((16, comps, 16, slots), BF16),
+            jax.ShapeDtypeStruct(leg.shape, BF16),
+            table,
+            table,
+            jax.ShapeDtypeStruct((2 * NBLK * levels * lats, high * LOW), F32),
+        ),
         scratch_shapes=[
             pltpu.VMEM(adj.shape, BF16),
-            pltpu.VMEM(leg.shape, BF16),
+            pltpu.VMEM(traj.shape, BF16),
             pltpu.VMEM((slots * comps, size), BF16),
             pltpu.VMEM((slots * comps, comps * 128), BF16),
             pltpu.VMEM((size, size), BF16),
+            pltpu.VMEM((-(-high // 8) * 8, count), F32),
+            pltpu.VMEM((-(-high // 8) * 8, count), F32),
             pltpu.SemaphoreType.DMA((slots // GROUP,)),
             pltpu.SemaphoreType.DMA((slots // GROUP,)),
+            pltpu.SemaphoreType.DMA,
         ],
-        compiler_params=pltpu.CompilerParams(vmem_limit_bytes=60 * 2**20),
+        compiler_params=pltpu.CompilerParams(vmem_limit_bytes=40_000_000),
         name="synthesis",
-    )(band, waves, weight[None, :], adj, leg)
-
-
-def analysis_kernel(band_ref, wave_ref, in_ref, leg_hbm, out_hbm, leg_ref, left_ref, out_ref, leg_sem, out_sem):
+    )(band, index, waves, order, weight, row, exps, traj, adj, leg)
+
+
+def analysis_kernel(band_ref, wave_ref, in_ref, leg_ref, out_hbm, left_ref, out_ref, out_sem):
     slots, heights, degrees = leg_ref.shape
     levels, _, comps, _ = out_ref.shape
     sources, _, sub, _ = in_ref.shape
     rows = GROUP * comps
     kinds = 2 * levels
     steps = slots // GROUP
-    fetches = []
-    for g in range(steps):
-        here = pl.ds(g * GROUP, GROUP)
-        fetches.append(pltpu.make_async_copy(leg_hbm.at[here], leg_ref.at[here], leg_sem.at[g]))
-        fetches[-1].start()
     size = sources * sub
     row = iota((size, kinds * 128), 0)
     col = iota((size, kinds * 128), 1)
@@ -168,7 +255,6 @@
         shape = left.shape
         own = (iota(shape, 0) % rows) // comps == iota(shape, 1) // heights
         left = left * jnp.where(own, 1.0, 0.0).astype(BF16)
-        fetches[g].wait()
         both = matmul(left, leg_ref[here].reshape(GROUP * heights, degrees), 1, 0)
         limit = limits(band_ref, wave_ref, g, slots, comps, degrees)
         degree = iota((rows, degrees), 1)
@@ -194,120 +280,20 @@
     shape = (levels, slots, comps, degrees)
     return pl.pallas_call(
         analysis_kernel,
-        in_specs=[smem, smem, vmem, hbm],
+        in_specs=[smem, smem, vmem, vmem],
         out_specs=hbm,
         out_shape=jax.ShapeDtypeStruct(shape, BF16),
         scratch_shapes=[
-            pltpu.VMEM(leg.shape, BF16),
             pltpu.VMEM((slots * comps, 2 * levels * 128), BF16),
             pltpu.VMEM(shape, BF16),
             pltpu.SemaphoreType.DMA((slots // GROUP,)),
-            pltpu.SemaphoreType.DMA((slots // GROUP,)),
         ],
-        compiler_params=pltpu.CompilerParams(vmem_limit_bytes=60 * 2**20),
+        compiler_params=pltpu.CompilerParams(vmem_limit_bytes=16 * 2**20),
         name="analysis",
     )(band, waves, sides, leg)
 
-NBLK = 4
-LOW = 16
-
-
-def turns(wave, b):
-    turn = (wave * b) & 3
-    cos_b = jnp.where(turn == 0, 1.0, jnp.where(turn == 2, -1.0, 0.0))
-    sin_b = jnp.where(turn == 1, 1.0, jnp.where(turn == 3, -1.0, 0.0))
-    return cos_b, sin_b
-
-
-def circle(product, lon_count):
-    quarter = lon_count // 4
-    count = jnp.floor(product * (1.0 / quarter) + 0.5)
-    angle = (product - count * quarter) * (2.0 * math.pi / lon_count)
-    turn = count.astype(I32) & 3
-    square = angle * angle
-    cos = 1.0 + square * (-1 / 2 + square * (1 / 24 + square * (-1 / 720 + square * (1 / 40320))))
-    sin = angle * (
-        1.0 + square * (-1 / 6 + square * (1 / 120 + square * (-1 / 5040 + square * (1 / 362880))))
-    )
-    swap = (turn & 1) == 1
-    near, far = jnp.where(swap, sin, cos), jnp.where(swap, cos, sin)
-    near = jnp.where((turn == 1) | (turn == 2), -near, near)
-    far = jnp.where(turn >= 2, -far, far)
-    return near, far
-
-
-def prepare_kernel(
-    order_ref, wave_ref, exp_ref, traj_ref, cos_ref, sin_ref, gain_hbm, token_ref,
-    cos_high_ref, sin_high_ref, gain_ref, gain_sem, *, norm
-):
-    levels, lats, lons = traj_ref.shape
-    width = lons // NBLK
-    wave = wave_ref[...].astype(F32)
-    shape = (LOW, wave.shape[1])
-    cos_low, sin_low = circle(iota(shape, 0).astype(F32) * wave, lons)
-    shape = cos_high_ref.shape
-    cos_high_ref[...], sin_high_ref[...] = circle((iota(shape, 0) * LOW).astype(F32) * wave, lons)
-
-    @pl.loop(0, cos_ref.shape[0] // LOW)
-    def _(i):
-        cos_high = cos_high_ref[pl.ds(i, 1), :]
-        sin_high = sin_high_ref[pl.ds(i, 1), :]
-        at = pl.ds(pl.multiple_of(i * LOW, LOW), LOW)
-        cos_ref[at, :] = (cos_high * cos_low - sin_high * sin_low).astype(BF16)
-        sin_ref[at, :] = (-(sin_high * cos_low + cos_high * sin_low)).astype(BF16)
-
-    sub = levels * lats
-    row, col = iota((sub, sub), 0), iota((sub, sub), 1)
-    held = jnp.zeros((sub, sub), I32)
-    for r in range(levels):
-        held = jnp.where(col // lats == r, order_ref[0, r], held)
-    lat = row // 4 % 2 * 2 + row // 8
-    pick = jnp.where((held == row % 4) & (col % lats == lat), 1.0, 0.0).astype(BF16)
-    power = jnp.concatenate([exp_ref[r] for r in range(levels)], axis=0).astype(F32)
-    scale = matmul(pick, jnp.exp2(power).astype(BF16), 1, 0)
-    stored = jnp.concatenate([traj_ref[r] for r in range(levels)], axis=0)
-    ordered = matmul(pick, stored, 1, 0)
-    full = cos_ref.shape[0]
-    ahead = iota((sub, full), 1)
-    reverse = jnp.where(iota((full, full), 0) + iota((full, full), 1) == full, 1.0, 0.0).astype(BF16)
-    for b in range(NBLK):
-        start = b * width
-        piece = ordered[:, start : start + full] * scale[:, b : b + 1]
-        gain = jnp.where(ahead <= width // 2, norm * (1.0 + jnp.tanh(piece)), 0.0)
-        gain_ref[b * sub : (b + 1) * sub, :] = gain
-        back = ordered[:, start + width - full : start + width].astype(BF16)
-        piece = matmul(back, reverse, 1, 0) * scale[:, b : b + 1]
-        gain = norm * (1.0 + jnp.tanh(piece))
-        gain = jnp.where((ahead >= 1) & (2 * ahead < width), gain, 0.0)
-        at = (NBLK + (b + 1) % NBLK) * sub
-        gain_ref[at : at + sub, :] = gain
-    send = pltpu.make_async_copy(gain_ref, gain_hbm, gain_sem)
-    send.start()
-    token_ref[...] = jnp.zeros(token_ref.shape, F32)
-    send.wait()
-
-
-def prepare(order, wave, exps, traj, norm):
-    levels, lats, lons = traj.shape
-    waves = wave.shape[1]
-    high = -(-(lons // NBLK // 2 + 1) // LOW)
-    table = jax.ShapeDtypeStruct((high * LOW, waves), BF16)
-    gain = jax.ShapeDtypeStruct((2 * NBLK * levels * lats, high * LOW), F32)
-    vmem = pl.BlockSpec(memory_space=pltpu.VMEM)
-    return pl.pallas_call(
-        functools.partial(prepare_kernel, norm=norm),
-        in_specs=[pl.BlockSpec(memory_space=pltpu.SMEM)] + [vmem] * 3,
-        out_specs=[vmem, vmem, pl.BlockSpec(memory_space=pltpu.HBM), vmem],
-        out_shape=(table, table, gain, jax.ShapeDtypeStruct((8, 128), F32)),
-        scratch_shapes=[pltpu.VMEM((-(-high // 8) * 8, waves), F32)] * 2
-        + [pltpu.VMEM(gain.shape, F32), pltpu.SemaphoreType.DMA],
-        compiler_params=pltpu.CompilerParams(vmem_limit_bytes=16 * 2**20),
-        cost_estimate=pl.CostEstimate(flops=12_000_000, bytes_accessed=20_000_000, transcendentals=0),
-        name="prepare",
-    )(order, wave, exps, traj)
-
-
-def gather_kernel(token_ref, in_ref, out_ref, total_ref):
+
+def gather_kernel(in_ref, out_ref, total_ref):
     sources, comps, sub, slots = in_ref.shape
     pick = one_hot(iota((8, comps * sub), 1) // 4, iota((8, comps * sub), 0))
     flat = [jnp.concatenate([in_ref[d, c] for d in range(sources)], axis=1) for c in range(comps)]
@@ -316,12 +302,12 @@
     total_ref[...] = matmul(pick, flat, 1, 0)
 
 
-def gather_rows(token, blocks):
+def gather_rows(blocks):
     sources, comps, sub, slots = blocks.shape
     vmem = pl.BlockSpec(memory_space=pltpu.VMEM)
     return pl.pallas_call(
         gather_kernel,
-        in_specs=[vmem] * 2,
+        in_specs=[vmem],
         out_specs=[vmem] * 2,
         out_shape=(
             jax.ShapeDtypeStruct((comps * sub, sources * slots), BF16),
@@ -329,7 +315,7 @@
         ),
         compiler_params=pltpu.CompilerParams(vmem_limit_bytes=8 * 2**20),
         name="gather_rows",
-    )(token, blocks)
+    )(blocks)
 
 
 def share_kernel(index_ref, pair_ref, share_ref, below_ref):
@@ -362,10 +348,8 @@
 
 def forcing_kernel(
     index_ref, coef_ref, total_ref, below_ref, four_ref, wave_ref, gain_ref, cos_ref, sin_ref,
-    out_ref, held_ref, held_sem, *, norm
+    out_ref, *, norm
 ):
-    fetch = pltpu.make_async_copy(gain_ref, held_ref, held_sem)
-    fetch.start()
     me = index_ref[0]
     groups = total_ref.shape[0]
     rows, waves = below_ref.shape
@@ -400,9 +384,8 @@
     even = matmul(with_cos, cos_ref[...], 1, 1)
     odd = matmul(with_sin, sin_ref[...], 1, 1)
     half = NBLK * sub
-    fetch.wait()
-    ahead = held_ref[:half, :] * (even + odd)
-    behind = held_ref[half:, :] * (even - odd)
+    ahead = gain_ref[:half, :] * (even + odd)
+    behind = gain_ref[half:, :] * (even - odd)
     forcing = jnp.concatenate([ahead, behind], axis=0).astype(BF16)
     by_cos = matmul(forcing, cos_ref[...], 1, 0)
     by_sin = matmul(forcing, sin_ref[...], 1, 0)
@@ -430,11 +413,10 @@
     smem = pl.BlockSpec(memory_space=pltpu.SMEM)
     return pl.pallas_call(
         functools.partial(forcing_kernel, norm=norm),
-        in_specs=[smem] * 2 + [vmem] * 4 + [pl.BlockSpec(memory_space=pltpu.HBM)] + [vmem] * 2,
+        in_specs=[smem] * 2 + [vmem] * 7,
         out_specs=vmem,
-        scratch_shapes=[pltpu.VMEM(gain.shape, F32), pltpu.SemaphoreType.DMA],
         out_shape=jax.ShapeDtypeStruct(shape, BF16),
-        compiler_params=pltpu.CompilerParams(vmem_limit_bytes=41_943_040),
+        compiler_params=pltpu.CompilerParams(vmem_limit_bytes=32 * 2**20),
         cost_estimate=pl.CostEstimate(flops=900_000_000, bytes_accessed=8_000_000, transcendentals=0),
         name="forcing_part",
     )(index, coef, totals, below, four, wave, gain, cos_t, sin_t)
@@ -447,10 +429,17 @@
     band = lax.axis_index("band").astype(I32)[None]
     index = lax.axis_index(("z", "core")).astype(I32)[None]
     wave = wave_of_slot[None, :]
-    blocks = synthesis(adj_spec, legendre, band, wave_of_slot, lat_weight)
+    adj_spec, table, traj, traj_exp, traj_order, lev_coef, wave_of_slot, weight = (
+        pltpu.with_memory_space_constraint(v, pltpu.HBM)
+        for v in (
+            adj_spec, legendre, traj, traj_exp, traj_order, lev_coef, wave_of_slot, lat_weight[None, :]
+        )
+    )
+    blocks, table, cos_t, sin_t, gain = synthesis(
+        adj_spec, table, band, index, wave_of_slot, wave, weight, traj_order, traj_exp, traj, norm
+    )
     blocks = lax.all_to_all(blocks, "band", split_axis=0, concat_axis=0, tiled=True)
-    cos_t, sin_t, gain, token = prepare(traj_order, wave, traj_exp, traj, norm)
-    four, total = gather_rows(token, blocks)
+    four, total = gather_rows(blocks)
     pair = lax.all_gather(total, "core")
     shares, below = share_rows(index, pair, groups)
     totals = lax.all_to_all(shares, ("z", "core"), split_axis=0, concat_axis=0, tiled=True)
@@ -458,7 +447,7 @@
         index, lev_coef, totals, below, four, wave, gain, cos_t, sin_t, blocks.shape, norm
     )
     sides = lax.all_to_all(sides, "band", split_axis=0, concat_axis=0, tiled=True)
-    return analysis(sides, legendre, band, wave_of_slot, levels)
+    return analysis(sides, table, band, wave_of_slot, levels)
 
 
 def solution(mesh):

time: 64.6 us -> 62.3 us (0.964)
  blocking collectives: 33 us -> 46.3 us
  starting transfers between devices: 7.59 us -> 0 us
  Pallas kernels: 18.9 us -> 15 us
  local copies, waits for them, and re-layouts: 2.67 us -> 0.7 us
  waiting for transfers between devices: 1.96 us -> 0 us
    all_to_all x0 -> x1, blocking collectives: none -> 14.3 us  [body(): lax.all_to_all(blocks, 'band', split_axis=0, concat_axis=0, tiled=True)]
    all_to_all x1 -> x0, starting transfers between devices: 7.59 us -> none  [body(): lax.all_to_all(blocks, 'band', split_axis=0, concat_axis=0, tiled=True)]
    pallas_call x4 -> x3, Pallas kernels: 16.1 us -> 12.3 us  [the longest x1 8.87 us: synthesis(): pl.pallas_call(functools.partial(synthesis_kernel, norm=norm), in_specs=[...]
    unnamed x14 -> x0, local copies, waits for them, and re-layouts: 2.66 us -> none
    all_to_all x1 -> x0, waiting for transfers between devices: 1.96 us -> none  [body(): lax.all_to_all(blocks, 'band', split_axis=0, concat_axis=0, tiled=True)]
    all_to_all x1, blocking collectives: 11.1 us -> 10.2 us  [body(): lax.all_to_all(sides, 'band', split_axis=0, concat_axis=0, tiled=True)]
    broadcast_in_dim x1, local copies, waits for them, and re-layouts: 0.01 us -> 0.7 us  [body(): wave = wave_of_slot[None, :]]
  transfers between devices with their start and end apart: 1 -> 0, of which waited for: 1 -> 0; matrix products, arithmetic and copies ran while one was open for 0% -> 0% of each run, Pallas kernels for 5% -> 0%
where the time goes in v6:
time: 62.3 us; the launch traced here: 61.9 us
  blocking collectives  46.3 us (74%)
  Pallas kernels  15 us (24%)
  local copies, waits for them, and re-layouts  0.7 us (1%)
    all_to_all x1, blocking collectives, body(): lax.all_to_all(shares, ('z', 'core'), split_axis=0, concat_axis=0, tiled=...  18.3 us
    all_to_all x1, blocking collectives, body(): lax.all_to_all(blocks, 'band', split_axis=0, concat_axis=0, tiled=True)  14.3 us
    all_to_all x1, blocking collectives, body(): lax.all_to_all(sides, 'band', split_axis=0, concat_axis=0, tiled=True)  10.2 us
    pallas_call x1, Pallas kernels, synthesis(): pl.pallas_call(functools.partial(synthesis_kernel, norm=norm), in_specs=[...  8.87 us
    all_gather x1, blocking collectives, body(): pair = lax.all_gather(total, 'core')  3.59 us
    pallas_call x1, Pallas kernels, analysis(): pl.pallas_call(analysis_kernel, in_specs=[smem, smem, vmem, vmem], out_sp...  3.24 us
    pallas_call x1, Pallas kernels, forcing_part(): pl.pallas_call(functools.partial(forcing_kernel, norm=norm), in_specs=[sm...  2.61 us

profile of v6, /device:TPU:1, one launch (start us, length us, event | category | flops | bytes accessed | tf_op | source)
XLA Modules:
  0.0 61.9 jit_solution(7167009085481300136)
XLA Ops:
  0.0 0.7 %broadcast_in_dim.15.row_ref.wave_ref = s32[1,1280]{1,0:T(1,128)S(1)} reshape(s32[1280]{0:T(1024)} %wave_ref.3) | data formatting | bytes 10240 | tf_op jit(solution)/shard_map/broadcast_in_dim | solution.py:431
  0.7 8.9 %synthesis.1 = (bf16[16,2,16,80]{3,2,1,0:T(8,128)(2,1)S(1)}, bf16[80,32,1280]{2,1,0:T(8,128)(2,1)S(1)}, bf16[656,1280]{1,0:T(8,128)(2,1)S(1)}, bf16[656,1280]{1,0:T(8,128)(2,1)S(1)}, f32[128,656]{1,0:T(8,128)S(1)}) custom-call(s32[1]{0:T(128)} %bitcast.band_ref, s32[1]{0:T(128)} %bitcast.1.index_ref, s32[1280]{0:T(1024)} %wave_ref.3, s32[1,4]{1,0:T(1,128)} %held_ref.1, ...), custom_call_target="tpu_custom_call" | custom-call | tf_op jit(solution)/shard_map/synthesis/pallas_call | solution.py:197
  9.6 14.3 %all_to_all.15.in_ref = bf16[16,2,16,80]{3,2,1,0:T(8,128)(2,1)S(1)} all-to-all(bf16[16,2,16,80]{3,2,1,0:T(8,128)(2,1)S(1)} %get-tuple-element.14), channel_id=1, replica_groups=mesh['band'=16,'z'=8,'core'=2] {'band'}, dimensions={0} | all-to-all | bytes 163840 | tf_op jit(solution)/shard_map/all_to_all | solution.py:441
  23.8 0.2 gather_rows.1
  24.0 3.6 %all-gather = f32[16,1280]{1,0:T(8,128)S(1)} all-gather(f32[8,1280]{1,0:T(8,128)S(1)} %get-tuple-element.15), channel_id=2, replica_groups=mesh['band'=16,'z'=8,'core'=2] {'core'}, dimensions={0}, use_global_device_ids=true | all-gather | bytes 122880 | tf_op jit(solution)/shard_map/all_gather | solution.py:443
  27.7 18.3 %all_to_all.16.total_ref = bf16[16,8,640]{2,1,0:T(8,128)(2,1)S(1)} all-to-all(bf16[16,8,640]{2,1,0:T(8,128)(2,1)S(1)} %get-tuple-element.16), channel_id=1, replica_groups=mesh['band'=16,'z'=8,'core'=2] {'z','core'}, dimensions={0} | all-to-all | bytes 327680 | tf_op jit(solution)/shard_map/all_to_all | solution.py:445
  45.9 2.6 %forcing_part.1 = bf16[16,2,16,80]{3,2,1,0:T(8,128)(2,1)S(1)} custom-call(s32[1]{0:T(128)} %bitcast.1.index_ref, f32[4]{0:T(128)} %coef_ref.1, bf16[16,8,640]{2,1,0:T(8,128)(2,1)S(1)} %all_to_all.16.total_ref, f32[8,1280]{1,0:T(8,128)S(1)} %get-tuple-element.17.below_ref, bf16[32,1280]{1,0:T(8,128)(2,1)S(1)} %get-tuple-element.18.four_ref, ...), custom_call_target="tpu_custom_call" | custom-call | flops 900000000 | bytes 8000000 | tf_op jit(solution)/shard_map/forcing_part/pallas_call | solution.py:414
  48.6 10.2 %all_to_all.17.in_ref = bf16[16,2,16,80]{3,2,1,0:T(8,128)(2,1)S(1)} all-to-all(bf16[16,2,16,80]{3,2,1,0:T(8,128)(2,1)S(1)} %forcing_part.1), channel_id=1, replica_groups=mesh['band'=16,'z'=8,'core'=2] {'band'}, dimensions={0} | all-to-all | bytes 163840 | tf_op jit(solution)/shard_map/all_to_all | solution.py:449
  58.7 3.2 %analysis.1 = bf16[4,80,2,1280]{3,2,1,0:T(2,128)(2,1)} custom-call(s32[1]{0:T(128)} %bitcast.band_ref, s32[1280]{0:T(1024)} %wave_ref.3, bf16[16,2,16,80]{3,2,1,0:T(8,128)(2,1)S(1)} %all_to_all.17.in_ref, bf16[80,32,1280]{2,1,0:T(8,128)(2,1)S(1)} %get-tuple-element.22.leg_ref), custom_call_target="tpu_custom_call" | custom-call | tf_op jit(solution)/shard_map/analysis/pallas_call | solution.py:281
  (1 shorter events, 0.0 us)

commit v7 on v6

--- a/solution.py
+++ b/solution.py
@@ -11,7 +11,7 @@
 
 F32, BF16, I32 = jnp.float32, jnp.bfloat16, jnp.int32
 GROUP = 8
-CHUNK = 2
+CHUNK = 10
 NBLK = 4
 LOW = 16
 
@@ -63,7 +63,7 @@
 
 
 def fill_tables(wave_ref, cos_ref, sin_ref, cos_high_ref, sin_high_ref, lons):
-    wave = wave_ref[...].astype(F32)
+    wave = wave_ref[...][None, :].astype(F32)
     shape = (LOW, wave.shape[1])
     cos_low, sin_low = circle(iota(shape, 0).astype(F32) * wave, lons)
     shape = cos_high_ref.shape
@@ -95,13 +95,14 @@
     full = gain_ref.shape[1]
     ahead = iota((sub, full), 1)
     reverse = jnp.where(iota((full, full), 0) + iota((full, full), 1) == full, 1.0, 0.0).astype(BF16)
+    back = [ordered[:, (b + 1) * width - full : (b + 1) * width] for b in range(NBLK)]
+    back = matmul(jnp.concatenate(back, axis=0).astype(BF16), reverse, 1, 0)
     for b in range(NBLK):
         start = b * width
         piece = ordered[:, start : start + full] * scale[:, b : b + 1]
         gain = jnp.where(ahead <= width // 2, norm * (1.0 + jnp.tanh(piece)), 0.0)
         gain_ref[b * sub : (b + 1) * sub, :] = gain
-        back = ordered[:, start + width - full : start + width].astype(BF16)
-        piece = matmul(back, reverse, 1, 0) * scale[:, b : b + 1]
+        piece = back[b * sub : (b + 1) * sub] * scale[:, b : b + 1]
         gain = norm * (1.0 + jnp.tanh(piece))
         gain = jnp.where((ahead >= 1) & (2 * ahead < width), gain, 0.0)
         at = (NBLK + (b + 1) % NBLK) * sub
@@ -183,7 +184,7 @@
             out_ref[d, c] = moved[16 * d : 16 * d + 16, 128 * c : 128 * c + slots]
 
 
-def synthesis(adj, leg, band, index, waves, row, weight, order, exps, traj, norm):
+def synthesis(adj, leg, band, index, waves, weight, order, exps, traj, norm):
     levels, slots, comps, degrees = adj.shape
     heights = leg.shape[1]
     lats, lons = traj.shape[1:]
@@ -219,7 +220,7 @@
         ],
         compiler_params=pltpu.CompilerParams(vmem_limit_bytes=40_000_000),
         name="synthesis",
-    )(band, index, waves, order, weight, row, exps, traj, adj, leg)
+    )(band, index, waves, order, weight, waves, exps, traj, adj, leg)
 
 
 def analysis_kernel(band_ref, wave_ref, in_ref, leg_ref, out_hbm, left_ref, out_ref, out_sem):
@@ -355,7 +356,7 @@
     rows, waves = below_ref.shape
     both = four_ref.shape[0]
     sub = both // 2
-    wave = wave_ref[...]
+    wave = wave_ref[...][None, :]
     parts = []
     for c in range(2):
         part = jnp.zeros(total_ref.shape[1:], F32)
@@ -428,7 +429,6 @@
     norm = 1.0 / math.sqrt(degrees)
     band = lax.axis_index("band").astype(I32)[None]
     index = lax.axis_index(("z", "core")).astype(I32)[None]
-    wave = wave_of_slot[None, :]
     adj_spec, table, traj, traj_exp, traj_order, lev_coef, wave_of_slot, weight = (
         pltpu.with_memory_space_constraint(v, pltpu.HBM)
         for v in (
@@ -436,7 +436,7 @@
         )
     )
     blocks, table, cos_t, sin_t, gain = synthesis(
-        adj_spec, table, band, index, wave_of_slot, wave, weight, traj_order, traj_exp, traj, norm
+        adj_spec, table, band, index, wave_of_slot, weight, traj_order, traj_exp, traj, norm
     )
     blocks = lax.all_to_all(blocks, "band", split_axis=0, concat_axis=0, tiled=True)
     four, total = gather_rows(blocks)
@@ -444,7 +444,7 @@
     shares, below = share_rows(index, pair, groups)
     totals = lax.all_to_all(shares, ("z", "core"), split_axis=0, concat_axis=0, tiled=True)
     sides = forcing_part(
-        index, lev_coef, totals, below, four, wave, gain, cos_t, sin_t, blocks.shape, norm
+        index, lev_coef, totals, below, four, wave_of_slot, gain, cos_t, sin_t, blocks.shape, norm
     )
     sides = lax.all_to_all(sides, "band", split_axis=0, concat_axis=0, tiled=True)
     return analysis(sides, table, band, wave_of_slot, levels)

time: 62.3 us -> 60.3 us (0.968)
  Pallas kernels: 15 us -> 13.7 us
  local copies, waits for them, and re-layouts: 0.7 us -> 0 us
    pallas_call x1, Pallas kernels: 8.87 us -> 7.7 us  [synthesis(): pl.pallas_call(functools.partial(synthesis_kernel, norm=norm), in_specs=[...]
    broadcast_in_dim x1 -> x0, local copies, waits for them, and re-layouts: 0.7 us -> none  [body(): wave = wave_of_slot[None, :]]
where the time goes in v7:
time: 60.3 us; the launch traced here: 60 us
  blocking collectives  46.2 us (77%)
  Pallas kernels  13.7 us (23%)
    all_to_all x1, blocking collectives, body(): lax.all_to_all(shares, ('z', 'core'), split_axis=0, concat_axis=0, tiled=...  18.3 us
    all_to_all x1, blocking collectives, body(): lax.all_to_all(blocks, 'band', split_axis=0, concat_axis=0, tiled=True)  14.3 us
    all_to_all x1, blocking collectives, body(): lax.all_to_all(sides, 'band', split_axis=0, concat_axis=0, tiled=True)  10.1 us
    pallas_call x1, Pallas kernels, synthesis(): pl.pallas_call(functools.partial(synthesis_kernel, norm=norm), in_specs=[...  7.7 us
    all_gather x1, blocking collectives, body(): pair = lax.all_gather(total, 'core')  3.59 us
    pallas_call x1, Pallas kernels, analysis(): pl.pallas_call(analysis_kernel, in_specs=[smem, smem, vmem, vmem], out_sp...  3.1 us
    pallas_call x1, Pallas kernels, forcing_part(): pl.pallas_call(functools.partial(forcing_kernel, norm=norm), in_specs=[sm...  2.65 us

profile of v7, /device:TPU:1, one launch (start us, length us, event | category | flops | bytes accessed | tf_op | source)
XLA Modules:
  0.0 60.0 jit_solution(2344130500118173625)
XLA Ops:
  0.0 7.7 %synthesis.1 = (bf16[16,2,16,80]{3,2,1,0:T(8,128)(2,1)S(1)}, bf16[80,32,1280]{2,1,0:T(8,128)(2,1)S(1)}, bf16[656,1280]{1,0:T(8,128)(2,1)S(1)}, bf16[656,1280]{1,0:T(8,128)(2,1)S(1)}, f32[128,656]{1,0:T(8,128)S(1)}) custom-call(s32[1]{0:T(128)} %bitcast.band_ref, s32[1]{0:T(128)} %bitcast.1.index_ref, s32[1280]{0:T(1024)} %wave_ref.5, s32[1,4]{1,0:T(1,128)} %held_ref.1, ...), custom_call_target="tpu_custom_call" | custom-call | tf_op jit(solution)/shard_map/synthesis/pallas_call | solution.py:198
  7.7 14.3 %all_to_all.15.in_ref = bf16[16,2,16,80]{3,2,1,0:T(8,128)(2,1)S(1)} all-to-all(bf16[16,2,16,80]{3,2,1,0:T(8,128)(2,1)S(1)} %get-tuple-element.14), channel_id=1, replica_groups=mesh['band'=16,'z'=8,'core'=2] {'band'}, dimensions={0} | all-to-all | bytes 163840 | tf_op jit(solution)/shard_map/all_to_all | solution.py:441
  22.0 0.2 gather_rows.1
  22.2 3.6 %all-gather = f32[16,1280]{1,0:T(8,128)S(1)} all-gather(f32[8,1280]{1,0:T(8,128)S(1)} %get-tuple-element.15), channel_id=2, replica_groups=mesh['band'=16,'z'=8,'core'=2] {'core'}, dimensions={0}, use_global_device_ids=true | all-gather | bytes 122880 | tf_op jit(solution)/shard_map/all_gather | solution.py:443
  25.8 18.3 %all_to_all.16.total_ref = bf16[16,8,640]{2,1,0:T(8,128)(2,1)S(1)} all-to-all(bf16[16,8,640]{2,1,0:T(8,128)(2,1)S(1)} %get-tuple-element.16), channel_id=1, replica_groups=mesh['band'=16,'z'=8,'core'=2] {'z','core'}, dimensions={0} | all-to-all | bytes 327680 | tf_op jit(solution)/shard_map/all_to_all | solution.py:445
  44.1 2.6 %forcing_part.1 = bf16[16,2,16,80]{3,2,1,0:T(8,128)(2,1)S(1)} custom-call(s32[1]{0:T(128)} %bitcast.1.index_ref, f32[4]{0:T(128)} %coef_ref.1, bf16[16,8,640]{2,1,0:T(8,128)(2,1)S(1)} %all_to_all.16.total_ref, f32[8,1280]{1,0:T(8,128)S(1)} %get-tuple-element.17.below_ref, bf16[32,1280]{1,0:T(8,128)(2,1)S(1)} %get-tuple-element.18.four_ref, s32[1280]{0:T(1024)} %wave_ref.5, ...), custom_call_target="tpu_custom_call" | custom-call | flops 900000000 | bytes 8000000 | tf_op jit(solution)/shard_map/forcing_part/pallas_call | solution.py:415
  46.7 10.1 %all_to_all.17.in_ref = bf16[16,2,16,80]{3,2,1,0:T(8,128)(2,1)S(1)} all-to-all(bf16[16,2,16,80]{3,2,1,0:T(8,128)(2,1)S(1)} %forcing_part.1), channel_id=1, replica_groups=mesh['band'=16,'z'=8,'core'=2] {'band'}, dimensions={0} | all-to-all | bytes 163840 | tf_op jit(solution)/shard_map/all_to_all | solution.py:449
  56.8 3.1 %analysis.1 = bf16[4,80,2,1280]{3,2,1,0:T(2,128)(2,1)} custom-call(s32[1]{0:T(128)} %bitcast.band_ref, s32[1280]{0:T(1024)} %wave_ref.5, bf16[16,2,16,80]{3,2,1,0:T(8,128)(2,1)S(1)} %all_to_all.17.in_ref, bf16[80,32,1280]{2,1,0:T(8,128)(2,1)S(1)} %get-tuple-element.22.leg_ref), custom_call_target="tpu_custom_call" | custom-call | tf_op jit(solution)/shard_map/analysis/pallas_call | solution.py:282
  (1 shorter events, 0.0 us)

commit v8 on v7

--- a/solution.py
+++ b/solution.py
@@ -11,7 +11,7 @@
 
 F32, BF16, I32 = jnp.float32, jnp.bfloat16, jnp.int32
 GROUP = 8
-CHUNK = 10
+CUTS = (0, 10)
 NBLK = 4
 LOW = 16
 
@@ -111,7 +111,7 @@
 
 def synthesis_kernel(
     band_ref, index_ref, wave_ref, held_ref, weight_ref, row_ref, exp_ref, traj_hbm, adj_hbm, leg_hbm,
-    out_ref, leg_ref, cos_ref, sin_ref, gain_ref,
+    out_ref, leg_ref, cos_ref, sin_ref, gain_ref, pick_ref, weave_ref,
     adj_ref, traj_ref, acc_ref, spread_ref, order_ref, cos_high_ref, sin_high_ref,
     adj_sem, leg_sem, traj_sem, *, norm
 ):
@@ -136,6 +136,11 @@
     slot = col % 128
     own = (source == slot * comps + col // 128) & (slot < slots)
     spread_ref[...] = jnp.where(own, 1.0, 0.0).astype(BF16)
+    row, col = iota(pick_ref.shape, 0), iota(pick_ref.shape, 1)
+    row = (row // 8 % 2 * levels + row % 4) * heights + row // 16 * 2 + row // 4 % 2
+    pick_ref[...] = one_hot(row, col // 128 * heights + col % heights)
+    row, col = iota(weave_ref.shape, 0), iota(weave_ref.shape, 1)
+    weave_ref[...] = one_hot(row % comps * slots + row // comps, col)
     size = 2 * levels * heights
     dest, origin = iota((size, size), 1), iota((size, size), 0)
     band, e, hh, l = dest // 16, dest // 8 % 2, dest // 4 % 2, dest % 4
@@ -148,8 +153,8 @@
     fill_tables(row_ref, cos_ref, sin_ref, cos_high_ref, sin_high_ref, traj_ref.shape[2])
     traj_fetch.wait()
     fill_gain(held_ref, exp_ref, traj_ref, gain_ref, norm)
-    for first in range(0, steps, CHUNK):
-        group = range(first, first + CHUNK)
+    for first, last in zip(CUTS, CUTS[1:]):
+        group = range(first, last)
         for g in group:
             for fetch in fetches[g]:
                 fetch.wait()
@@ -176,7 +181,7 @@
                     mix = jnp.where(lane == r, part, mix)
                 blocks.append(mix.astype(BF16))
             wide.append(jnp.concatenate(blocks, axis=1))
-        acc_ref[first * rows : (first + CHUNK) * rows, :] = jnp.concatenate(wide, axis=0)
+        acc_ref[first * rows : last * rows, :] = jnp.concatenate(wide, axis=0)
     wide = matmul(acc_ref[...], order_ref[...], 1, 0).astype(BF16)
     moved = matmul(wide, spread_ref[...], 0, 0).astype(BF16)
     for d in range(size // 16):
@@ -198,13 +203,15 @@
     return pl.pallas_call(
         functools.partial(synthesis_kernel, norm=norm),
         in_specs=[smem] * 4 + [vmem] * 3 + [hbm] * 3,
-        out_specs=[vmem] * 5,
+        out_specs=[vmem] * 7,
         out_shape=(
             jax.ShapeDtypeStruct((16, comps, 16, slots), BF16),
             jax.ShapeDtypeStruct(leg.shape, BF16),
             table,
             table,
             jax.ShapeDtypeStruct((2 * NBLK * levels * lats, high * LOW), F32),
+            jax.ShapeDtypeStruct((16 * 16, 2 * levels * 128), BF16),
+            jax.ShapeDtypeStruct((slots * comps, slots * comps), BF16),
         ),
         scratch_shapes=[
             pltpu.VMEM(adj.shape, BF16),
@@ -223,29 +230,21 @@
     )(band, index, waves, order, weight, waves, exps, traj, adj, leg)
 
 
-def analysis_kernel(band_ref, wave_ref, in_ref, leg_ref, out_hbm, left_ref, out_ref, out_sem):
+def analysis_kernel(
+    band_ref, wave_ref, in_ref, pick_ref, weave_ref, leg_ref, out_hbm, left_ref, out_ref, out_sem
+):
     slots, heights, degrees = leg_ref.shape
     levels, _, comps, _ = out_ref.shape
     sources, _, sub, _ = in_ref.shape
     rows = GROUP * comps
     kinds = 2 * levels
     steps = slots // GROUP
-    size = sources * sub
-    row = iota((size, kinds * 128), 0)
-    col = iota((size, kinds * 128), 1)
-    row_key = (row // 8 % 2 * levels + row % 4) * heights + row // 16 * 2 + row // 4 % 2
-    pick = one_hot(row_key, col // 128 * heights + col % heights)
     parts = []
     for c in range(comps):
         flat = jnp.concatenate([in_ref[d, c] for d in range(sources)], axis=0)
-        parts.append(matmul(flat, pick, 0, 0).astype(BF16))
+        parts.append(matmul(flat, pick_ref[...], 0, 0).astype(BF16))
     apart = jnp.concatenate(parts, axis=0)
-    total = slots * comps
-    weave = one_hot(
-        iota((total, total), 0) % comps * slots + iota((total, total), 0) // comps,
-        iota((total, total), 1),
-    )
-    left_ref[...] = matmul(weave, apart, 1, 0).astype(BF16)
+    left_ref[...] = matmul(weave_ref[...], apart, 1, 0).astype(BF16)
     half = levels * rows
     sends = []
     for g in range(steps):
@@ -272,7 +271,7 @@
         send.wait()
 
 
-def analysis(sides, leg, band, waves, levels):
+def analysis(sides, pick, weave, leg, band, waves, levels):
     sources, comps, sub, slots = sides.shape
     heights, degrees = leg.shape[1:]
     smem = pl.BlockSpec(memory_space=pltpu.SMEM)
@@ -281,7 +280,7 @@
     shape = (levels, slots, comps, degrees)
     return pl.pallas_call(
         analysis_kernel,
-        in_specs=[smem, smem, vmem, vmem],
+        in_specs=[smem, smem] + [vmem] * 4,
         out_specs=hbm,
         out_shape=jax.ShapeDtypeStruct(shape, BF16),
         scratch_shapes=[
@@ -291,19 +290,21 @@
         ],
         compiler_params=pltpu.CompilerParams(vmem_limit_bytes=16 * 2**20),
         name="analysis",
-    )(band, waves, sides, leg)
-
-
-def gather_kernel(in_ref, out_ref, total_ref):
+    )(band, waves, sides, pick, weave, leg)
+
+
+def gather_kernel(in_ref, out_ref, share_ref):
     sources, comps, sub, slots = in_ref.shape
     pick = one_hot(iota((8, comps * sub), 1) // 4, iota((8, comps * sub), 0))
     flat = [jnp.concatenate([in_ref[d, c] for d in range(sources)], axis=1) for c in range(comps)]
     flat = jnp.concatenate(flat, axis=0)
     out_ref[...] = flat
-    total_ref[...] = matmul(pick, flat, 1, 0)
-
-
-def gather_rows(blocks):
+    total = matmul(pick, flat, 1, 0).astype(BF16)
+    for d in range(share_ref.shape[0]):
+        share_ref[d] = total
+
+
+def gather_rows(blocks, groups):
     sources, comps, sub, slots = blocks.shape
     vmem = pl.BlockSpec(memory_space=pltpu.VMEM)
     return pl.pallas_call(
@@ -312,58 +313,25 @@
         out_specs=[vmem] * 2,
         out_shape=(
             jax.ShapeDtypeStruct((comps * sub, sources * slots), BF16),
-            jax.ShapeDtypeStruct((comps * sub // 4, sources * slots), F32),
+            jax.ShapeDtypeStruct((groups, comps * sub // 4, sources * slots), BF16),
         ),
         compiler_params=pltpu.CompilerParams(vmem_limit_bytes=8 * 2**20),
         name="gather_rows",
     )(blocks)
 
 
-def share_kernel(index_ref, pair_ref, share_ref, below_ref):
-    core = index_ref[0] % 2
-    chip = pair_ref[0] + pair_ref[1]
-    below_ref[...] = pair_ref[1 - core]
-    rows, waves = chip.shape
-    half = waves // 2
-    chip = jnp.where(core == 0, chip[: rows // 2], chip[rows // 2 :])
-    share = jnp.concatenate([chip[:, :half], chip[:, half:]], axis=0).astype(BF16)
-    for d in range(share_ref.shape[0]):
-        share_ref[d] = share
-
-
-def share_rows(index, pair, groups):
-    _, rows, waves = pair.shape
-    vmem = pl.BlockSpec(memory_space=pltpu.VMEM)
-    return pl.pallas_call(
-        share_kernel,
-        in_specs=[pl.BlockSpec(memory_space=pltpu.SMEM), vmem],
-        out_specs=[vmem] * 2,
-        out_shape=(
-            jax.ShapeDtypeStruct((groups, rows, waves // 2), BF16),
-            jax.ShapeDtypeStruct((rows, waves), F32),
-        ),
-        compiler_params=pltpu.CompilerParams(vmem_limit_bytes=8 * 2**20),
-        name="share_rows",
-    )(index, pair)
-
-
 def forcing_kernel(
-    index_ref, coef_ref, total_ref, below_ref, four_ref, wave_ref, gain_ref, cos_ref, sin_ref,
+    index_ref, coef_ref, total_ref, four_ref, wave_ref, gain_ref, cos_ref, sin_ref,
     out_ref, *, norm
 ):
     me = index_ref[0]
-    groups = total_ref.shape[0]
-    rows, waves = below_ref.shape
+    groups, rows, waves = total_ref.shape
     both = four_ref.shape[0]
     sub = both // 2
     wave = wave_ref[...][None, :]
-    parts = []
-    for c in range(2):
-        part = jnp.zeros(total_ref.shape[1:], F32)
-        for z in range(groups // 2):
-            part = part + jnp.where(z < me // 2, total_ref[2 * z + c].astype(F32), 0.0)
-        parts.append(jnp.concatenate([part[: rows // 2], part[rows // 2 :]], axis=1))
-    carry = jnp.concatenate(parts, axis=0) + jnp.where(me % 2 == 1, below_ref[...], 0.0)
+    carry = jnp.zeros((rows, waves), F32)
+    for g in range(groups):
+        carry = carry + jnp.where(g < me, total_ref[g].astype(F32), 0.0)
     four = four_ref[...]
     row, col = iota((both, both), 0), iota((both, both), 1)
     earlier = jnp.where((row // 4 == col // 4) & (col < row), 1.0, 0.0).astype(BF16)
@@ -409,18 +377,18 @@
             out_ref[d, c] = sides[:, slots * d : slots * (d + 1)]
 
 
-def forcing_part(index, coef, totals, below, four, wave, gain, cos_t, sin_t, shape, norm):
+def forcing_part(index, coef, totals, four, wave, gain, cos_t, sin_t, shape, norm):
     vmem = pl.BlockSpec(memory_space=pltpu.VMEM)
     smem = pl.BlockSpec(memory_space=pltpu.SMEM)
     return pl.pallas_call(
         functools.partial(forcing_kernel, norm=norm),
-        in_specs=[smem] * 2 + [vmem] * 7,
+        in_specs=[smem] * 2 + [vmem] * 6,
         out_specs=vmem,
         out_shape=jax.ShapeDtypeStruct(shape, BF16),
         compiler_params=pltpu.CompilerParams(vmem_limit_bytes=32 * 2**20),
         cost_estimate=pl.CostEstimate(flops=900_000_000, bytes_accessed=8_000_000, transcendentals=0),
         name="forcing_part",
-    )(index, coef, totals, below, four, wave, gain, cos_t, sin_t)
+    )(index, coef, totals, four, wave, gain, cos_t, sin_t)
 
 
 def body(adj_spec, wave_of_slot, legendre, lat_weight, traj, traj_exp, traj_order, lev_coef):
@@ -435,19 +403,17 @@
             adj_spec, legendre, traj, traj_exp, traj_order, lev_coef, wave_of_slot, lat_weight[None, :]
         )
     )
-    blocks, table, cos_t, sin_t, gain = synthesis(
+    blocks, table, cos_t, sin_t, gain, pick, weave = synthesis(
         adj_spec, table, band, index, wave_of_slot, weight, traj_order, traj_exp, traj, norm
     )
     blocks = lax.all_to_all(blocks, "band", split_axis=0, concat_axis=0, tiled=True)
-    four, total = gather_rows(blocks)
-    pair = lax.all_gather(total, "core")
-    shares, below = share_rows(index, pair, groups)
+    four, shares = gather_rows(blocks, groups)
     totals = lax.all_to_all(shares, ("z", "core"), split_axis=0, concat_axis=0, tiled=True)
     sides = forcing_part(
-        index, lev_coef, totals, below, four, wave_of_slot, gain, cos_t, sin_t, blocks.shape, norm
+        index, lev_coef, totals, four, wave_of_slot, gain, cos_t, sin_t, blocks.shape, norm
     )
     sides = lax.all_to_all(sides, "band", split_axis=0, concat_axis=0, tiled=True)
-    return analysis(sides, table, band, wave_of_slot, levels)
+    return analysis(sides, pick, weave, table, band, wave_of_slot, levels)
 
 
 def solution(mesh):

time: 60.3 us -> 61.9 us (1.027)
  blocking collectives: 46.2 us -> 48 us
    all_to_all x1, blocking collectives: 18.3 us -> 23.4 us  [body(): lax.all_to_all(shares, ('z', 'core'), split_axis=0, concat_axis=0, tiled=...]
    all_gather x1 -> x0, blocking collectives: 3.59 us -> none  [body(): pair = lax.all_gather(total, 'core')]
    pallas_call x2 -> x1, Pallas kernels: 3.13 us -> 3.07 us  [analysis(): pl.pallas_call(analysis_kernel, in_specs=[smem, smem] + [vmem] * 4, out_s...]
where the time goes in v8:
time: 61.9 us; the launch traced here: 61.6 us
  blocking collectives  48 us (78%)
  Pallas kernels  13.6 us (22%)
    all_to_all x1, blocking collectives, body(): lax.all_to_all(shares, ('z', 'core'), split_axis=0, concat_axis=0, tiled=...  23.4 us
    all_to_all x1, blocking collectives, body(): lax.all_to_all(blocks, 'band', split_axis=0, concat_axis=0, tiled=True)  14.3 us
    all_to_all x1, blocking collectives, body(): lax.all_to_all(sides, 'band', split_axis=0, concat_axis=0, tiled=True)  10.3 us
    pallas_call x1, Pallas kernels, synthesis(): pl.pallas_call(functools.partial(synthesis_kernel, norm=norm), in_specs=[...  7.69 us
    pallas_call x1, Pallas kernels, analysis(): pl.pallas_call(analysis_kernel, in_specs=[smem, smem] + [vmem] * 4, out_s...  3.07 us
    pallas_call x1, Pallas kernels, forcing_part(): pl.pallas_call(functools.partial(forcing_kernel, norm=norm), in_specs=[sm...  2.65 us

profile of v8, /device:TPU:1, one launch (start us, length us, event | category | flops | bytes accessed | tf_op | source)
XLA Modules:
  0.0 61.6 jit_solution(9019174446547461212)
XLA Ops:
  0.0 7.7 %synthesis.1 = (bf16[16,2,16,80]{3,2,1,0:T(8,128)(2,1)S(1)}, bf16[80,32,1280]{2,1,0:T(8,128)(2,1)S(1)}, bf16[656,1280]{1,0:T(8,128)(2,1)S(1)}, bf16[656,1280]{1,...) custom-call(s32[1]{0:T(128)} %bitcast.band_ref, ...), custom_call_target="tpu_custom_call" | custom-call | tf_op jit(solution)/shard_map/synthesis/pallas_call | solution.py:203
  7.7 14.3 %all_to_all.15.in_ref = bf16[16,2,16,80]{3,2,1,0:T(8,128)(2,1)S(1)} all-to-all(bf16[16,2,16,80]{3,2,1,0:T(8,128)(2,1)S(1)} %get-tuple-element.14), channel_id=1, replica_groups=mesh['band'=16,'z'=8,'core'=2] {'band'}, dimensions={0} | all-to-all | bytes 163840 | tf_op jit(solution)/shard_map/all_to_all | solution.py:409
  22.0 0.2 gather_rows.1
  22.2 23.4 %all_to_all.16.total_ref = bf16[16,8,1280]{2,1,0:T(8,128)(2,1)S(1)} all-to-all(bf16[16,8,1280]{2,1,0:T(8,128)(2,1)S(1)} %get-tuple-element.15), channel_id=1, replica_groups=mesh['band'=16,'z'=8,'core'=2] {'z','core'}, dimensions={0} | all-to-all | bytes 655360 | tf_op jit(solution)/shard_map/all_to_all | solution.py:411
  45.6 2.7 %forcing_part.1 = bf16[16,2,16,80]{3,2,1,0:T(8,128)(2,1)S(1)} custom-call(s32[1]{0:T(128)} %bitcast.1.index_ref, f32[4]{0:T(128)} %coef_ref.1, bf16[16,8,1280]{2,1,0:T(8,128)(2,1)S(1)} %all_to_all.16.total_ref, bf16[32,1280]{1,0:T(8,128)(2,1)S(1)} %get-tuple-element.16.four_ref, s32[1280]{0:T(1024)} %wave_ref.5, f32[128,656]{1,0:T(8,128)S(1)} %get-tuple-element.17.gain_ref, ...), custom_call_target="tpu_custom_call" | custom-call | flops 900000000 | bytes 8000000 | tf_op jit(solution)/shard_map/forcing_part/pallas_call | solution.py:383
  48.3 10.3 %all_to_all.17.in_ref = bf16[16,2,16,80]{3,2,1,0:T(8,128)(2,1)S(1)} all-to-all(bf16[16,2,16,80]{3,2,1,0:T(8,128)(2,1)S(1)} %forcing_part.1), channel_id=1, replica_groups=mesh['band'=16,'z'=8,'core'=2] {'band'}, dimensions={0} | all-to-all | bytes 163840 | tf_op jit(solution)/shard_map/all_to_all | solution.py:415
  58.5 3.1 %analysis.1 = bf16[4,80,2,1280]{3,2,1,0:T(2,128)(2,1)} custom-call(s32[1]{0:T(128)} %bitcast.band_ref, s32[1280]{0:T(1024)} %wave_ref.5, bf16[16,2,16,80]{3,2,1,0:T(8,128)(2,1)S(1)} %all_to_all.17.in_ref, bf16[256,1024]{1,0:T(8,128)(2,1)S(1)} %get-tuple-element.20.pick_ref, bf16[160,160]{1,0:T(8,128)(2,1)S(1)} %get-tuple-element.21.weave_ref, ...), custom_call_target="tpu_custom_call" | custom-call | tf_op jit(solution)/shard_map/analysis/pallas_call | solution.py:281

commit v9 on v7

--- a/solution.py
+++ b/solution.py
@@ -319,32 +319,27 @@
     )(blocks)
 
 
-def share_kernel(index_ref, pair_ref, share_ref, below_ref):
-    core = index_ref[0] % 2
-    chip = pair_ref[0] + pair_ref[1]
-    below_ref[...] = pair_ref[1 - core]
+def share_kernel(index_ref, total_ref, below_ref, share_ref):
+    chip = total_ref[...] + below_ref[...]
     rows, waves = chip.shape
     half = waves // 2
-    chip = jnp.where(core == 0, chip[: rows // 2], chip[rows // 2 :])
+    chip = jnp.where(index_ref[0] % 2 == 0, chip[: rows // 2], chip[rows // 2 :])
     share = jnp.concatenate([chip[:, :half], chip[:, half:]], axis=0).astype(BF16)
     for d in range(share_ref.shape[0]):
         share_ref[d] = share
 
 
-def share_rows(index, pair, groups):
-    _, rows, waves = pair.shape
+def share_rows(index, total, below, groups):
+    rows, waves = total.shape
     vmem = pl.BlockSpec(memory_space=pltpu.VMEM)
     return pl.pallas_call(
         share_kernel,
-        in_specs=[pl.BlockSpec(memory_space=pltpu.SMEM), vmem],
-        out_specs=[vmem] * 2,
-        out_shape=(
-            jax.ShapeDtypeStruct((groups, rows, waves // 2), BF16),
-            jax.ShapeDtypeStruct((rows, waves), F32),
-        ),
+        in_specs=[pl.BlockSpec(memory_space=pltpu.SMEM), vmem, vmem],
+        out_specs=vmem,
+        out_shape=jax.ShapeDtypeStruct((groups, rows, waves // 2), BF16),
         compiler_params=pltpu.CompilerParams(vmem_limit_bytes=8 * 2**20),
         name="share_rows",
-    )(index, pair)
+    )(index, total, below)
 
 
 def forcing_kernel(
@@ -440,8 +435,8 @@
     )
     blocks = lax.all_to_all(blocks, "band", split_axis=0, concat_axis=0, tiled=True)
     four, total = gather_rows(blocks)
-    pair = lax.all_gather(total, "core")
-    shares, below = share_rows(index, pair, groups)
+    below = lax.ppermute(total, "core", [(0, 1), (1, 0)])
+    shares = share_rows(index, total, below, groups)
     totals = lax.all_to_all(shares, ("z", "core"), split_axis=0, concat_axis=0, tiled=True)
     sides = forcing_part(
         index, lev_coef, totals, below, four, wave_of_slot, gain, cos_t, sin_t, blocks.shape, norm

time: 60.3 us -> 59.7 us (0.990)
  blocking collectives: 46.2 us -> 42.6 us
  starting transfers between devices: 0 us -> 2.16 us
  waiting for transfers between devices: 0 us -> 0.87 us
    all_gather x1 -> x0, blocking collectives: 3.59 us -> none  [body(): pair = lax.all_gather(total, 'core')]
    ppermute x0 -> x1, starting transfers between devices: none -> 2.16 us  [body(): below = lax.ppermute(total, 'core', [(0, 1), (1, 0)])]
    ppermute x0 -> x1, waiting for transfers between devices: none -> 0.87 us  [body(): below = lax.ppermute(total, 'core', [(0, 1), (1, 0)])]
  transfers between devices with their start and end apart: 0 -> 1, of which waited for: 0 -> 1; matrix products, arithmetic and copies ran while one was open for 0% -> 0% of each run, Pallas kernels for 0% -> 0%
where the time goes in v9:
time: 59.7 us; the launch traced here: 59.4 us
  blocking collectives  42.6 us (71%)
  Pallas kernels  13.7 us (23%)
  starting transfers between devices  2.16 us (4%)
  waiting for transfers between devices  0.87 us (1%)
    all_to_all x1, blocking collectives, body(): lax.all_to_all(shares, ('z', 'core'), split_axis=0, concat_axis=0, tiled=...  18.3 us
    all_to_all x1, blocking collectives, body(): lax.all_to_all(blocks, 'band', split_axis=0, concat_axis=0, tiled=True)  14.3 us
    all_to_all x1, blocking collectives, body(): lax.all_to_all(sides, 'band', split_axis=0, concat_axis=0, tiled=True)  10.1 us
    pallas_call x1, Pallas kernels, synthesis(): pl.pallas_call(functools.partial(synthesis_kernel, norm=norm), in_specs=[...  7.7 us
    pallas_call x1, Pallas kernels, analysis(): pl.pallas_call(analysis_kernel, in_specs=[smem, smem, vmem, vmem], out_sp...  3.1 us
    pallas_call x1, Pallas kernels, forcing_part(): pl.pallas_call(functools.partial(forcing_kernel, norm=norm), in_specs=[sm...  2.66 us
    ppermute x1, starting transfers between devices, body(): below = lax.ppermute(total, 'core', [(0, 1), (1, 0)])  2.16 us
  transfers between devices with their start and end apart: 1, of which 1 were waited for; matrix products, arithmetic and copies ran while one was open for 0% of the time, Pallas kernels for 0%

profile of v9, /device:TPU:1, one launch (start us, length us, event | category | flops | bytes accessed | tf_op | source)
XLA Modules:
  0.0 59.4 jit_solution(2992908624317859123)
XLA Ops:
  0.0 7.7 %synthesis.1 = (bf16[16,2,16,80]{3,2,1,0:T(8,128)(2,1)S(1)}, bf16[80,32,1280]{2,1,0:T(8,128)(2,1)S(1)}, bf16[656,1280]{1,0:T(8,128)(2,1)S(1)}, bf16[656,1280]{1,0:T(8,128)(2,1)S(1)}, f32[128,656]{1,0:T(8,128)S(1)}) custom-call(s32[1]{0:T(128)} %bitcast.band_ref, s32[1]{0:T(128)} %bitcast.1.index_ref, s32[1280]{0:T(1024)} %wave_ref.5, s32[1,4]{1,0:T(1,128)} %held_ref.1, ...), custom_call_target="tpu_custom_call" | custom-call | tf_op jit(solution)/shard_map/synthesis/pallas_call | solution.py:198
  7.7 14.3 %all_to_all.15.in_ref = bf16[16,2,16,80]{3,2,1,0:T(8,128)(2,1)S(1)} all-to-all(bf16[16,2,16,80]{3,2,1,0:T(8,128)(2,1)S(1)} %get-tuple-element.12), channel_id=1, replica_groups=mesh['band'=16,'z'=8,'core'=2] {'band'}, dimensions={0} | all-to-all | bytes 163840 | tf_op jit(solution)/shard_map/all_to_all | solution.py:436
  22.0 0.2 gather_rows.1
  22.2 2.2 %collective-permute-start = (f32[8,1280]{1,0:T(8,128)S(1)}, f32[8,1280]{1,0:T(8,128)S(1)}, u32[]{:S(2)}, u32[]{:S(2)}) collective-permute-start(f32[8,1280]{1,0:T(8,128)S(1)} %get-tuple-element.13.total_ref), channel_id=1, source_target_pairs={{0,1},{1,0},{2,3},{3,2},{4,5},{5,4},{6,7},{7,6},{8,9},{9,8},{10,11... | collective-permute-start | bytes 122888 | tf_op jit(solution)/shard_map/ppermute | solution.py:438
  24.3 0.9 %collective-permute-done.below_ref = f32[8,1280]{1,0:T(8,128)S(1)} collective-permute-done((f32[8,1280]{1,0:T(8,128)S(1)}, f32[8,1280]{1,0:T(8,128)S(1)}, u32[]{:S(2)}, u32[]{:S(2)}) %collective-permute-start) | collective-permute-done | bytes 40992 | tf_op jit(solution)/shard_map/ppermute | solution.py:438
  25.2 18.3 %all_to_all.16.total_ref = bf16[16,8,640]{2,1,0:T(8,128)(2,1)S(1)} all-to-all(bf16[16,8,640]{2,1,0:T(8,128)(2,1)S(1)} %share_rows.1), channel_id=1, replica_groups=mesh['band'=16,'z'=8,'core'=2] {'z','core'}, dimensions={0} | all-to-all | bytes 327680 | tf_op jit(solution)/shard_map/all_to_all | solution.py:440
  43.5 2.7 %forcing_part.1 = bf16[16,2,16,80]{3,2,1,0:T(8,128)(2,1)S(1)} custom-call(s32[1]{0:T(128)} %bitcast.1.index_ref, f32[4]{0:T(128)} %coef_ref.1, bf16[16,8,640]{2,1,0:T(8,128)(2,1)S(1)} %all_to_all.16.total_ref, f32[8,1280]{1,0:T(8,128)S(1)} %collective-permute-done.below_ref, bf16[32,1280]{1,0:T(8,128)(2,1)S(1)} %get-tuple-element.14.four_ref, ...), custom_call_target="tpu_custom_call" | custom-call | flops 900000000 | bytes 8000000 | tf_op jit(solution)/shard_map/forcing_part/pallas_call | solution.py:410
  46.2 10.1 %all_to_all.17.in_ref = bf16[16,2,16,80]{3,2,1,0:T(8,128)(2,1)S(1)} all-to-all(bf16[16,2,16,80]{3,2,1,0:T(8,128)(2,1)S(1)} %forcing_part.1), channel_id=1, replica_groups=mesh['band'=16,'z'=8,'core'=2] {'band'}, dimensions={0} | all-to-all | bytes 163840 | tf_op jit(solution)/shard_map/all_to_all | solution.py:444
  56.3 3.1 %analysis.1 = bf16[4,80,2,1280]{3,2,1,0:T(2,128)(2,1)} custom-call(s32[1]{0:T(128)} %bitcast.band_ref, s32[1280]{0:T(1024)} %wave_ref.5, bf16[16,2,16,80]{3,2,1,0:T(8,128)(2,1)S(1)} %all_to_all.17.in_ref, bf16[80,32,1280]{2,1,0:T(8,128)(2,1)S(1)} %get-tuple-element.18.leg_ref), custom_call_target="tpu_custom_call" | custom-call | tf_op jit(solution)/shard_map/analysis/pallas_call | solution.py:282
  (1 shorter events, 0.0 us)
Async XLA Ops:
  22.2 3.0 %collective-permute-start = (f32[8,1280]{1,0:T(8,128)S(1)}, f32[8,1280]{1,0:T(8,128)S(1)}, u32[]{:S(2)}, u32[]{:S(2)}) collective-permute-start(f32[8,1280]{1,0:T(8,128)S(1)} %get-tuple-element.13.total_ref), channel_id=1, source_target_pairs={{0,1},{1,0},{2,3},{3,2},{4,5},{5,4},{6,7},{7,6},{8,9},{9,8},{10,11... | collective-permute-start | bytes 122888 | tf_op jit(solution)/shard_map/ppermute | solution.py:438

commit v10 on v9

--- a/solution.py
+++ b/solution.py
@@ -342,22 +342,38 @@
     )(index, total, below)
 
 
+def prior_kernel(index_ref, total_ref, prior_ref):
+    prior = jnp.zeros(prior_ref.shape, F32)
+    for z in range(total_ref.shape[0]):
+        prior = prior + jnp.where(z < index_ref[0] // 2, total_ref[z].astype(F32), 0.0)
+    prior_ref[...] = prior
+
+
+def prior_rows(index, totals):
+    vmem = pl.BlockSpec(memory_space=pltpu.VMEM)
+    return pl.pallas_call(
+        prior_kernel,
+        in_specs=[pl.BlockSpec(memory_space=pltpu.SMEM), vmem],
+        out_specs=vmem,
+        out_shape=jax.ShapeDtypeStruct(totals.shape[1:], F32),
+        compiler_params=pltpu.CompilerParams(vmem_limit_bytes=8 * 2**20),
+        name="prior_rows",
+    )(index, totals)
+
+
 def forcing_kernel(
-    index_ref, coef_ref, total_ref, below_ref, four_ref, wave_ref, gain_ref, cos_ref, sin_ref,
+    index_ref, coef_ref, mine_ref, other_ref, below_ref, four_ref, wave_ref, gain_ref, cos_ref, sin_ref,
     out_ref, *, norm
 ):
     me = index_ref[0]
-    groups = total_ref.shape[0]
     rows, waves = below_ref.shape
     both = four_ref.shape[0]
     sub = both // 2
     wave = wave_ref[...][None, :]
-    parts = []
-    for c in range(2):
-        part = jnp.zeros(total_ref.shape[1:], F32)
-        for z in range(groups // 2):
-            part = part + jnp.where(z < me // 2, total_ref[2 * z + c].astype(F32), 0.0)
-        parts.append(jnp.concatenate([part[: rows // 2], part[rows // 2 :]], axis=1))
+    mine, other = mine_ref[...], other_ref[...]
+    upper = me % 2 == 1
+    parts = (jnp.where(upper, other, mine), jnp.where(upper, mine, other))
+    parts = [jnp.concatenate([v[: rows // 2], v[rows // 2 :]], axis=1) for v in parts]
     carry = jnp.concatenate(parts, axis=0) + jnp.where(me % 2 == 1, below_ref[...], 0.0)
     four = four_ref[...]
     row, col = iota((both, both), 0), iota((both, both), 1)
@@ -404,23 +420,23 @@
             out_ref[d, c] = sides[:, slots * d : slots * (d + 1)]
 
 
-def forcing_part(index, coef, totals, below, four, wave, gain, cos_t, sin_t, shape, norm):
+def forcing_part(index, coef, mine, other, below, four, wave, gain, cos_t, sin_t, shape, norm):
     vmem = pl.BlockSpec(memory_space=pltpu.VMEM)
     smem = pl.BlockSpec(memory_space=pltpu.SMEM)
     return pl.pallas_call(
         functools.partial(forcing_kernel, norm=norm),
-        in_specs=[smem] * 2 + [vmem] * 7,
+        in_specs=[smem] * 2 + [vmem] * 8,
         out_specs=vmem,
         out_shape=jax.ShapeDtypeStruct(shape, BF16),
         compiler_params=pltpu.CompilerParams(vmem_limit_bytes=32 * 2**20),
         cost_estimate=pl.CostEstimate(flops=900_000_000, bytes_accessed=8_000_000, transcendentals=0),
         name="forcing_part",
-    )(index, coef, totals, below, four, wave, gain, cos_t, sin_t)
+    )(index, coef, mine, other, below, four, wave, gain, cos_t, sin_t)
 
 
 def body(adj_spec, wave_of_slot, legendre, lat_weight, traj, traj_exp, traj_order, lev_coef):
     levels, degrees = adj_spec.shape[0], adj_spec.shape[3]
-    groups = lax.axis_size(("z", "core"))
+    groups = lax.axis_size("z")
     norm = 1.0 / math.sqrt(degrees)
     band = lax.axis_index("band").astype(I32)[None]
     index = lax.axis_index(("z", "core")).astype(I32)[None]
@@ -437,9 +453,11 @@
     four, total = gather_rows(blocks)
     below = lax.ppermute(total, "core", [(0, 1), (1, 0)])
     shares = share_rows(index, total, below, groups)
-    totals = lax.all_to_all(shares, ("z", "core"), split_axis=0, concat_axis=0, tiled=True)
+    totals = lax.all_to_all(shares, "z", split_axis=0, concat_axis=0, tiled=True)
+    mine = prior_rows(index, totals)
+    other = lax.ppermute(mine, "core", [(0, 1), (1, 0)])
     sides = forcing_part(
-        index, lev_coef, totals, below, four, wave_of_slot, gain, cos_t, sin_t, blocks.shape, norm
+        index, lev_coef, mine, other, below, four, wave_of_slot, gain, cos_t, sin_t, blocks.shape, norm
     )
     sides = lax.all_to_all(sides, "band", split_axis=0, concat_axis=0, tiled=True)
     return analysis(sides, table, band, wave_of_slot, levels)

time: 59.7 us -> 59 us (0.988)
  blocking collectives: 42.6 us -> 39.2 us
  starting transfers between devices: 2.16 us -> 4.12 us
  waiting for transfers between devices: 0.87 us -> 1.71 us
    all_to_all x1, blocking collectives: 18.3 us -> 15.3 us  [body(): lax.all_to_all(shares, 'z', split_axis=0, concat_axis=0, tiled=True)]
    ppermute x0 -> x1, starting transfers between devices: none -> 1.96 us  [body(): other = lax.ppermute(mine, 'core', [(0, 1), (1, 0)])]
    ppermute x0 -> x1, waiting for transfers between devices: none -> 0.84 us  [body(): other = lax.ppermute(mine, 'core', [(0, 1), (1, 0)])]
  transfers between devices with their start and end apart: 1 -> 2, of which waited for: 1 -> 2; matrix products, arithmetic and copies ran while one was open for 0% -> 0% of each run, Pallas kernels for 0% -> 0%
where the time goes in v10:
time: 59 us; the launch traced here: 58.7 us
  blocking collectives  39.2 us (66%)
  Pallas kernels  13.7 us (23%)
  starting transfers between devices  4.12 us (7%)
  waiting for transfers between devices  1.71 us (3%)
    all_to_all x1, blocking collectives, body(): lax.all_to_all(shares, 'z', split_axis=0, concat_axis=0, tiled=True)  15.3 us
    all_to_all x1, blocking collectives, body(): lax.all_to_all(blocks, 'band', split_axis=0, concat_axis=0, tiled=True)  14.3 us
    all_to_all x1, blocking collectives, body(): lax.all_to_all(sides, 'band', split_axis=0, concat_axis=0, tiled=True)  9.63 us
    pallas_call x1, Pallas kernels, synthesis(): pl.pallas_call(functools.partial(synthesis_kernel, norm=norm), in_specs=[...  7.7 us
    pallas_call x1, Pallas kernels, analysis(): pl.pallas_call(analysis_kernel, in_specs=[smem, smem, vmem, vmem], out_sp...  3.1 us
    pallas_call x1, Pallas kernels, forcing_part(): pl.pallas_call(functools.partial(forcing_kernel, norm=norm), in_specs=[sm...  2.64 us
    ppermute x1, starting transfers between devices, body(): below = lax.ppermute(total, 'core', [(0, 1), (1, 0)])  2.16 us
    ppermute x1, starting transfers between devices, body(): other = lax.ppermute(mine, 'core', [(0, 1), (1, 0)])  1.96 us
  transfers between devices with their start and end apart: 2, of which 2 were waited for; matrix products, arithmetic and copies ran while one was open for 0% of the time, Pallas kernels for 0%

profile of v10, /device:TPU:1, one launch (start us, length us, event | category | flops | bytes accessed | tf_op | source)
XLA Modules:
  0.0 58.7 jit_solution(16271077241917956642)
XLA Ops:
  0.0 7.7 %synthesis.1 = (bf16[16,2,16,80]{3,2,1,0:T(8,128)(2,1)S(1)}, bf16[80,32,1280]{2,1,0:T(8,128)(2,1)S(1)}, bf16[656,1280]{1,0:T(8,128)(2,1)S(1)}, bf16[656,1280]{1,0:T(8,128)(2,1)S(1)}, f32[128,656]{1,0:T(8,128)S(1)}) custom-call(s32[1]{0:T(128)} %bitcast.band_ref, s32[1]{0:T(128)} %bitcast.1.index_ref, s32[1280]{0:T(1024)} %wave_ref.5, s32[1,4]{1,0:T(1,128)} %held_ref.1, ...), custom_call_target="tpu_custom_call" | custom-call | tf_op jit(solution)/shard_map/synthesis/pallas_call | solution.py:198
  7.7 14.3 %all_to_all.15.in_ref = bf16[16,2,16,80]{3,2,1,0:T(8,128)(2,1)S(1)} all-to-all(bf16[16,2,16,80]{3,2,1,0:T(8,128)(2,1)S(1)} %get-tuple-element.12), channel_id=1, replica_groups=mesh['band'=16,'z'=8,'core'=2] {'band'}, dimensions={0} | all-to-all | bytes 163840 | tf_op jit(solution)/shard_map/all_to_all | solution.py:452
  22.0 0.2 gather_rows.1
  22.2 2.2 %collective-permute-start = (f32[8,1280]{1,0:T(8,128)S(1)}, f32[8,1280]{1,0:T(8,128)S(1)}, u32[]{:S(2)}, u32[]{:S(2)}) collective-permute-start(f32[8,1280]{1,0:T(8,128)S(1)} %get-tuple-element.13.total_ref), channel_id=1, source_target_pairs={{0,1},{1,0},{2,3},{3,2},{4,5},{5,4},{6,7},{7,6},{8,9},{9,8},{10,11... | collective-permute-start | bytes 122888 | tf_op jit(solution)/shard_map/ppermute | solution.py:454
  24.3 0.9 %collective-permute-done.below_ref = f32[8,1280]{1,0:T(8,128)S(1)} collective-permute-done((f32[8,1280]{1,0:T(8,128)S(1)}, f32[8,1280]{1,0:T(8,128)S(1)}, u32[]{:S(2)}, u32[]{:S(2)}) %collective-permute-start) | collective-permute-done | bytes 40992 | tf_op jit(solution)/shard_map/ppermute | solution.py:454
  25.2 15.3 %all_to_all.16.total_ref = bf16[8,8,640]{2,1,0:T(8,128)(2,1)S(1)} all-to-all(bf16[8,8,640]{2,1,0:T(8,128)(2,1)S(1)} %share_rows.1), channel_id=1, replica_groups=mesh['band'=16,'z'=8,'core'=2] {'z'}, dimensions={0} | all-to-all | bytes 163840 | tf_op jit(solution)/shard_map/all_to_all | solution.py:456
  40.5 2.0 %collective-permute-start.1 = (f32[8,640]{1,0:T(8,128)S(1)}, f32[8,640]{1,0:T(8,128)S(1)}, u32[]{:S(2)}, u32[]{:S(2)}) collective-permute-start(f32[8,640]{1,0:T(8,128)S(1)} %prior_rows.1.mine_ref), channel_id=1, source_target_pairs={{0,1},{1,0},{2,3},{3,2},{4,5},{5,4},{6,7},{7,6},{8,9},{9,8},{10,11... | collective-permute-start | bytes 61448 | tf_op jit(solution)/shard_map/ppermute | solution.py:458
  42.5 0.8 %collective-permute-done.1.other_ref = f32[8,640]{1,0:T(8,128)S(1)} collective-permute-done((f32[8,640]{1,0:T(8,128)S(1)}, f32[8,640]{1,0:T(8,128)S(1)}, u32[]{:S(2)}, u32[]{:S(2)}) %collective-permute-start.1) | collective-permute-done | bytes 20512 | tf_op jit(solution)/shard_map/ppermute | solution.py:458
  43.3 2.6 %forcing_part.1 = bf16[16,2,16,80]{3,2,1,0:T(8,128)(2,1)S(1)} custom-call(s32[1]{0:T(128)} %bitcast.1.index_ref, f32[4]{0:T(128)} %coef_ref.1, f32[8,640]{1,0:T(8,128)S(1)} %prior_rows.1.mine_ref, f32[8,640]{1,0:T(8,128)S(1)} %collective-permute-done.1.other_ref, f32[8,1280]{1,0:T(8,128)S(1)} %collective-permute-done.below_ref, ...), custom_call_target="tpu_custom_call" | custom-call | flops 900000000 | bytes 8000000 | tf_op jit(solution)/shard_map/forcing_part/pallas_call | solution.py:426
  46.0 9.6 %all_to_all.17.in_ref = bf16[16,2,16,80]{3,2,1,0:T(8,128)(2,1)S(1)} all-to-all(bf16[16,2,16,80]{3,2,1,0:T(8,128)(2,1)S(1)} %forcing_part.1), channel_id=1, replica_groups=mesh['band'=16,'z'=8,'core'=2] {'band'}, dimensions={0} | all-to-all | bytes 163840 | tf_op jit(solution)/shard_map/all_to_all | solution.py:462
  55.6 3.1 %analysis.1 = bf16[4,80,2,1280]{3,2,1,0:T(2,128)(2,1)} custom-call(s32[1]{0:T(128)} %bitcast.band_ref, s32[1280]{0:T(1024)} %wave_ref.5, bf16[16,2,16,80]{3,2,1,0:T(8,128)(2,1)S(1)} %all_to_all.17.in_ref, bf16[80,32,1280]{2,1,0:T(8,128)(2,1)S(1)} %get-tuple-element.18.leg_ref), custom_call_target="tpu_custom_call" | custom-call | tf_op jit(solution)/shard_map/analysis/pallas_call | solution.py:282
  (2 shorter events, 0.0 us)
Async XLA Ops:
  22.2 3.0 %collective-permute-start = (f32[8,1280]{1,0:T(8,128)S(1)}, f32[8,1280]{1,0:T(8,128)S(1)}, u32[]{:S(2)}, u32[]{:S(2)}) collective-permute-start(f32[8,1280]{1,0:T(8,128)S(1)} %get-tuple-element.13.total_ref), channel_id=1, source_target_pairs={{0,1},{1,0},{2,3},{3,2},{4,5},{5,4},{6,7},{7,6},{8,9},{9,8},{10,11... | collective-permute-start | bytes 122888 | tf_op jit(solution)/shard_map/ppermute | solution.py:454
  40.5 2.8 %collective-permute-start.1 = (f32[8,640]{1,0:T(8,128)S(1)}, f32[8,640]{1,0:T(8,128)S(1)}, u32[]{:S(2)}, u32[]{:S(2)}) collective-permute-start(f32[8,640]{1,0:T(8,128)S(1)} %prior_rows.1.mine_ref), channel_id=1, source_target_pairs={{0,1},{1,0},{2,3},{3,2},{4,5},{5,4},{6,7},{7,6},{8,9},{9,8},{10,11... | collective-permute-start | bytes 61448 | tf_op jit(solution)/shard_map/ppermute | solution.py:458
